TPU v7x, 32 devices: a whole 2x2x4 slice. The times are simulated.
32 devices in a mesh: blk: 16 (over z, y, core), fsdp: 2 (over x).
Axes of the slice: x: 2, y: 2, z: 4, core: 2. Of those that a mesh axis runs over, the one named last changes fastest.
Arguments:
- tokens: bfloat16 [2, 2048, 1536], P('fsdp', 'blk'), may hold values from -6 to 6
- cotangent: bfloat16 [2, 2048, 1536], P('fsdp', 'blk'), may hold values from -6 to 6
- segments: int32 [2, 2048], P('fsdp'), may hold values from 0 to 3, as said below
- positions: int32 [2, 2048], P('fsdp', 'blk'), may hold values from 0 to 1919, as said below
- gain_attn: bfloat16 [1536], P(('blk', 'fsdp')), may hold values from 0.5 to 1.5
- gain_ffn: bfloat16 [1536], P(('blk', 'fsdp')), may hold values from 0.5 to 1.5
- w_query: bfloat16 [1536, 1536], P(('blk', 'fsdp')), may hold values from -0.15625 to 0.15625
- w_key: bfloat16 [768, 1536], P(('blk', 'fsdp')), may hold values from -0.15625 to 0.15625
- w_value: bfloat16 [768, 1536], P(('blk', 'fsdp')), may hold values from -0.15625 to 0.15625
- w_output: bfloat16 [1536, 1536], P(('blk', 'fsdp')), may hold values from -2.5 to 2.5
- w_gate: bfloat16 [4096, 1536], P(('blk', 'fsdp')), may hold values from -0.15625 to 0.15625
- w_up: bfloat16 [4096, 1536], P(('blk', 'fsdp')), may hold values from -0.15625 to 0.15625
- w_down: bfloat16 [4096, 1536], P(('blk', 'fsdp')), may hold values from -0.09375 to 0.09375
Outputs:
- result: bfloat16 [2, 2048, 1536], P('fsdp', 'blk')
- grad_tokens: float32 [2, 2048, 1536], P('fsdp', 'blk')
- grad_gain_attn: float32 [1536], P(('blk', 'fsdp'))
- grad_gain_ffn: float32 [1536], P(('blk', 'fsdp'))
- grad_query: float32 [1536, 1536], P(('blk', 'fsdp'))
- grad_key: float32 [768, 1536], P(('blk', 'fsdp'))
- grad_value: float32 [768, 1536], P(('blk', 'fsdp'))
- grad_output: float32 [1536, 1536], P(('blk', 'fsdp'))
- grad_gate: float32 [4096, 1536], P(('blk', 'fsdp'))
- grad_up: float32 [4096, 1536], P(('blk', 'fsdp'))
- grad_down: float32 [4096, 1536], P(('blk', 'fsdp'))
Inputs may be any that keep to these rules, and one draw needn't show every extreme that they name: `segments`: in each group, segment numbers never fall along the tokens and every one of the 4 numbers has at least one token; sequence 1 has exactly 1920 tokens and begins within the first 128 tokens. `positions`: A token's offset from the first token of its sequence in the same group.
All inputs are finite; a program needn't handle non-finite values.
Results may differ from a plain program's by a relative error of at most 0.02.
Values may be sent and summed in bfloat16 or wider, within the bound.
No kernel may reach another device: no remote copies, remote signals or barrier semaphores. Data moves between devices by JAX's collectives and lax.ppermute only.
A program may use at most 320 MiB of HBM per device.

v0:
```python
import jax
import jax.numpy as jnp
from jax import lax
from jax.sharding import PartitionSpec as P

HEADS = 16
KVH = 8
HD = 96


EPS = 1e-05
ROPE_BASE = 100000.0
NEG = -1e30


def passed_along(block, axis, distance):
    devices = range(lax.axis_size(axis))
    route = [(i - distance, i) for i in devices if i - distance in devices]
    return lax.ppermute(block, axis, route)


def passed_along_2(x, axis, by):
    length = lax.axis_size(axis)
    return lax.ppermute(x, axis, [(i, (i + by) % length) for i in range(length)])


def product_t(left, right):
    return lax.dot_general(
        left, right, (((1,), (1,)), ((), ())), preferred_element_type=jnp.float32
    )


def product(left, right):
    return jnp.dot(left, right, preferred_element_type=jnp.float32)


def product_tn(left, right):
    return lax.dot_general(
        left, right, (((0,), (0,)), ((), ())), preferred_element_type=jnp.float32
    )


def rms_scale(values):
    return lax.rsqrt(jnp.mean(values * values, axis=-1, keepdims=True) + EPS)


def norm_back(grad, values, scale, gain):
    weighted = grad * gain
    inner = jnp.mean(weighted * values, axis=-1, keepdims=True)
    return (scale * weighted - values * scale**3 * inner, jnp.sum(grad * values * scale, axis=0))


def rotation(positions):
    half = HD // 2
    freqs = ROPE_BASE ** (-(jnp.arange(half, dtype=jnp.float32) * 2.0 / HD))
    angles = positions.astype(jnp.float32)[:, None] * freqs[None, :]
    return (jnp.cos(angles)[:, None, :], jnp.sin(angles)[:, None, :])


def rotate(values, cosine, sine, heads, sign):
    count = values.shape[0]
    split = values.reshape(count, heads, HD)
    half = HD // 2
    first = split[..., :half]
    second = split[..., half:]
    turned = jnp.concatenate(
        [first * cosine - sign * second * sine, second * cosine + sign * first * sine], axis=-1
    )
    return turned.reshape(count, heads * HD)


def block_mask(query_seg, query_idx, key_seg, key_idx):
    return (query_seg[:, None] == key_seg[None, :]) & (key_idx[None, :] <= query_idx[:, None])


def scores_of(queries, keys, allowed):
    raw = jnp.einsum("qhgd,khd->hgqk", queries, keys, preferred_element_type=jnp.float32) * HD ** (
        -0.5
    )
    return jnp.where(allowed[None, None], raw, NEG)


def key_blocks(keys_seen, values_seen, key_segs):
    total = keys_seen.shape[0]
    size = min(512, total)
    count = total // size
    return (
        keys_seen.reshape(count, size, KVH, HD),
        values_seen.reshape(count, size, KVH, HD),
        key_segs.reshape(count, size),
        jnp.arange(total, dtype=jnp.int32).reshape(count, size),
    )


def attend(queries, blocks, query_seg, query_idx):
    rows = queries.shape[0]
    groups = HEADS // KVH
    start = (
        jnp.full((KVH, groups, rows, 1), NEG, jnp.float32),
        jnp.zeros((KVH, groups, rows, 1), jnp.float32),
    )

    def stats_step(carry, block):
        keys, values, segs, idxs = block
        allowed = block_mask(query_seg, query_idx, segs, idxs)
        top, running = carry
        scores = scores_of(queries, keys, allowed)
        new_top = jnp.maximum(top, jnp.max(scores, axis=-1, keepdims=True))
        new_sum = running * jnp.exp(top - new_top) + jnp.sum(
            jnp.exp(scores - new_top), axis=-1, keepdims=True
        )
        return ((new_top, new_sum), None)

    (top, running), unused = lax.scan(stats_step, start, blocks)
    lse = top + jnp.log(running)

    def value_step(total_acc, block):
        keys, values, segs, idxs = block
        allowed = block_mask(query_seg, query_idx, segs, idxs)
        weights = jnp.exp(scores_of(queries, keys, allowed) - lse).astype(jnp.bfloat16)
        return (
            total_acc
            + jnp.einsum("hgqk,khd->qhgd", weights, values, preferred_element_type=jnp.float32),
            None,
        )

    mixed, unused = lax.scan(value_step, jnp.zeros((rows, KVH, groups, HD), jnp.float32), blocks)
    return (mixed, lse)


def cycle_back(queries, own_keys, own_values, key_segs, query_seg, query_idx, lse, grad_out, delta):
    rows = queries.shape[0]
    groups = HEADS // KVH
    scale = HD ** (-0.5)
    me = lax.axis_index("blk")
    count = lax.axis_size("blk")
    local = jnp.arange(rows, dtype=jnp.int32)

    def step(carry, turn):
        grad_q, key_blk, value_blk, grad_k, grad_v = carry
        anchor = (me - turn) % count
        begin = anchor * rows
        segs = lax.dynamic_slice_in_dim(key_segs, begin, rows)
        allowed = block_mask(query_seg, query_idx, segs, begin + local)
        acc_k = grad_k
        acc_v = grad_v
        probs = jnp.exp(scores_of(queries, key_blk, allowed) - lse)
        grad_probs = jnp.einsum(
            "qhgd,khd->hgqk", grad_out, value_blk, preferred_element_type=jnp.float32
        )
        grad_scores = (probs * (grad_probs - delta)).astype(jnp.bfloat16)
        new_acc = grad_q + jnp.einsum(
            "hgqk,khd->qhgd", grad_scores, key_blk, preferred_element_type=jnp.float32
        )
        new_k = (
            acc_k
            + jnp.einsum("hgqk,qhgd->khd", grad_scores, queries, preferred_element_type=jnp.float32)
            * scale
        )
        new_v = acc_v + jnp.einsum(
            "hgqk,qhgd->khd",
            probs.astype(jnp.bfloat16),
            grad_out,
            preferred_element_type=jnp.float32,
        )
        grad_k = new_k
        grad_v = new_v
        key_blk, value_blk = passed_along((key_blk, value_blk), "blk", 1)
        grad_k, grad_v = (
            passed_along_2(grad_k.astype(jnp.bfloat16), "blk", 1).astype(grad_k.dtype),
            passed_along_2(grad_v.astype(jnp.bfloat16), "blk", 1).astype(grad_v.dtype),
        )
        return ((new_acc, key_blk, value_blk, grad_k, grad_v), None)

    zero_kv = jnp.zeros((rows, KVH, HD), jnp.float32)
    start = (
        jnp.zeros((rows, KVH, groups, HD), jnp.float32),
        own_keys.reshape(rows, KVH, HD),
        own_values.reshape(rows, KVH, HD),
        zero_kv,
        zero_kv,
    )
    final, unused = lax.scan(step, start, jnp.arange(count, dtype=jnp.int32))
    grad_q, ignored_k, ignored_v, grad_k, grad_v = final
    return (grad_q * scale, grad_k.reshape(rows, KVH * HD), grad_v.reshape(rows, KVH * HD))


def fetch_attention(gain_attn, gain_ffn, w_query, w_key, w_value, w_output):
    return (
        lax.all_gather(gain_attn, ("blk", "fsdp"), axis=0, tiled=True),
        lax.all_gather(gain_ffn, ("blk", "fsdp"), axis=0, tiled=True),
        lax.all_gather(w_query, ("blk", "fsdp"), axis=0, tiled=True),
        lax.all_gather(w_key, ("blk", "fsdp"), axis=0, tiled=True),
        lax.all_gather(w_value, ("blk", "fsdp"), axis=0, tiled=True),
        lax.all_gather(w_output, ("blk", "fsdp"), axis=0, tiled=True),
    )


def fetch_ffn(w_gate, w_up, w_down):
    return (
        lax.all_gather(w_gate, ("blk", "fsdp"), axis=0, tiled=True),
        lax.all_gather(w_up, ("blk", "fsdp"), axis=0, tiled=True),
        lax.all_gather(w_down, ("blk", "fsdp"), axis=0, tiled=True),
    )


def shards(
    tokens,
    cotangent,
    segments,
    positions,
    gain_attn,
    gain_ffn,
    w_query,
    w_key,
    w_value,
    w_output,
    w_gate,
    w_up,
    w_down,
):
    rows = tokens.shape[1]
    groups = HEADS // KVH
    xin = tokens[0].astype(jnp.float32)
    offset = lax.axis_index("blk") * rows
    query_idx = offset + jnp.arange(rows, dtype=jnp.int32)
    key_segs = segments[0]
    query_seg = lax.dynamic_slice_in_dim(key_segs, offset, rows)
    cosine, sine = rotation(positions[0])
    gain_one, gain_two, query_all, key_all, value_all, output_all = fetch_attention(
        gain_attn, gain_ffn, w_query, w_key, w_value, w_output
    )
    first_gain = gain_one.astype(jnp.float32)
    second_gain = gain_two.astype(jnp.float32)
    first_scale = rms_scale(xin)
    normed = (xin * first_scale * first_gain).astype(jnp.bfloat16)
    queries = rotate(product_t(normed, query_all), cosine, sine, HEADS, 1.0).astype(jnp.bfloat16)
    keys = rotate(product_t(normed, key_all), cosine, sine, KVH, 1.0).astype(jnp.bfloat16)
    values = product_t(normed, value_all).astype(jnp.bfloat16)
    keys_seen, values_seen = (
        lax.all_gather(keys, "blk", axis=0, tiled=True),
        lax.all_gather(values, "blk", axis=0, tiled=True),
    )
    query_heads = queries.reshape(rows, KVH, groups, HD)
    mixed, lse = attend(
        query_heads, key_blocks(keys_seen, values_seen, key_segs), query_seg, query_idx
    )
    attended = mixed.reshape(rows, HEADS * HD).astype(jnp.bfloat16)
    middle = xin + product_t(attended, output_all)
    second_scale = rms_scale(middle)
    normed_two = (middle * second_scale * second_gain).astype(jnp.bfloat16)
    gate_rows, up_rows, down_rows = fetch_ffn(w_gate, w_up, w_down)
    gate = product_t(normed_two, gate_rows)
    up = product_t(normed_two, up_rows)
    sigma = jax.nn.sigmoid(gate)
    activated = gate * sigma
    hidden = (activated * up).astype(jnp.bfloat16)
    branch = product(hidden, down_rows)
    result = (middle + branch).astype(jnp.bfloat16)
    grad_in = cotangent[0]
    gate_rows, up_rows, down_rows = fetch_ffn(w_gate, w_up, w_down)
    grad_hidden = product_t(grad_in, down_rows)
    grad_gate = (grad_hidden * up * sigma * (1.0 + gate * (1.0 - sigma))).astype(jnp.bfloat16)
    grad_up = (grad_hidden * activated).astype(jnp.bfloat16)
    gate_grad = product_tn(grad_gate, normed_two)
    up_grad = product_tn(grad_up, normed_two)
    down_grad = product_tn(hidden, grad_in)
    grad_normed_two = product(grad_gate, gate_rows) + product(grad_up, up_rows)
    gate_grad, up_grad, down_grad = (
        lax.psum_scatter(gate_grad, ("blk", "fsdp"), scatter_dimension=0, tiled=True),
        lax.psum_scatter(up_grad, ("blk", "fsdp"), scatter_dimension=0, tiled=True),
        lax.psum_scatter(down_grad, ("blk", "fsdp"), scatter_dimension=0, tiled=True),
    )
    grad_middle_norm, second_gain_grad = norm_back(
        grad_normed_two, middle, second_scale, second_gain
    )
    grad_middle = grad_in.astype(jnp.float32) + grad_middle_norm
    grad_branch = grad_middle.astype(jnp.bfloat16)
    output_grad = product_tn(grad_branch, attended)
    grad_attended = product(grad_branch, output_all).astype(jnp.bfloat16)
    grad_heads = grad_attended.reshape(rows, KVH, groups, HD)
    delta = jnp.transpose(jnp.sum(grad_heads.astype(jnp.float32) * mixed, axis=-1), (1, 2, 0))[
        ..., None
    ]
    grad_q, grad_keys, grad_values = cycle_back(
        query_heads, keys, values, key_segs, query_seg, query_idx, lse, grad_heads, delta
    )
    grad_q_pre = rotate(grad_q.reshape(rows, HEADS * HD), cosine, sine, HEADS, -1.0).astype(
        jnp.bfloat16
    )
    grad_k_pre = rotate(grad_keys, cosine, sine, KVH, -1.0).astype(jnp.bfloat16)
    grad_v = grad_values.astype(jnp.bfloat16)
    query_grad = product_tn(grad_q_pre, normed)
    key_grad = product_tn(grad_k_pre, normed)
    value_grad = product_tn(grad_v, normed)
    grad_normed = (
        product(grad_q_pre, query_all) + product(grad_k_pre, key_all) + product(grad_v, value_all)
    )
    grad_x_norm, first_gain_grad = norm_back(grad_normed, xin, first_scale, first_gain)
    grad_tokens = grad_middle + grad_x_norm
    first_gain_grad, second_gain_grad, query_grad, key_grad, value_grad, output_grad = (
        lax.psum_scatter(first_gain_grad, ("blk", "fsdp"), scatter_dimension=0, tiled=True),
        lax.psum_scatter(second_gain_grad, ("blk", "fsdp"), scatter_dimension=0, tiled=True),
        lax.psum_scatter(query_grad, ("blk", "fsdp"), scatter_dimension=0, tiled=True),
        lax.psum_scatter(key_grad, ("blk", "fsdp"), scatter_dimension=0, tiled=True),
        lax.psum_scatter(value_grad, ("blk", "fsdp"), scatter_dimension=0, tiled=True),
        lax.psum_scatter(output_grad, ("blk", "fsdp"), scatter_dimension=0, tiled=True),
    )
    return (
        result[None],
        grad_tokens[None],
        first_gain_grad,
        second_gain_grad,
        query_grad,
        key_grad,
        value_grad,
        output_grad,
        gate_grad,
        up_grad,
        down_grad,
    )


def solution(mesh):
    in_specs = (
        P("fsdp", "blk", None),
        P("fsdp", "blk", None),
        P("fsdp", None),
        P("fsdp", "blk"),
        P(("blk", "fsdp")),
        P(("blk", "fsdp")),
        P(("blk", "fsdp"), None),
        P(("blk", "fsdp"), None),
        P(("blk", "fsdp"), None),
        P(("blk", "fsdp"), None),
        P(("blk", "fsdp"), None),
        P(("blk", "fsdp"), None),
        P(("blk", "fsdp"), None),
    )
    out_specs = (
        P("fsdp", "blk", None),
        P("fsdp", "blk", None),
        P(("blk", "fsdp")),
        P(("blk", "fsdp")),
        P(("blk", "fsdp"), None),
        P(("blk", "fsdp"), None),
        P(("blk", "fsdp"), None),
        P(("blk", "fsdp"), None),
        P(("blk", "fsdp"), None),
        P(("blk", "fsdp"), None),
        P(("blk", "fsdp"), None),
    )
    return jax.shard_map(shards, mesh=mesh, in_specs=in_specs, out_specs=out_specs, check_vma=False)
```

profile of v0, /device:TPU:0, one launch (start us, length us, event | category | flops | bytes accessed | tf_op | source)
XLA Modules:
  0.0 2346.6 jit_solution(85150431136969843)
XLA Ops:
  11.2 42.1 %all-reduce.5 = (bf16[1536]{0:T(1024)(128)(2,1)S(1)}, bf16[1536]{0:T(1024)(128)(2,1)S(1)}) all-reduce(bf16[1536]{0:T(1024)(128)(2,1)S(1)} %dynamic-update-slice, bf16[1536]{0:T(1024)(128)(2,1)S(1)} %dynamic-update-slice.1), channel_id=1, replica_groups=mesh['blk'=16,'fsdp'=2] {'blk','fsdp'}, use_global_device_ids=true, to_apply=%add | all-reduce | flops 3072 | bytes 12288
  55.0 16.1 all-gather.10.cloned.1.call-done
  75.3 54.9 %all-gather.14.cloned.1.call-done = bf16[768,1536]{1,0:T(8,128)(2,1)} async-done(((bf16[24,1536]{1,0:T(8,128)(2,1)}), bf16[768,1536]{1,0:T(8,128)(2,1)}) %all-gather.14.cloned.1.call-update) | async-done | bytes 2359312 | tf_op jit(solution)/shard_map/all_gather | solution.py:193
  139.8 55.9 %all-gather.18.cloned.1.call-done = bf16[1536,1536]{1,0:T(8,128)(2,1)} async-done(((bf16[48,1536]{1,0:T(8,128)(2,1)}), bf16[1536,1536]{1,0:T(8,128)(2,1)}) %all-gather.18.cloned.1.call-update) | async-done | bytes 4718608 | tf_op jit(solution)/shard_map/all_gather | solution.py:192
  199.7 42.8 %all-gather.12.cloned.1.call-done = bf16[2048,768]{1,0:T(8,128)(2,1)} async-done(((bf16[128,768]{1,0:T(8,128)(2,1)}), bf16[2048,768]{1,0:T(8,128)(2,1)}) %all-gather.12.cloned.1.call-update) | async-done | bytes 3145744 | tf_op jit(solution)/shard_map/all_gather | solution.py:242
  242.4 8.3 reshape.438
  250.7 7.4 copy.50
  258.1 32.4 %all-gather.16.cloned.1.call-done = bf16[2048,768]{0,1:T(8,128)(2,1)} async-done(((bf16[128,768]{0,1:T(8,128)(2,1)}), bf16[2048,768]{0,1:T(8,128)(2,1)}) %all-gather.16.cloned.1.call-update) | async-done | bytes 3145744 | tf_op jit(solution)/shard_map/all_gather | solution.py:241
  290.5 6.1 reshape.422
  300.9 30.0 %while.45 = (s32[]{:T(128)}, f32[8,2,128,1]{2,1,0,3:T(2,128)S(1)}, f32[8,2,128,1]{2,1,0,3:T(2,128)S(1)}, s32[128]{0:T(128)S(1)}, s32[4,512]{1,0:T(4,128)S(1)}, /...) while((s32[]{:T(128)}, f32[8,2,128,1]{2,1,0,3:T(2,128)S(1)}, ...), condition=%wide.region_4.5_spmd.clone, body=%wide.region_1.4_spmd.clone.sunk | while | flops 208873600 | bytes 9885324 | solution.py:114
  330.9 13.8 while.46
  344.8 10.3 all-gather.20.cloned.1.call-done
  359.4 93.5 %all-gather.22.cloned.1.call-done = bf16[4096,1536]{1,0:T(8,128)(2,1)} async-done(((bf16[128,1536]{1,0:T(8,128)(2,1)}), bf16[4096,1536]{1,0:T(8,128)(2,1)}) %all-gather.22.cloned.1.call-update) | async-done | bytes 12582928 | tf_op jit(solution)/shard_map/all_gather | solution.py:201
  452.8 10.0 fusion.92
  462.8 87.2 %all-gather.24.cloned.1.call-done = bf16[4096,1536]{1,0:T(8,128)(2,1)} async-done(((bf16[128,1536]{1,0:T(8,128)(2,1)}), bf16[4096,1536]{1,0:T(8,128)(2,1)}) %all-gather.24.cloned.1.call-update) | async-done | bytes 12582928 | tf_op jit(solution)/shard_map/all_gather | solution.py:202
  550.0 9.9 fusion.93
  560.0 87.2 %all-gather.26.cloned.1.call-done = bf16[4096,1536]{1,0:T(8,128)(2,1)} async-done(((bf16[128,1536]{1,0:T(8,128)(2,1)}), bf16[4096,1536]{1,0:T(8,128)(2,1)}) %all-gather.26.cloned.1.call-update) | async-done | bytes 12582928 | tf_op jit(solution)/shard_map/all_gather | solution.py:203
  647.2 11.2 multiply_convert_fusion
  658.3 7.2 fusion.94
  665.6 7.3 multiply_reduce_fusion
  678.8 400.9 %while.47 = (s32[]{:T(128)}, f32[128,8,2,96]{0,3,2,1:T(8,128)S(1)}, bf16[128,8,96]{0,2,1:T(8,128)(2,1)}, bf16[128,8,96]{0,2,1:T(8,128)(2,1)}, f32[128,8,96]{0,2,...) while((s32[]{:T(128)}, f32[128,8,2,96]{0,3,2,1:T(8,128)S(1)}, ...), condition=%wide.region_11.12_spmd.clone, body=%wide.region_10.11_spmd.clone.sunk | while | flops 254820624 | bytes 16372292 | solution.py:183
  694.7 6.4 collective-permute-done.2
  719.3 6.7 collective-permute-done.2
  744.3 6.7 collective-permute-done.2
  769.3 6.7 collective-permute-done.2
  794.3 6.7 collective-permute-done.2
  819.3 6.7 collective-permute-done.2
  844.3 6.7 collective-permute-done.2
  869.2 6.7 collective-permute-done.2
  894.2 6.7 collective-permute-done.2
  919.2 6.7 collective-permute-done.2
  944.2 6.7 collective-permute-done.2
  969.2 6.7 collective-permute-done.2
  994.2 6.7 collective-permute-done.2
  1019.2 6.7 collective-permute-done.2
  1044.1 6.7 collective-permute-done.2
  1069.1 6.7 collective-permute-done.2
  1100.8 10.5 fusion.96
  1112.5 10.3 fusion.97
  1124.1 10.8 fusion.68
  1141.3 37.3 %all-reduce.4 = (f32[1536]{0:T(1024)S(1)}, f32[1536]{0:T(1024)S(1)}) all-reduce(f32[1536]{0:T(1024)S(1)} %get-tuple-element.513, f32[1536]{0:T(1024)S(1)} %copy-done.26), channel_id=2, replica_groups=mesh['blk'=16,'fsdp'=2] {'blk','fsdp'}, use_global_device_ids=true, to_apply=%region_14.15.clone | all-reduce | flops 3072 | bytes 24576
  1182.2 7.2 fusion.48
  1189.4 111.0 %reduce-scatter.12.cloned.1.call-done = f32[24,1536]{1,0:T(8,128)} async-done(((f32[768,1536]{1,0:T(8,128)}), f32[24,1536]{1,0:T(8,128)}) %reduce-scatter.12.cloned.1.call-update) | async-done | bytes 147472 | tf_op jit(solution)/shard_map/reduce_scatter | solution.py:306
  1300.3 140.9 %reduce-scatter.8.cloned.1.call-done = f32[48,1536]{1,0:T(8,128)} async-done(((f32[1536,1536]{1,0:T(8,128)}), f32[48,1536]{1,0:T(8,128)}) %reduce-scatter.8.cloned.1.call-update) | async-done | bytes 294928 | tf_op jit(solution)/shard_map/reduce_scatter | solution.py:304
  1441.3 142.2 %reduce-scatter.14.cloned.1.call-done = f32[48,1536]{1,0:T(8,128)} async-done(((f32[1536,1536]{1,0:T(8,128)}), f32[48,1536]{1,0:T(8,128)}) %reduce-scatter.14.cloned.1.call-update) | async-done | bytes 294928 | tf_op jit(solution)/shard_map/reduce_scatter | solution.py:307
  1583.5 251.2 %reduce-scatter.16.cloned.1.call-done = f32[128,1536]{1,0:T(8,128)} async-done(((f32[4096,1536]{1,0:T(8,128)}), f32[128,1536]{1,0:T(8,128)}) %reduce-scatter.16.cloned.1.call-update) | async-done | bytes 786448 | tf_op jit(solution)/shard_map/reduce_scatter | solution.py:270
  1834.7 253.0 %reduce-scatter.18.cloned.1.call-done = f32[128,1536]{1,0:T(8,128)} async-done(((f32[4096,1536]{1,0:T(8,128)}), f32[128,1536]{1,0:T(8,128)}) %reduce-scatter.18.cloned.1.call-update) | async-done | bytes 786448 | tf_op jit(solution)/shard_map/reduce_scatter | solution.py:271
  2087.8 251.9 %reduce-scatter.20.cloned.1.call-done = f32[128,1536]{1,0:T(8,128)} async-done(((f32[4096,1536]{1,0:T(8,128)}), f32[128,1536]{1,0:T(8,128)}) %reduce-scatter.20.cloned.1.call-update) | async-done | bytes 786448 | tf_op jit(solution)/shard_map/reduce_scatter | solution.py:272
  (567 shorter events, 395.5 us)
Async XLA Ops:
  7.2 63.8 %all-gather.10.cloned.1.call-start = ((), (), s32[]{:S(2)}) async-start(), calls=%async_computation.7 | async-start | bytes 2433024 | tf_op jit(solution)/shard_map/all_gather | solution.py:194
  7.9 122.3 %all-gather.14.cloned.1.call-start = ((), (), s32[]{:S(2)}) async-start(), calls=%async_computation.9 | async-start | bytes 2433024 | tf_op jit(solution)/shard_map/all_gather | solution.py:193
  8.7 187.0 %all-gather.18.cloned.1.call-start = ((), (), s32[]{:S(2)}) async-start(), calls=%async_computation.11 | async-start | bytes 4866048 | tf_op jit(solution)/shard_map/all_gather | solution.py:192
  9.4 233.0 %all-gather.12.cloned.1.call-start = ((), (), s32[]{:S(2)}) async-start(), calls=%async_computation.8 | async-start | bytes 3342336 | tf_op jit(solution)/shard_map/all_gather | solution.py:242
  74.4 216.1 %all-gather.16.cloned.1.call-start = ((), (), s32[]{:S(2)}) async-start(), calls=%async_computation.10 | async-start | bytes 3342336 | tf_op jit(solution)/shard_map/all_gather | solution.py:241
  133.5 221.6 %all-gather.20.cloned.1.call-start = ((), (), s32[]{:S(2)}) async-start(), calls=%async_computation.12 | async-start | bytes 4866048 | tf_op jit(solution)/shard_map/all_gather | solution.py:195
  134.1 318.7 %all-gather.22.cloned.1.call-start = ((), (), s32[]{:S(2)}) async-start(), calls=%async_computation.13 | async-start | bytes 12976128 | tf_op jit(solution)/shard_map/all_gather | solution.py:201
  134.9 415.2 %all-gather.24.cloned.1.call-start = ((), (), s32[]{:S(2)}) async-start(), calls=%async_computation.14 | async-start | bytes 12976128 | tf_op jit(solution)/shard_map/all_gather | solution.py:202
  135.6 511.6 %all-gather.26.cloned.1.call-start = ((), (), s32[]{:S(2)}) async-start(), calls=%async_computation.15 | async-start | bytes 12976128 | tf_op jit(solution)/shard_map/all_gather | solution.py:203
  136.3 1053.0 %reduce-scatter.10.cloned.1.call-start = ((), (), s32[]{:S(2)}) async-start(), calls=%async_computation.17 | async-start | bytes 4866048 | tf_op jit(solution)/shard_map/reduce_scatter | solution.py:305
  679.7 25.2 %collective-permute-start = (bf16[128,8,96]{0,2,1:T(8,128)(2,1)S(1)}, bf16[128,8,96]{0,2,1:T(8,128)(2,1)}, u32[]{:S(2)}, u32[]{:S(2)}) collective-permute-start(bf16[128,8,96]{0,2,1:T(8,128)(2,1)S(1)} %copy.92), channel_id=1, source_target_pairs={{0,2},{2,4},{4,6},{6,8},{8,10},{10,12},{12,14},{14,16},{16,18},{18... | collective-permute-start | bytes 589832 | tf_op jit(solution)/shard_map/while/body/eval_jaxpr/ppermute | solution.py:19
  684.2 20.7 collective-permute-start.1
  705.8 24.1 %collective-permute-start = (bf16[128,8,96]{0,2,1:T(8,128)(2,1)S(1)}, bf16[128,8,96]{0,2,1:T(8,128)(2,1)}, u32[]{:S(2)}, u32[]{:S(2)}) collective-permute-start(bf16[128,8,96]{0,2,1:T(8,128)(2,1)S(1)} %copy.92), channel_id=1, source_target_pairs={{0,2},{2,4},{4,6},{6,8},{8,10},{10,12},{12,14},{14,16},{16,18},{18... | collective-permute-start | bytes 589832 | tf_op jit(solution)/shard_map/while/body/eval_jaxpr/ppermute | solution.py:19
  709.4 20.5 collective-permute-start.1
  730.8 24.1 %collective-permute-start = (bf16[128,8,96]{0,2,1:T(8,128)(2,1)S(1)}, bf16[128,8,96]{0,2,1:T(8,128)(2,1)}, u32[]{:S(2)}, u32[]{:S(2)}) collective-permute-start(bf16[128,8,96]{0,2,1:T(8,128)(2,1)S(1)} %copy.92), channel_id=1, source_target_pairs={{0,2},{2,4},{4,6},{6,8},{8,10},{10,12},{12,14},{14,16},{16,18},{18... | collective-permute-start | bytes 589832 | tf_op jit(solution)/shard_map/while/body/eval_jaxpr/ppermute | solution.py:19
  734.4 20.5 collective-permute-start.1
  755.8 24.1 %collective-permute-start = (bf16[128,8,96]{0,2,1:T(8,128)(2,1)S(1)}, bf16[128,8,96]{0,2,1:T(8,128)(2,1)}, u32[]{:S(2)}, u32[]{:S(2)}) collective-permute-start(bf16[128,8,96]{0,2,1:T(8,128)(2,1)S(1)} %copy.92), channel_id=1, source_target_pairs={{0,2},{2,4},{4,6},{6,8},{8,10},{10,12},{12,14},{14,16},{16,18},{18... | collective-permute-start | bytes 589832 | tf_op jit(solution)/shard_map/while/body/eval_jaxpr/ppermute | solution.py:19
  759.4 20.5 collective-permute-start.1
  780.8 24.1 %collective-permute-start = (bf16[128,8,96]{0,2,1:T(8,128)(2,1)S(1)}, bf16[128,8,96]{0,2,1:T(8,128)(2,1)}, u32[]{:S(2)}, u32[]{:S(2)}) collective-permute-start(bf16[128,8,96]{0,2,1:T(8,128)(2,1)S(1)} %copy.92), channel_id=1, source_target_pairs={{0,2},{2,4},{4,6},{6,8},{8,10},{10,12},{12,14},{14,16},{16,18},{18... | collective-permute-start | bytes 589832 | tf_op jit(solution)/shard_map/while/body/eval_jaxpr/ppermute | solution.py:19
  784.4 20.5 collective-permute-start.1
  805.8 24.1 %collective-permute-start = (bf16[128,8,96]{0,2,1:T(8,128)(2,1)S(1)}, bf16[128,8,96]{0,2,1:T(8,128)(2,1)}, u32[]{:S(2)}, u32[]{:S(2)}) collective-permute-start(bf16[128,8,96]{0,2,1:T(8,128)(2,1)S(1)} %copy.92), channel_id=1, source_target_pairs={{0,2},{2,4},{4,6},{6,8},{8,10},{10,12},{12,14},{14,16},{16,18},{18... | collective-permute-start | bytes 589832 | tf_op jit(solution)/shard_map/while/body/eval_jaxpr/ppermute | solution.py:19
  809.4 20.5 collective-permute-start.1
  830.8 24.1 %collective-permute-start = (bf16[128,8,96]{0,2,1:T(8,128)(2,1)S(1)}, bf16[128,8,96]{0,2,1:T(8,128)(2,1)}, u32[]{:S(2)}, u32[]{:S(2)}) collective-permute-start(bf16[128,8,96]{0,2,1:T(8,128)(2,1)S(1)} %copy.92), channel_id=1, source_target_pairs={{0,2},{2,4},{4,6},{6,8},{8,10},{10,12},{12,14},{14,16},{16,18},{18... | collective-permute-start | bytes 589832 | tf_op jit(solution)/shard_map/while/body/eval_jaxpr/ppermute | solution.py:19
  834.4 20.5 collective-permute-start.1
  855.8 24.1 %collective-permute-start = (bf16[128,8,96]{0,2,1:T(8,128)(2,1)S(1)}, bf16[128,8,96]{0,2,1:T(8,128)(2,1)}, u32[]{:S(2)}, u32[]{:S(2)}) collective-permute-start(bf16[128,8,96]{0,2,1:T(8,128)(2,1)S(1)} %copy.92), channel_id=1, source_target_pairs={{0,2},{2,4},{4,6},{6,8},{8,10},{10,12},{12,14},{14,16},{16,18},{18... | collective-permute-start | bytes 589832 | tf_op jit(solution)/shard_map/while/body/eval_jaxpr/ppermute | solution.py:19
  859.3 20.5 collective-permute-start.1
  880.7 24.1 %collective-permute-start = (bf16[128,8,96]{0,2,1:T(8,128)(2,1)S(1)}, bf16[128,8,96]{0,2,1:T(8,128)(2,1)}, u32[]{:S(2)}, u32[]{:S(2)}) collective-permute-start(bf16[128,8,96]{0,2,1:T(8,128)(2,1)S(1)} %copy.92), channel_id=1, source_target_pairs={{0,2},{2,4},{4,6},{6,8},{8,10},{10,12},{12,14},{14,16},{16,18},{18... | collective-permute-start | bytes 589832 | tf_op jit(solution)/shard_map/while/body/eval_jaxpr/ppermute | solution.py:19
  884.3 20.5 collective-permute-start.1
  905.7 24.1 %collective-permute-start = (bf16[128,8,96]{0,2,1:T(8,128)(2,1)S(1)}, bf16[128,8,96]{0,2,1:T(8,128)(2,1)}, u32[]{:S(2)}, u32[]{:S(2)}) collective-permute-start(bf16[128,8,96]{0,2,1:T(8,128)(2,1)S(1)} %copy.92), channel_id=1, source_target_pairs={{0,2},{2,4},{4,6},{6,8},{8,10},{10,12},{12,14},{14,16},{16,18},{18... | collective-permute-start | bytes 589832 | tf_op jit(solution)/shard_map/while/body/eval_jaxpr/ppermute | solution.py:19
  909.3 20.5 collective-permute-start.1
  930.7 24.1 %collective-permute-start = (bf16[128,8,96]{0,2,1:T(8,128)(2,1)S(1)}, bf16[128,8,96]{0,2,1:T(8,128)(2,1)}, u32[]{:S(2)}, u32[]{:S(2)}) collective-permute-start(bf16[128,8,96]{0,2,1:T(8,128)(2,1)S(1)} %copy.92), channel_id=1, source_target_pairs={{0,2},{2,4},{4,6},{6,8},{8,10},{10,12},{12,14},{14,16},{16,18},{18... | collective-permute-start | bytes 589832 | tf_op jit(solution)/shard_map/while/body/eval_jaxpr/ppermute | solution.py:19
  934.3 20.5 collective-permute-start.1
  955.7 24.1 %collective-permute-start = (bf16[128,8,96]{0,2,1:T(8,128)(2,1)S(1)}, bf16[128,8,96]{0,2,1:T(8,128)(2,1)}, u32[]{:S(2)}, u32[]{:S(2)}) collective-permute-start(bf16[128,8,96]{0,2,1:T(8,128)(2,1)S(1)} %copy.92), channel_id=1, source_target_pairs={{0,2},{2,4},{4,6},{6,8},{8,10},{10,12},{12,14},{14,16},{16,18},{18... | collective-permute-start | bytes 589832 | tf_op jit(solution)/shard_map/while/body/eval_jaxpr/ppermute | solution.py:19
  959.3 20.5 collective-permute-start.1
  980.7 24.1 %collective-permute-start = (bf16[128,8,96]{0,2,1:T(8,128)(2,1)S(1)}, bf16[128,8,96]{0,2,1:T(8,128)(2,1)}, u32[]{:S(2)}, u32[]{:S(2)}) collective-permute-start(bf16[128,8,96]{0,2,1:T(8,128)(2,1)S(1)} %copy.92), channel_id=1, source_target_pairs={{0,2},{2,4},{4,6},{6,8},{8,10},{10,12},{12,14},{14,16},{16,18},{18... | collective-permute-start | bytes 589832 | tf_op jit(solution)/shard_map/while/body/eval_jaxpr/ppermute | solution.py:19
  984.3 20.5 collective-permute-start.1
  1005.7 24.1 %collective-permute-start = (bf16[128,8,96]{0,2,1:T(8,128)(2,1)S(1)}, bf16[128,8,96]{0,2,1:T(8,128)(2,1)}, u32[]{:S(2)}, u32[]{:S(2)}) collective-permute-start(bf16[128,8,96]{0,2,1:T(8,128)(2,1)S(1)} %copy.92), channel_id=1, source_target_pairs={{0,2},{2,4},{4,6},{6,8},{8,10},{10,12},{12,14},{14,16},{16,18},{18... | collective-permute-start | bytes 589832 | tf_op jit(solution)/shard_map/while/body/eval_jaxpr/ppermute | solution.py:19
  1009.3 20.5 collective-permute-start.1
  1030.7 24.1 %collective-permute-start = (bf16[128,8,96]{0,2,1:T(8,128)(2,1)S(1)}, bf16[128,8,96]{0,2,1:T(8,128)(2,1)}, u32[]{:S(2)}, u32[]{:S(2)}) collective-permute-start(bf16[128,8,96]{0,2,1:T(8,128)(2,1)S(1)} %copy.92), channel_id=1, source_target_pairs={{0,2},{2,4},{4,6},{6,8},{8,10},{10,12},{12,14},{14,16},{16,18},{18... | collective-permute-start | bytes 589832 | tf_op jit(solution)/shard_map/while/body/eval_jaxpr/ppermute | solution.py:19
  1034.2 20.5 collective-permute-start.1
  1055.6 24.1 %collective-permute-start = (bf16[128,8,96]{0,2,1:T(8,128)(2,1)S(1)}, bf16[128,8,96]{0,2,1:T(8,128)(2,1)}, u32[]{:S(2)}, u32[]{:S(2)}) collective-permute-start(bf16[128,8,96]{0,2,1:T(8,128)(2,1)S(1)} %copy.92), channel_id=1, source_target_pairs={{0,2},{2,4},{4,6},{6,8},{8,10},{10,12},{12,14},{14,16},{16,18},{18... | collective-permute-start | bytes 589832 | tf_op jit(solution)/shard_map/while/body/eval_jaxpr/ppermute | solution.py:19
  1059.2 20.5 collective-permute-start.1
  1083.8 216.5 %reduce-scatter.12.cloned.1.call-start = ((), (), s32[]{:S(2)}) async-start(), calls=%async_computation.18 | async-start | bytes 4866048 | tf_op jit(solution)/shard_map/reduce_scatter | solution.py:306
  1086.9 354.3 %reduce-scatter.8.cloned.1.call-start = ((), (), s32[]{:S(2)}) async-start(), calls=%async_computation.16 | async-start | bytes 9732096 | tf_op jit(solution)/shard_map/reduce_scatter | solution.py:304
  1093.2 490.3 %reduce-scatter.14.cloned.1.call-start = ((), (), s32[]{:S(2)}) async-start(), calls=%async_computation.19 | async-start | bytes 9732096 | tf_op jit(solution)/shard_map/reduce_scatter | solution.py:307
  1099.4 735.3 %reduce-scatter.16.cloned.1.call-start = ((), (), s32[]{:S(2)}) async-start(), calls=%async_computation.20 | async-start | bytes 25952256 | tf_op jit(solution)/shard_map/reduce_scatter | solution.py:270
  1111.3 976.5 %reduce-scatter.18.cloned.1.call-start = ((), (), s32[]{:S(2)}) async-start(), calls=%async_computation.21 | async-start | bytes 25952256 | tf_op jit(solution)/shard_map/reduce_scatter | solution.py:271
  1122.9 1216.8 %reduce-scatter.20.cloned.1.call-start = ((), (), s32[]{:S(2)}) async-start(), calls=%async_computation.22 | async-start | bytes 25952256 | tf_op jit(solution)/shard_map/reduce_scatter | solution.py:272
  (77 other events, 876.9 us)
Sparse Core Ops, SparseCore 0:
  10.9 60.0 all-gather.9
  73.9 56.2 all-gather.13
  133.1 62.5 all-gather.17
  198.4 43.9 all-gather.11
  244.4 46.0 all-gather.15
  293.3 61.7 all-gather.19
  358.0 94.7 all-gather.21
  455.7 94.2 all-gather.23
  552.9 94.2 all-gather.25
  1083.9 103.3 reduce-scatter.9
  1194.3 106.0 reduce-scatter.11
  1306.7 134.5 reduce-scatter.7
  1448.8 134.7 reduce-scatter.13
  1590.4 244.3 reduce-scatter.15
  1842.7 245.0 reduce-scatter.17
  2094.6 244.9 reduce-scatter.19
where the time goes:
time: 2360 us; the launch traced here: 2350 us
  waiting for transfers between devices  1750 us (74%)
  matrix products  230 us (10%)
  local copies, waits for them, and re-layouts  114 us (5%)
  other arithmetic  80.3 us (3%)
  blocking collectives  79.4 us (3%)
  starting transfers between devices  66.1 us (3%)
    reduce_scatter x1, waiting for transfers between devices, shards(): lax.psum_scatter(up_grad, ('blk', 'fsdp'), scatter_dimension=0, tiled=True)  253 us
    reduce_scatter x1, waiting for transfers between devices, shards(): lax.psum_scatter(down_grad, ('blk', 'fsdp'), scatter_dimension=0, tiled=T...  252 us
    reduce_scatter x1, waiting for transfers between devices, shards(): lax.psum_scatter(gate_grad, ('blk', 'fsdp'), scatter_dimension=0, tiled=T...  251 us
    reduce_scatter x1, waiting for transfers between devices, shards(): lax.psum_scatter(output_grad, ('blk', 'fsdp'), scatter_dimension=0, tiled...  142 us
    reduce_scatter x1, waiting for transfers between devices, shards(): lax.psum_scatter(query_grad, ('blk', 'fsdp'), scatter_dimension=0, tiled=...  141 us
    ppermute x32, waiting for transfers between devices, passed_along_2(): lax.ppermute(x, axis, [(i, (i + by) % length) for i in range(length)])  114 us
    reduce_scatter x1, waiting for transfers between devices, shards(): lax.psum_scatter(value_grad, ('blk', 'fsdp'), scatter_dimension=0, tiled=...  111 us
    all_gather x1, waiting for transfers between devices, fetch_ffn(): lax.all_gather(w_gate, ('blk', 'fsdp'), axis=0, tiled=True)  93.5 us
  transfers between devices with their start and end apart: 80, of which 47 were waited for; matrix products, arithmetic and copies ran while one was open for 16% of the time, Pallas kernels for 0%

commit v1 on v0

--- a/solution.py
+++ b/solution.py
@@ -1,6 +1,8 @@
 import jax
 import jax.numpy as jnp
 from jax import lax
+from jax.experimental import pallas as pl
+from jax.experimental.pallas import tpu as pltpu
 from jax.sharding import PartitionSpec as P
 
 HEADS = 16
@@ -321,6 +323,564 @@
     )
 
 
+CHIPS = 8
+TOK = 128
+PAIR = 2 * HD
+LANES = 128
+LOG2E = 1.4426950408889634
+RING = (0, 2, 4, 6, 7, 5, 3, 1)
+SAME_CORE = [[2 * c + core for c in range(CHIPS)] for core in range(2)]
+
+
+def ring_route(step):
+    return [
+        (RING[k] * 2 + core, RING[(k + step) % CHIPS] * 2 + core)
+        for k in range(CHIPS)
+        for core in range(2)
+    ]
+
+
+def ring_up(value):
+    return lax.ppermute(value, "blk", ring_route(1))
+
+
+def ring_down(value):
+    return lax.ppermute(value, "blk", ring_route(-1))
+
+
+def flipped(value, bit):
+    return lax.ppermute(value, "blk", [(i, i ^ bit) for i in range(2 * CHIPS)])
+
+
+def core_swap(value):
+    return flipped(value, 1)
+
+
+def x_swap(value):
+    return lax.ppermute(value, "fsdp", [(0, 1), (1, 0)])
+
+
+def ring_gather(block):
+    up = block
+    down = block
+    found = [None] * CHIPS
+    found[0] = block
+    for step in (1, 2, 3):
+        up = ring_up(up)
+        down = ring_down(down)
+        found[CHIPS - step] = up
+        found[step] = down
+    half = block.shape[0] // 2
+    found[4] = jnp.concatenate([ring_up(up[:half]), ring_down(down[half:])], axis=0)
+    return found
+
+
+def ring_scatter(parts):
+    low = jnp.bfloat16
+    full = jnp.float32
+    half = parts[0].shape[0] // 2
+    up = ring_up(parts[4][:half].astype(low)).astype(full)
+    down = ring_down(parts[4][half:].astype(low)).astype(full)
+    up = jnp.concatenate([parts[3][:half] + up, parts[3][half:]], axis=0)
+    down = jnp.concatenate([parts[5][:half], parts[5][half:] + down], axis=0)
+    for step in (2, 1, 0):
+        up = ring_up(up.astype(low)).astype(full)
+        down = ring_down(down.astype(low)).astype(full)
+        if step:
+            up = up + parts[step]
+            down = down + parts[CHIPS - step]
+    return parts[0] + (up + down)
+
+
+def gathered_vector(local, bits):
+    for bit, axis_bit in bits:
+        other = x_swap(local) if axis_bit is None else flipped(local, axis_bit)
+        local = jnp.where(
+            bit == 0,
+            jnp.concatenate([local, other], axis=-1),
+            jnp.concatenate([other, local], axis=-1),
+        )
+    return local
+
+
+def scattered_vector(whole, bits):
+    for bit, axis_bit in reversed(bits):
+        half = whole.shape[-1] // 2
+        first, second = whole[..., :half], whole[..., half:]
+        keep = jnp.where(bit == 0, first, second)
+        send = jnp.where(bit == 0, second, first)
+        other = x_swap(send) if axis_bit is None else flipped(send, axis_bit)
+        whole = keep + other
+    return whole
+
+
+def dot_nt(left, right):
+    return lax.dot_general(
+        left, right, (((1,), (1,)), ((), ())), preferred_element_type=jnp.float32
+    )
+
+
+def dot_nn(left, right):
+    return lax.dot_general(
+        left, right, (((1,), (0,)), ((), ())), preferred_element_type=jnp.float32
+    )
+
+
+def project_kernel(table, *refs):
+    blocks = refs[:CHIPS]
+    gain, weight, cosine, sine, normed_out, query_out, kv_out = refs[CHIPS:]
+    for j in range(CHIPS):
+        values = blocks[j][...].astype(jnp.float32)
+        scale = lax.rsqrt(jnp.mean(values * values, axis=-1, keepdims=True) + EPS)
+        normed = (values * scale * gain[...]).astype(jnp.bfloat16)
+        normed_out[j * TOK : (j + 1) * TOK, :] = normed
+        pre = dot_nt(normed, weight[...])
+        rows = pl.ds(pl.multiple_of(table[j] * TOK, TOK), TOK)
+        cos = cosine[rows, :]
+        sin = sine[rows, :]
+        for head in range(3):
+            part = pre[:, head * LANES : (head + 1) * LANES]
+            turned = (part * cos + pltpu.roll(part, LANES // 2, 1) * sin).astype(jnp.bfloat16)
+            if head < 2:
+                query_out[rows, head * LANES : (head + 1) * LANES] = turned
+            else:
+                kv_out[rows, :LANES] = turned
+        kv_out[rows, LANES:] = pre[:, 3 * LANES :].astype(jnp.bfloat16)
+
+
+def project(table, blocks, gain, weight, cosine, sine):
+    tokens = CHIPS * TOK
+    width = blocks[0].shape[1]
+    whole = pl.BlockSpec(memory_space=pltpu.VMEM)
+    return pl.pallas_call(
+        project_kernel,
+        out_shape=(
+            jax.ShapeDtypeStruct((tokens, width), jnp.bfloat16),
+            jax.ShapeDtypeStruct((tokens, 2 * LANES), jnp.bfloat16),
+            jax.ShapeDtypeStruct((tokens, 2 * LANES), jnp.bfloat16),
+        ),
+        in_specs=[pl.BlockSpec(memory_space=pltpu.SMEM)] + [whole] * (CHIPS + 4),
+        out_specs=(whole, whole, whole),
+        compiler_params=pltpu.CompilerParams(vmem_limit_bytes=48 << 20),
+        cost_estimate=pl.CostEstimate(
+            flops=2 * tokens * width * 4 * LANES, bytes_accessed=10 << 20, transcendentals=0
+        ),
+        name="project",
+    )(table, *blocks, gain, weight, cosine, sine)
+
+
+def key_index(core, count):
+    row = lax.broadcasted_iota(jnp.int32, (count, 1), 0)
+    return (row // TOK) * (2 * TOK) + core * TOK + row % TOK
+
+
+def query_index(core, chip):
+    lane = lax.broadcasted_iota(jnp.int32, (1, 2 * TOK), 1)
+    return lane % TOK + (2 * chip + core) * TOK
+
+
+def both_heads(ref, rows):
+    return jnp.concatenate([ref[rows, :LANES], ref[rows, LANES:]], axis=0)
+
+
+def attend_kernel(core_ref, query, own, peer, begin, attended, mixed, lse):
+    core = core_ref[0]
+    factor = HD ** (-0.5) * LOG2E
+    sides = ((own, core), (peer, 1 - core))
+    values_t = [jnp.transpose(kv[:, LANES:]) for kv, _ in sides]
+    for chip in range(CHIPS):
+        count = (chip + 1) * TOK
+        rows = slice(chip * TOK, count)
+        queries = both_heads(query, rows)
+        at = query_index(core, chip)
+        first = begin[chip]
+        scores = []
+        for kv, side in sides:
+            raw = dot_nt(kv[:count, :LANES], queries) * factor
+            keys_at = key_index(side, count)
+            scores.append(jnp.where((keys_at <= at) & (keys_at >= first), raw, NEG))
+        top = jnp.maximum(
+            jnp.max(scores[0], axis=0, keepdims=True), jnp.max(scores[1], axis=0, keepdims=True)
+        )
+        weights = [jnp.exp2(part - top) for part in scores]
+        total = jnp.sum(weights[0], axis=0, keepdims=True) + jnp.sum(
+            weights[1], axis=0, keepdims=True
+        )
+        mix = dot_nn(values_t[0][:, :count], weights[0].astype(jnp.bfloat16)) + dot_nn(
+            values_t[1][:, :count], weights[1].astype(jnp.bfloat16)
+        )
+        mix = mix / total
+        mixed[chip] = mix
+        lse[chip] = top + jnp.log2(total)
+        back = jnp.transpose(mix).astype(jnp.bfloat16)
+        attended[rows, :HD] = back[:TOK, :HD]
+        attended[rows, HD:] = back[TOK:, :HD]
+
+
+def attend_heads(core, query, own, peer, begin):
+    tokens = CHIPS * TOK
+    whole = pl.BlockSpec(memory_space=pltpu.VMEM)
+    return pl.pallas_call(
+        attend_kernel,
+        out_shape=(
+            jax.ShapeDtypeStruct((tokens, PAIR), jnp.bfloat16),
+            jax.ShapeDtypeStruct((CHIPS, LANES, 2 * TOK), jnp.float32),
+            jax.ShapeDtypeStruct((CHIPS, 1, 2 * TOK), jnp.float32),
+        ),
+        in_specs=[pl.BlockSpec(memory_space=pltpu.SMEM)] + [whole] * 4,
+        out_specs=(whole, whole, whole),
+        compiler_params=pltpu.CompilerParams(vmem_limit_bytes=48 << 20),
+        cost_estimate=pl.CostEstimate(
+            flops=4 * 36 * 256 * 256 * LANES, bytes_accessed=5 << 20, transcendentals=36 * 256 * 256
+        ),
+        name="attend",
+    )(core, query, own, peer, begin)
+
+
+def attend_back_kernel(
+    core_ref, query, own, peer, begin, grad_out, mixed, lse, cosine, sine,
+    grad_query, grad_own, grad_peer,
+):
+    core = core_ref[0]
+    scale = HD ** (-0.5)
+    factor = scale * LOG2E
+    sides = ((own, core, grad_own), (peer, 1 - core, grad_peer))
+    keys_t = [jnp.transpose(kv[:, :LANES]) for kv, _, _ in sides]
+    grad_own[...] = jnp.zeros_like(grad_own)
+    grad_peer[...] = jnp.zeros_like(grad_peer)
+    pad = jnp.zeros((TOK, LANES - HD), jnp.bfloat16)
+    for chip in range(CHIPS):
+        count = (chip + 1) * TOK
+        rows = slice(chip * TOK, count)
+        queries = both_heads(query, rows)
+        grad_rows = grad_out[rows, :]
+        grads = jnp.concatenate(
+            [
+                jnp.concatenate([grad_rows[:, :HD], pad], axis=1),
+                jnp.concatenate([grad_rows[:, HD:], pad], axis=1),
+            ],
+            axis=0,
+        )
+        delta = jnp.sum(
+            jnp.transpose(grads.astype(jnp.float32)) * mixed[chip], axis=0, keepdims=True
+        )
+        at = query_index(core, chip)
+        first = begin[chip]
+        level = lse[chip]
+        grad_q = jnp.zeros((LANES, 2 * TOK), jnp.float32)
+        for (kv, side, grad_kv), key_t in zip(sides, keys_t):
+            raw = dot_nt(kv[:count, :LANES], queries) * factor
+            keys_at = key_index(side, count)
+            allowed = (keys_at <= at) & (keys_at >= first)
+            probs = jnp.exp2(jnp.where(allowed, raw - level, NEG))
+            grad_probs = dot_nt(kv[:count, LANES:], grads)
+            grad_scores = (probs * (grad_probs - delta)).astype(jnp.bfloat16)
+            grad_kv[:count, LANES:] += dot_nn(probs.astype(jnp.bfloat16), grads)
+            grad_kv[:count, :LANES] += dot_nn(grad_scores, queries)
+            grad_q += dot_nn(key_t[:, :count], grad_scores)
+        grad_q = jnp.transpose(grad_q) * scale
+        cos = cosine[rows, :]
+        sin = sine[rows, :]
+        for head in range(2):
+            part = grad_q[head * TOK : (head + 1) * TOK]
+            turned = part * cos - pltpu.roll(part, LANES // 2, 1) * sin
+            grad_query[rows, head * LANES : (head + 1) * LANES] = turned.astype(jnp.bfloat16)
+    for grad_kv in (grad_own, grad_peer):
+        grad_kv[:, :LANES] = grad_kv[:, :LANES] * scale
+
+
+def attend_back(core, query, own, peer, begin, grad_out, mixed, lse, cosine, sine):
+    tokens = CHIPS * TOK
+    whole = pl.BlockSpec(memory_space=pltpu.VMEM)
+    return pl.pallas_call(
+        attend_back_kernel,
+        out_shape=(
+            jax.ShapeDtypeStruct((tokens, 2 * LANES), jnp.bfloat16),
+            jax.ShapeDtypeStruct((tokens, 2 * LANES), jnp.float32),
+            jax.ShapeDtypeStruct((tokens, 2 * LANES), jnp.float32),
+        ),
+        in_specs=[pl.BlockSpec(memory_space=pltpu.SMEM)] + [whole] * 9,
+        out_specs=(whole, whole, whole),
+        compiler_params=pltpu.CompilerParams(vmem_limit_bytes=48 << 20),
+        cost_estimate=pl.CostEstimate(
+            flops=10 * 36 * 256 * 256 * LANES, bytes_accessed=8 << 20, transcendentals=36 * 256 * 256
+        ),
+        name="attend_back",
+    )(core, query, own, peer, begin, grad_out, mixed, lse, cosine, sine)
+
+
+def collect_kernel(table, grad_query, grad_own, grad_other, cosine, sine, out):
+    for j in range(CHIPS):
+        rows = pl.ds(pl.multiple_of(table[j] * TOK, TOK), TOK)
+        here = slice(j * TOK, (j + 1) * TOK)
+        out[here, : 2 * LANES] = grad_query[rows, :]
+        total = grad_own[rows, :] + grad_other[rows, :]
+        part = total[:, :LANES]
+        turned = part * cosine[rows, :] - pltpu.roll(part, LANES // 2, 1) * sine[rows, :]
+        out[here, 2 * LANES : 3 * LANES] = turned.astype(jnp.bfloat16)
+        out[here, 3 * LANES :] = total[:, LANES:].astype(jnp.bfloat16)
+
+
+def collect(table, grad_query, grad_own, grad_other, cosine, sine):
+    tokens = CHIPS * TOK
+    whole = pl.BlockSpec(memory_space=pltpu.VMEM)
+    return pl.pallas_call(
+        collect_kernel,
+        out_shape=jax.ShapeDtypeStruct((tokens, 4 * LANES), jnp.bfloat16),
+        in_specs=[pl.BlockSpec(memory_space=pltpu.SMEM)] + [whole] * 5,
+        out_specs=whole,
+        compiler_params=pltpu.CompilerParams(vmem_limit_bytes=32 << 20),
+        cost_estimate=pl.CostEstimate(
+            flops=8 * tokens * LANES, bytes_accessed=5 << 20, transcendentals=0
+        ),
+        name="collect",
+    )(table, grad_query, grad_own, grad_other, cosine, sine)
+
+
+def head_weights(w_query, w_key, w_value, core, side):
+    packed = jnp.concatenate([w_query, w_key, w_value], axis=0)
+    other = x_swap(packed)
+    pair = jnp.where(side == 0, jnp.stack([packed, other]), jnp.stack([other, packed]))
+    far = core_swap(pair)
+    quad = jnp.where(core == 0, jnp.stack([pair, far]), jnp.stack([far, pair]))
+    width = w_query.shape[1]
+    nq = w_query.shape[0]
+    nk = w_key.shape[0]
+    gap = jnp.zeros((LANES // 2 - HD // 2, width), w_query.dtype)
+    rows = []
+    for c in range(2):
+        for f in range(2):
+            rows += [quad[c, f, :nq], gap]
+    for c in range(2):
+        rows += [quad[c, 0, nq : nq + nk], quad[c, 1, nq : nq + nk], gap]
+    for c in range(2):
+        rows += [quad[c, 0, nq + nk :], quad[c, 1, nq + nk :]]
+    rows += [gap, gap]
+    return jnp.concatenate(rows, axis=0)
+
+
+def head_gradient(grad, core, side):
+    half = LANES // 2
+    nq = HD // 2
+    nk = HD // 4
+    pieces = []
+    for c in range(2):
+        for f in range(2):
+            piece = [
+                grad[c * LANES + f * half : c * LANES + f * half + nq],
+                grad[2 * LANES + c * half + f * nk : 2 * LANES + c * half + (f + 1) * nk],
+                grad[3 * LANES + (2 * c + f) * nk : 3 * LANES + (2 * c + f + 1) * nk],
+            ]
+            pieces.append(jnp.concatenate(piece, axis=0))
+    pairs = [jnp.stack(pieces[:2]), jnp.stack(pieces[2:])]
+    mine = jnp.where(core == 0, pairs[0], pairs[1])
+    mine = mine + core_swap(jnp.where(core == 0, pairs[1], pairs[0]))
+    total = jnp.where(side == 0, mine[0], mine[1]) + x_swap(
+        jnp.where(side == 0, mine[1], mine[0])
+    )
+    return total[:nq], total[nq : nq + nk], total[nq + nk :]
+
+
+def plane_shards(
+    tokens,
+    cotangent,
+    segments,
+    positions,
+    gain_attn,
+    gain_ffn,
+    w_query,
+    w_key,
+    w_value,
+    w_output,
+    w_gate,
+    w_up,
+    w_down,
+):
+    full = jnp.float32
+    low = jnp.bfloat16
+    block = tokens[0]
+    width = block.shape[1]
+    index = lax.axis_index("blk")
+    side = lax.axis_index("fsdp")
+    core = index % 2
+    chip = index // 2
+    spot = jnp.where(chip % 2 == 0, chip // 2, CHIPS - 1 - chip // 2)
+    table = jnp.asarray(RING, jnp.int32)[(spot + jnp.arange(CHIPS, dtype=jnp.int32)) % CHIPS]
+    core_id = core.astype(jnp.int32)[None]
+    bits = [(side, None)] + [((index >> b) & 1, 1 << b) for b in range(4)]
+
+    x_blocks = ring_gather(block)
+    gains = gathered_vector(jnp.stack([gain_attn, gain_ffn]), bits).astype(full)
+    gain_one = gains[:1]
+    gain_two = gains[1:]
+    w_heads = head_weights(w_query, w_key, w_value, core, side)
+    w_out = lax.all_gather(w_output, ("blk", "fsdp"), axis=0, tiled=True)
+
+    segs = segments[0]
+    local = jnp.arange(TOK, dtype=jnp.int32)
+    own_segs = lax.dynamic_index_in_dim(segs.reshape(CHIPS, 2, TOK), core, 1, keepdims=False)
+    begin = jnp.zeros_like(own_segs)
+    for number in range(1, 4):
+        begin = jnp.where(own_segs == number, jnp.sum((segs < number).astype(jnp.int32)), begin)
+    where = jnp.arange(CHIPS, dtype=jnp.int32)[:, None] * (2 * TOK) + core * TOK + local[None, :]
+    place = (where - begin).reshape(CHIPS * TOK)
+    half = HD // 2
+    freqs = ROPE_BASE ** (-(jnp.arange(half, dtype=full) * 2.0 / HD))
+    spare = jnp.zeros((LANES // 2 - half,), full)
+    both = jnp.concatenate([freqs, spare, freqs, spare])
+    angles = place.astype(full)[:, None] * both[None, :]
+    sign = jnp.where(jnp.arange(LANES) < LANES // 2, -1.0, 1.0).astype(full)
+    cosine = jnp.cos(angles)
+    sine = jnp.sin(angles) * sign[None, :]
+    begin2 = jnp.concatenate([begin, begin], axis=1)[:, None, :]
+
+    normed, query, kv = project(table, x_blocks, gain_one, w_heads, cosine, sine)
+    kv_peer = core_swap(kv)
+    attended_heads, mixed, lse = attend_heads(core_id, query, kv, kv_peer, begin2)
+    attended = lax.all_to_all(
+        attended_heads.reshape(CHIPS, TOK, PAIR),
+        "blk",
+        split_axis=0,
+        concat_axis=0,
+        axis_index_groups=SAME_CORE,
+        tiled=True,
+    )
+    attended = jnp.transpose(attended, (1, 0, 2)).reshape(TOK, CHIPS * PAIR)
+
+    x_own = block.astype(full)
+    middle = x_own + product_t(attended, w_out)
+    second_scale = rms_scale(middle)
+    normed_two = (middle * second_scale * gain_two).astype(low)
+
+    count = w_gate.shape[0]
+    packed = jnp.concatenate([w_gate, w_up, w_down], axis=0)
+    packed_x = x_swap(packed)
+    packed_c = core_swap(packed)
+    packed_cx = core_swap(packed_x)
+    four = (packed, packed_x, packed_c, packed_cx)
+    gates = [p[:count] for p in four]
+    ups = [p[count : 2 * count] for p in four]
+    w_gu = jnp.concatenate(gates[:2] + ups[:2] + gates[2:] + ups[2:], axis=0)
+    w_dn = jnp.concatenate([p[2 * count :] for p in four], axis=0)
+
+    tied, _ = lax.optimization_barrier((cotangent[0], x_blocks[4]))
+    e_blocks = ring_gather(tied)
+    e_all = jnp.concatenate(e_blocks, axis=0)
+    grad_hidden_all = product_t(e_all, w_dn)
+
+    h_blocks = ring_gather(normed_two)
+    wide = 2 * count
+    groups = ((0, 1, 7), (2, 6), (3, 4, 5))
+    z_parts = [None] * CHIPS
+    d_parts = [None] * CHIPS
+    hiddens = [None] * CHIPS
+    grads_gu = [None] * CHIPS
+    for group in groups:
+        rows = jnp.concatenate([h_blocks[j] for j in group], axis=0)
+        grad_hidden = jnp.concatenate(
+            [grad_hidden_all[j * TOK : (j + 1) * TOK] for j in group], axis=0
+        )
+        pre = product_t(rows, w_gu)
+        hid = []
+        dgu = []
+        for part in range(2):
+            gate = pre[:, part * 2 * wide : part * 2 * wide + wide]
+            up = pre[:, part * 2 * wide + wide : (part + 1) * 2 * wide]
+            dhid = grad_hidden[:, part * wide : (part + 1) * wide]
+            sigma = jax.nn.sigmoid(gate)
+            activated = gate * sigma
+            hid.append((activated * up).astype(low))
+            dgu.append((dhid * up * sigma * (1.0 + gate * (1.0 - sigma))).astype(low))
+            dgu.append((dhid * activated).astype(low))
+        hid = jnp.concatenate(hid, axis=1)
+        dgu = jnp.concatenate(dgu, axis=1)
+        back = product(dgu, w_gu)
+        branch = product(hid, w_dn)
+        for n, j in enumerate(group):
+            cut = slice(n * TOK, (n + 1) * TOK)
+            d_parts[j] = back[cut]
+            z_parts[j] = branch[cut]
+            hiddens[j] = hid[cut]
+            grads_gu[j] = dgu[cut]
+    grad_normed_two = ring_scatter(d_parts)
+    branch = ring_scatter(z_parts)
+    result = (middle + branch).astype(low)
+
+    h_all = jnp.concatenate(h_blocks, axis=0)
+    hid_all = jnp.concatenate(hiddens, axis=0)
+    dgu_all = jnp.concatenate(grads_gu, axis=0)
+    send_gu = product_tn(dgu_all[:, 2 * wide :], h_all)
+    send_dn = product_tn(hid_all[:, wide:], e_all)
+    keep_gu = product_tn(dgu_all[:, : 2 * wide], h_all)
+    keep_dn = product_tn(hid_all[:, :wide], e_all)
+    sum_gu = keep_gu + core_swap(send_gu)
+    sum_dn = keep_dn + core_swap(send_dn)
+    sent = jnp.concatenate([sum_gu[count:wide], sum_gu[wide + count :], sum_dn[count:]], axis=0)
+    received = x_swap(sent)
+    gate_grad = sum_gu[:count] + received[:count]
+    up_grad = sum_gu[wide : wide + count] + received[count:wide]
+    down_grad = sum_dn[:count] + received[wide:]
+
+    grad_in = cotangent[0]
+    grad_middle_norm, second_gain_grad = norm_back(
+        grad_normed_two, middle, second_scale, gain_two
+    )
+    grad_middle = grad_in.astype(full) + grad_middle_norm
+    grad_branch = grad_middle.astype(low)
+    grad_attended = product(grad_branch, w_out).astype(low)
+    grad_attended = jnp.transpose(grad_attended.reshape(TOK, CHIPS, PAIR), (1, 0, 2))
+    grad_heads = lax.all_to_all(
+        grad_attended,
+        "blk",
+        split_axis=0,
+        concat_axis=0,
+        axis_index_groups=SAME_CORE,
+        tiled=True,
+    ).reshape(CHIPS * TOK, PAIR)
+    output_grad = lax.psum_scatter(
+        product_tn(grad_branch, attended).astype(low),
+        ("blk", "fsdp"),
+        scatter_dimension=0,
+        tiled=True,
+    ).astype(full)
+
+    grad_query, grad_own, grad_peer = attend_back(
+        core_id, query, kv, kv_peer, begin2, grad_heads, mixed, lse, cosine, sine
+    )
+    grad_heads_all = collect(table, grad_query, grad_own, core_swap(grad_peer), cosine, sine)
+    grad_normed_all = product(grad_heads_all, w_heads)
+    parts = [grad_normed_all[j * TOK : (j + 1) * TOK] for j in range(CHIPS)]
+    first_gain_grad = 0.0
+    for j in range(CHIPS):
+        values = x_blocks[j].astype(full)
+        first_gain_grad = first_gain_grad + jnp.sum(
+            parts[j] * values * rms_scale(values), axis=0
+        )
+    gain_grads = scattered_vector(jnp.stack([first_gain_grad, second_gain_grad]), bits)
+    grad_normed = ring_scatter(parts)
+    heads_grad = product_tn(grad_heads_all, normed)
+    query_grad, key_grad, value_grad = head_gradient(heads_grad, core, side)
+    grad_x_norm, _ = norm_back(grad_normed, x_own, rms_scale(x_own), gain_one)
+    grad_tokens = grad_middle + grad_x_norm
+    return (
+        result[None],
+        grad_tokens[None],
+        gain_grads[0],
+        gain_grads[1],
+        query_grad,
+        key_grad,
+        value_grad,
+        output_grad,
+        gate_grad,
+        up_grad,
+        down_grad,
+    )
+
+
+def by_plane(mesh):
+    return dict(mesh.shape) == {"blk": 2 * CHIPS, "fsdp": 2} and KVH == CHIPS
+
+
 def solution(mesh):
     in_specs = (
         P("fsdp", "blk", None),
@@ -350,4 +910,5 @@
         P(("blk", "fsdp"), None),
         P(("blk", "fsdp"), None),
     )
-    return jax.shard_map(shards, mesh=mesh, in_specs=in_specs, out_specs=out_specs, check_vma=False)
+    body = plane_shards if by_plane(mesh) else shards
+    return jax.shard_map(body, mesh=mesh, in_specs=in_specs, out_specs=out_specs, check_vma=False)

time: 2360 us -> 474 us (0.20)
  waiting for transfers between devices: 1750 us -> 228 us
  matrix products: 230 us -> 43.3 us
  blocking collectives: 79.4 us -> 0 us
  local copies, waits for them, and re-layouts: 114 us -> 52.4 us
  other arithmetic: 80.3 us -> 20.6 us
    reduce_scatter x7 -> x1, waiting for transfers between devices: 1150 us -> 0.01 us  [plane_shards(): lax.psum_scatter(product_tn(grad_branch, attended).astype(low), ('blk', '...]
    all_gather x9 -> x1, waiting for transfers between devices: 480 us -> 0.01 us  [plane_shards(): w_out = lax.all_gather(w_output, ('blk', 'fsdp'), axis=0, tiled=True)]
    ppermute x64 -> x70, waiting for transfers between devices: 114 us -> 223 us  [the longest x24 93.2 us: ring_up(): return lax.ppermute(value, 'blk', ring_route(1))]
    dot_general x88 -> x0, matrix products: 109 us -> none  [the longest x16 30.9 us: step(): jnp.einsum('hgqk,qhgd->khd', grad_scores, queries, preferred_element_type...]
    unnamed x2 -> x0, blocking collectives: 79.4 us -> none
    convert_element_type x41 -> x11, other arithmetic: 56 us -> 5.97 us  [the longest x1 2.01 us: plane_shards(): angles = place.astype(full)[:, None] * both[None, :]]
    while x68 -> x0, local copies, waits for them, and re-layouts: 40.8 us -> none
    dynamic_slice x41 -> x1, local copies, waits for them, and re-layouts: 33.6 us -> 0.01 us  [plane_shards(): lax.dynamic_index_in_dim(segs.reshape(CHIPS, 2, TOK), core, 1, keepdims=F...]
  transfers between devices with their start and end apart: 80 -> 74, of which waited for: 47 -> 45; matrix products, arithmetic and copies ran while one was open for 16% -> 19% of each run, Pallas kernels for 0% -> 5%
where the time goes in v1:
time: 474 us; the launch traced here: 466 us
  waiting for transfers between devices  228 us (48%)
  starting transfers between devices  82.3 us (17%)
  local copies, waits for them, and re-layouts  52.4 us (11%)
  matrix products  43.3 us (9%)
  Pallas kernels  23.3 us (5%)
  other arithmetic  20.6 us (4%)
  between operations  15.9 us (3%)
    ppermute x24, waiting for transfers between devices, ring_up(): return lax.ppermute(value, 'blk', ring_route(1))  93.2 us
    ppermute x6, waiting for transfers between devices, x_swap(): return lax.ppermute(value, 'fsdp', [(0, 1), (1, 0)])  82.8 us
    ppermute x24, waiting for transfers between devices, ring_down(): return lax.ppermute(value, 'blk', ring_route(-1))  35.7 us
    unnamed x153, local copies, waits for them, and re-layouts  32.6 us
    ppermute x24, starting transfers between devices, ring_down(): return lax.ppermute(value, 'blk', ring_route(-1))  29.4 us
    ppermute x24, starting transfers between devices, ring_up(): return lax.ppermute(value, 'blk', ring_route(1))  25.4 us
    dot_general x6, matrix products, product_tn(): lax.dot_general(left, right, (((0,), (0,)), ((), ())), preferred_element_...  22.1 us
    dot_general x5, matrix products, product_t(): lax.dot_general(left, right, (((1,), (1,)), ((), ())), preferred_element_...  12 us
  transfers between devices with their start and end apart: 74, of which 45 were waited for; matrix products, arithmetic and copies ran while one was open for 19% of the time, Pallas kernels for 5%

profile of v1, /device:TPU:0, one launch (start us, length us, event | category | flops | bytes accessed | tf_op | source)
XLA Modules:
  0.0 465.9 jit_solution(3586365764804186273)
XLA Ops:
  7.3 3.1 collective-permute-start.3
  20.0 2.0 fusion.105
  24.0 19.7 %collective-permute-done.8 = bf16[2,48]{1,0:T(2,128)(2,1)S(1)} collective-permute-done((bf16[2,48]{1,0:T(2,128)(2,1)S(1)}, bf16[2,48]{1,0:T(2,128)(2,1)S(1)}, u32[]{:S(2)}, u32[]{:S(2)}) %collective-permute-start.8) | collective-permute-done | bytes 224 | tf_op jit(solution)/shard_map/ppermute | solution.py:360
  52.3 2.7 collective-permute-start.12
  58.5 5.2 %collective-permute-done.13 = bf16[96,1536]{1,0:T(8,128)(2,1)S(1)} collective-permute-done((bf16[96,1536]{1,0:T(8,128)(2,1)S(1)}, bf16[96,1536]{1,0:T(8,128)(2,1)S(1)}, u32[]{:S(2)}, u32[]{:S(2)}) %collective-permute-start.13) | collective-permute-done | bytes 294944 | tf_op jit(solution)/shard_map/ppermute | solution.py:360
  66.5 15.3 %collective-permute-done.4.refs_6_ = bf16[128,1536]{1,0:T(8,128)(2,1)S(1)} collective-permute-done((bf16[128,1536]{1,0:T(8,128)(2,1)S(1)}, bf16[128,1536]{1,0:T(8,128)(2,1)S(1)}, u32[]{:S(2)}, u32[]{:S(2)}) %collective-permute-start.4) | collective-permute-done | bytes 393248 | tf_op jit(solution)/shard_map/ppermute | solution.py:344
  81.8 3.0 collective-permute-start.5
  88.4 8.4 %collective-permute-done.5.refs_5_ = bf16[128,1536]{1,0:T(8,128)(2,1)S(1)} collective-permute-done((bf16[128,1536]{1,0:T(8,128)(2,1)S(1)}, bf16[128,1536]{1,0:T(8,128)(2,1)S(1)}, u32[]{:S(2)}, u32[]{:S(2)}) %collective-permute-start.5) | collective-permute-done | bytes 393248 | tf_op jit(solution)/shard_map/ppermute | solution.py:344
  101.8 2.1 fusion.126
  107.9 7.4 %project.1 = (bf16[1024,1536]{1,0:T(8,128)(2,1)}, bf16[1024,256]{1,0:T(8,128)(2,1)S(1)}, bf16[1024,256]{1,0:T(8,128)(2,1)S(1)}) custom-call(s32[8]{0:T(128)S(1)} %gather_fusion, bf16[128,1536]{1,0:T(8,128)(2,1)S(1)} %bitcast.125, bf16[128,1536]{1,0:T(8,128)(2,1)S(1)} %collective-permute-done.refs_1_, bf16[128,1536]{1,0:T(8,128)(2,1)S(1)} %collective-permute-done.1.refs_2_, ...), custom_call_target="tpu_custom_call" | custom-call | flops 1610612736 | bytes 10485760 | tf_op jit(solution)/shard_map/project/pallas_call | solution.py:455
  121.8 5.4 %attend.1 = (bf16[1024,192]{1,0:T(8,128)(2,1)S(1)}, f32[8,128,256]{2,1,0:T(8,128)S(1)}, f32[8,1,256]{2,1,0:T(1,128)S(1)}) custom-call(s32[1]{0:T(128)} %bitcast.1.core_ref, bf16[1024,256]{1,0:T(8,128)(2,1)S(1)} %get-tuple-element.21.query, bf16[1024,256]{1,0:T(8,128)(2,1)S(1)} %get-tuple-element.22.own, bf16[1024,256]{1,0:T(8,128)(2,1)S(1)} %collective-permute-done.15.peer, ...), custom_call_target="tpu_custom_call" | custom-call | flops 1207959552 | bytes 5242880 | tf_op jit(solution)/shard_map/attend/pallas_call | solution.py:523
  129.0 2.0 copy.26
  131.0 4.1 all-to-all-start
  140.8 2.1 fusion.127
  142.8 2.1 fusion.128
  144.9 5.6 %collective-permute-done.40 = bf16[128,1536]{1,0:T(8,128)(2,1)S(1)} collective-permute-done((bf16[128,1536]{1,0:T(8,128)(2,1)}, bf16[128,1536]{1,0:T(8,128)(2,1)S(1)}, u32[]{:S(2)}, u32[]{:S(2)}) %collective-permute-start.40) | collective-permute-done | bytes 393248 | tf_op jit(solution)/shard_map/ppermute | solution.py:344
  150.5 2.8 collective-permute-start.41
  154.1 2.9 collective-permute-done.41
  157.8 2.1 collective-permute-done.42
  164.9 4.3 multiply_reduce_fusion.2
  171.5 3.9 fusion.118
  175.4 3.4 collective-permute-done.16
  186.3 4.4 collective-permute-done.21
  197.1 6.8 %collective-permute-done.24 = bf16[128,1536]{1,0:T(8,128)(2,1)S(1)} collective-permute-done((bf16[128,1536]{1,0:T(8,128)(2,1)S(1)}, bf16[128,1536]{1,0:T(8,128)(2,1)S(1)}, u32[]{:S(2)}, u32[]{:S(2)}) %collective-permute-start.24) | collective-permute-done | bytes 393248 | tf_op jit(solution)/shard_map/ppermute | solution.py:344
  206.1 3.5 collective-permute-done.25
  215.4 4.4 fusion.62
  224.1 7.3 %collective-permute-done.43 = bf16[64,1536]{1,0:T(8,128)(2,1)S(1)} collective-permute-done((bf16[64,1536]{1,0:T(8,128)(2,1)S(1)}, bf16[64,1536]{1,0:T(8,128)(2,1)S(1)}, u32[]{:S(2)}, u32[]{:S(2)}) %collective-permute-start.43) | collective-permute-done | bytes 196640 | tf_op jit(solution)/shard_map/ppermute | solution.py:344
  236.6 7.7 %collective-permute-done.48 = bf16[128,1536]{1,0:T(8,128)(2,1)S(1)} collective-permute-done((bf16[128,1536]{1,0:T(8,128)(2,1)S(1)}, bf16[128,1536]{1,0:T(8,128)(2,1)S(1)}, u32[]{:S(2)}, u32[]{:S(2)}) %collective-permute-start.48) | collective-permute-done | bytes 393248 | tf_op jit(solution)/shard_map/ppermute | solution.py:348
  247.8 4.9 %collective-permute-done.32 = bf16[128,1536]{1,0:T(8,128)(2,1)S(1)} collective-permute-done((bf16[128,1536]{1,0:T(8,128)(2,1)S(1)}, bf16[128,1536]{1,0:T(8,128)(2,1)S(1)}, u32[]{:S(2)}, u32[]{:S(2)}) %collective-permute-start.32) | collective-permute-done | bytes 393248 | tf_op jit(solution)/shard_map/ppermute | solution.py:348
  256.2 6.2 %collective-permute-done.45 = bf16[128,1536]{1,0:T(8,128)(2,1)S(1)} collective-permute-done((bf16[128,1536]{1,0:T(8,128)(2,1)S(1)}, bf16[128,1536]{1,0:T(8,128)(2,1)S(1)}, u32[]{:S(2)}, u32[]{:S(2)}) %collective-permute-start.45) | collective-permute-done | bytes 393248 | tf_op jit(solution)/shard_map/ppermute | solution.py:344
  264.6 6.1 %collective-permute-done.29 = bf16[128,1536]{1,0:T(8,128)(2,1)S(1)} collective-permute-done((bf16[128,1536]{1,0:T(8,128)(2,1)S(1)}, bf16[128,1536]{1,0:T(8,128)(2,1)S(1)}, u32[]{:S(2)}, u32[]{:S(2)}) %collective-permute-start.29) | collective-permute-done | bytes 393248 | tf_op jit(solution)/shard_map/ppermute | solution.py:344
  273.0 6.1 %collective-permute-done.46 = bf16[128,1536]{1,0:T(8,128)(2,1)S(1)} collective-permute-done((bf16[128,1536]{1,0:T(8,128)(2,1)S(1)}, bf16[128,1536]{1,0:T(8,128)(2,1)S(1)}, u32[]{:S(2)}, u32[]{:S(2)}) %collective-permute-start.46) | collective-permute-done | bytes 393248 | tf_op jit(solution)/shard_map/ppermute | solution.py:344
  279.5 6.2 %collective-permute-done.30 = bf16[128,1536]{1,0:T(8,128)(2,1)S(1)} collective-permute-done((bf16[128,1536]{1,0:T(8,128)(2,1)S(1)}, bf16[128,1536]{1,0:T(8,128)(2,1)S(1)}, u32[]{:S(2)}, u32[]{:S(2)}) %collective-permute-start.30) | collective-permute-done | bytes 393248 | tf_op jit(solution)/shard_map/ppermute | solution.py:344
  291.2 4.1 all-to-all-start.1
  300.9 4.7 %all-to-all-done.1 = bf16[8,128,192]{1,2,0:T(8,128)(2,1)} async-done(((bf16[8,128,192]{1,2,0:T(8,128)(2,1)}), bf16[8,128,192]{1,2,0:T(8,128)(2,1)}, u32[]{:S(2)}, u32[]{:S(2)}) %all-to-all-start.1) | async-done | bytes 393248 | tf_op jit(solution)/shard_map/all_to_all | solution.py:832
  305.7 2.0 copy.28
  311.9 8.9 %attend_back.1 = (bf16[1024,256]{1,0:T(8,128)(2,1)S(1)}, f32[1024,256]{1,0:T(8,128)S(1)}, f32[1024,256]{1,0:T(8,128)}) custom-call(s32[1]{0:T(128)} %bitcast.1.core_ref, bf16[1024,256]{1,0:T(8,128)(2,1)S(1)} %copy-done.16, bf16[1024,256]{1,0:T(8,128)(2,1)S(1)} %copy-done.12, bf16[1024,256]{1,0:T(8,128)(2,1)S(1)} %copy-done.14, ...), custom_call_target="tpu_custom_call" | custom-call | flops 3019898880 | bytes 8388608 | tf_op jit(solution)/shard_map/attend_back/pallas_call | solution.py:595
  320.8 3.5 fusion.14
  324.8 4.6 convolution_convert_fusion
  329.4 3.6 convolution_add_fusion.1
  338.6 2.1 fusion.133
  343.2 4.6 collective-permute-done.52
  350.9 7.5 %collective-permute-done.57 = bf16[128,1536]{1,0:T(8,128)(2,1)S(1)} collective-permute-done((bf16[128,1536]{1,0:T(8,128)(2,1)S(1)}, bf16[128,1536]{1,0:T(8,128)(2,1)S(1)}, u32[]{:S(2)}, u32[]{:S(2)}) %collective-permute-start.57) | collective-permute-done | bytes 393248 | tf_op jit(solution)/shard_map/ppermute | solution.py:348
  361.6 4.0 convolution_add_fusion
  365.6 2.7 collective-permute-done.54
  371.6 5.6 %collective-permute-done.55 = bf16[128,1536]{1,0:T(8,128)(2,1)S(1)} collective-permute-done((bf16[128,1536]{1,0:T(8,128)(2,1)S(1)}, bf16[128,1536]{1,0:T(8,128)(2,1)S(1)}, u32[]{:S(2)}, u32[]{:S(2)}) %collective-permute-start.55) | collective-permute-done | bytes 393248 | tf_op jit(solution)/shard_map/ppermute | solution.py:344
  384.7 2.7 collective-permute-done.61
  395.2 58.0 %collective-permute-done.64 = f32[2,48]{1,0:T(2,128)S(1)} collective-permute-done((f32[2,48]{1,0:T(2,128)S(1)}, f32[2,48]{1,0:T(2,128)S(1)}, u32[]{:S(2)}, u32[]{:S(2)}) %collective-permute-start.64) | collective-permute-done | bytes 416 | tf_op jit(solution)/shard_map/ppermute | solution.py:360
  (409 shorter events, 158.5 us)
Async XLA Ops:
  7.3 157.6 %all-gather.2.cloned.1.call-start = ((), (), s32[]{:S(2)}) async-start(), calls=%async_computation.3 | async-start | bytes 4866048 | tf_op jit(solution)/shard_map/all_gather | solution.py:717
  7.3 56.7 %collective-permute-start.3 = (bf16[128,1536]{1,0:T(8,128)(2,1)}, bf16[128,1536]{1,0:T(8,128)(2,1)S(1)}, u32[]{:S(2)}, u32[]{:S(2)}) collective-permute-start(bf16[128,1536]{1,0:T(8,128)(2,1)} %bitcast.123), channel_id=1, source_target_pairs={{0,8},{2,10},{8,16},{10,18},{16,24},{18,26},{24,28},{26,30},{28,20... | collective-permute-start | bytes 1179656 | tf_op jit(solution)/shard_map/ppermute | solution.py:344
  10.4 55.4 %collective-permute-start = (bf16[128,1536]{1,0:T(8,128)(2,1)}, bf16[128,1536]{1,0:T(8,128)(2,1)S(1)}, u32[]{:S(2)}, u32[]{:S(2)}) collective-permute-start(bf16[128,1536]{1,0:T(8,128)(2,1)} %bitcast.124), channel_id=1, source_target_pairs={{0,4},{2,6},{8,0},{10,2},{16,8},{18,10},{24,16},{26,18},{28,24},{3... | collective-permute-start | bytes 1179656 | tf_op jit(solution)/shard_map/ppermute | solution.py:348
  14.9 84.0 %collective-permute-start.18 = (bf16[384,1536]{1,0:T(8,128)(2,1)}, bf16[384,1536]{1,0:T(8,128)(2,1)}, u32[]{:S(2)}, u32[]{:S(2)}) collective-permute-start(bf16[384,1536]{1,0:T(8,128)(2,1)} %constant_dynamic-update-slice_fusion.20), channel_id=1, source_target_pairs={{0,1},{1,0},{2,3},{3,2},{4,5},{5,4},{6,7},{7,6},{8,9},{9,8},{10,11... | collective-permute-start | bytes 3538952 | tf_op jit(solution)/shard_map/ppermute | solution.py:360
  16.8 87.1 %collective-permute-start.19 = (bf16[384,1536]{1,0:T(8,128)(2,1)}, bf16[384,1536]{1,0:T(8,128)(2,1)}, u32[]{:S(2)}, u32[]{:S(2)}) collective-permute-start(bf16[384,1536]{1,0:T(8,128)(2,1)} %constant_dynamic-update-slice_fusion.20), channel_id=1, source_target_pairs={{0,2},{2,0},{4,6},{6,4},{8,10},{10,8},{12,14},{14,12},{16,18},{18,... | collective-permute-start | bytes 3538952 | tf_op jit(solution)/shard_map/ppermute | solution.py:352
  16.9 26.8 %collective-permute-start.8 = (bf16[2,48]{1,0:T(2,128)(2,1)S(1)}, bf16[2,48]{1,0:T(2,128)(2,1)S(1)}, u32[]{:S(2)}, u32[]{:S(2)}) collective-permute-start(bf16[2,48]{1,0:T(2,128)(2,1)S(1)} %pad_maximum_fusion.23), channel_id=1, source_target_pairs={{0,1},{1,0},{2,3},{3,2},{4,5},{5,4},{6,7},{7,6},{8,9},{9,8},{10,11... | collective-permute-start | bytes 584 | tf_op jit(solution)/shard_map/ppermute | solution.py:360
  63.8 24.1 %collective-permute-start.14 = (bf16[2,96,1536]{2,1,0:T(8,128)(2,1)S(1)}, bf16[2,96,1536]{2,1,0:T(8,128)(2,1)S(1)}, u32[]{:S(2)}, u32[]{:S(2)}) collective-permute-start(bf16[2,96,1536]{2,1,0:T(8,128)(2,1)S(1)} %maximum_select_fusion.2), channel_id=1, source_target_pairs={{0,2},{2,0},{4,6},{6,4},{8,10},{10,8},{12,14},{14,12},{16,18},{18,... | collective-permute-start | bytes 1769480 | tf_op jit(solution)/shard_map/ppermute | solution.py:352
  64.0 17.8 %collective-permute-start.4 = (bf16[128,1536]{1,0:T(8,128)(2,1)S(1)}, bf16[128,1536]{1,0:T(8,128)(2,1)S(1)}, u32[]{:S(2)}, u32[]{:S(2)}) collective-permute-start(bf16[128,1536]{1,0:T(8,128)(2,1)S(1)} %collective-permute-done.3.refs_7_), channel_id=1, source_target_pairs={{0,8},{2,10},{8,16},{10,18},{16,24},{18,26},{24,28},{26,30},{28,20... | collective-permute-start | bytes 1179656 | tf_op jit(solution)/shard_map/ppermute | solution.py:344
  65.8 20.2 %collective-permute-start.1 = (bf16[128,1536]{1,0:T(8,128)(2,1)S(1)}, bf16[128,1536]{1,0:T(8,128)(2,1)S(1)}, u32[]{:S(2)}, u32[]{:S(2)}) collective-permute-start(bf16[128,1536]{1,0:T(8,128)(2,1)S(1)} %collective-permute-done.refs_1_), channel_id=1, source_target_pairs={{0,4},{2,6},{8,0},{10,2},{16,8},{18,10},{24,16},{26,18},{28,24},{3... | collective-permute-start | bytes 1179656 | tf_op jit(solution)/shard_map/ppermute | solution.py:348
  81.8 14.9 %collective-permute-start.5 = (bf16[128,1536]{1,0:T(8,128)(2,1)S(1)}, bf16[128,1536]{1,0:T(8,128)(2,1)S(1)}, u32[]{:S(2)}, u32[]{:S(2)}) collective-permute-start(bf16[128,1536]{1,0:T(8,128)(2,1)S(1)} %collective-permute-done.4.refs_6_), channel_id=1, source_target_pairs={{0,8},{2,10},{8,16},{10,18},{16,24},{18,26},{24,28},{26,30},{28,20... | collective-permute-start | bytes 1179656 | tf_op jit(solution)/shard_map/ppermute | solution.py:344
  86.0 11.1 %collective-permute-start.2 = (bf16[128,1536]{1,0:T(8,128)(2,1)S(1)}, bf16[128,1536]{1,0:T(8,128)(2,1)S(1)}, u32[]{:S(2)}, u32[]{:S(2)}) collective-permute-start(bf16[128,1536]{1,0:T(8,128)(2,1)S(1)} %collective-permute-done.1.refs_2_), channel_id=1, source_target_pairs={{0,4},{2,6},{8,0},{10,2},{16,8},{18,10},{24,16},{26,18},{28,24},{3... | collective-permute-start | bytes 1179656 | tf_op jit(solution)/shard_map/ppermute | solution.py:348
  98.9 40.0 %collective-permute-start.20 = (bf16[384,1536]{1,0:T(8,128)(2,1)}, bf16[384,1536]{1,0:T(8,128)(2,1)}, u32[]{:S(2)}, u32[]{:S(2)}) collective-permute-start(bf16[384,1536]{1,0:T(8,128)(2,1)} %collective-permute-done.18), channel_id=1, source_target_pairs={{0,2},{2,0},{4,6},{6,4},{8,10},{10,8},{12,14},{14,12},{16,18},{18,... | collective-permute-start | bytes 3538952 | tf_op jit(solution)/shard_map/ppermute | solution.py:352
  105.8 11.7 %collective-permute-start.35 = (bf16[128,1536]{1,0:T(8,128)(2,1)S(1)}, bf16[128,1536]{1,0:T(8,128)(2,1)}, u32[]{:S(2)}, u32[]{:S(2)}) collective-permute-start(bf16[128,1536]{1,0:T(8,128)(2,1)S(1)} %bitcast.132), channel_id=1, source_target_pairs={{0,4},{2,6},{8,0},{10,2},{16,8},{18,10},{24,16},{26,18},{28,24},{3... | collective-permute-start | bytes 1179656 | tf_op jit(solution)/shard_map/ppermute | solution.py:348
  107.6 11.6 %collective-permute-start.38 = (bf16[128,1536]{1,0:T(8,128)(2,1)S(1)}, bf16[128,1536]{1,0:T(8,128)(2,1)}, u32[]{:S(2)}, u32[]{:S(2)}) collective-permute-start(bf16[128,1536]{1,0:T(8,128)(2,1)S(1)} %bitcast.133), channel_id=1, source_target_pairs={{0,8},{2,10},{8,16},{10,18},{16,24},{18,26},{24,28},{26,30},{28,20... | collective-permute-start | bytes 1179656 | tf_op jit(solution)/shard_map/ppermute | solution.py:344
  117.5 17.6 %collective-permute-start.36 = (bf16[128,1536]{1,0:T(8,128)(2,1)}, bf16[128,1536]{1,0:T(8,128)(2,1)}, u32[]{:S(2)}, u32[]{:S(2)}) collective-permute-start(bf16[128,1536]{1,0:T(8,128)(2,1)} %collective-permute-done.35), channel_id=1, source_target_pairs={{0,4},{2,6},{8,0},{10,2},{16,8},{18,10},{24,16},{26,18},{28,24},{3... | collective-permute-start | bytes 1179656 | tf_op jit(solution)/shard_map/ppermute | solution.py:348
  119.2 17.7 %collective-permute-start.39 = (bf16[128,1536]{1,0:T(8,128)(2,1)}, bf16[128,1536]{1,0:T(8,128)(2,1)}, u32[]{:S(2)}, u32[]{:S(2)}) collective-permute-start(bf16[128,1536]{1,0:T(8,128)(2,1)} %collective-permute-done.38), channel_id=1, source_target_pairs={{0,8},{2,10},{8,16},{10,18},{16,24},{18,26},{24,28},{26,30},{28,20... | collective-permute-start | bytes 1179656 | tf_op jit(solution)/shard_map/ppermute | solution.py:344
  131.0 33.9 %all-to-all-start = ((bf16[8,128,192]{1,2,0:T(8,128)(2,1)}), bf16[8,128,192]{1,2,0:T(8,128)(2,1)}, u32[]{:S(2)}, u32[]{:S(2)}) async-start(bf16[8,128,192]{1,2,0:T(8,128)(2,1)} %copy.26), calls=%async_computation | async-start | bytes 786432 | tf_op jit(solution)/shard_map/all_to_all | solution.py:740
  135.1 18.2 %collective-permute-start.37 = (bf16[128,1536]{1,0:T(8,128)(2,1)}, bf16[128,1536]{1,0:T(8,128)(2,1)S(1)}, u32[]{:S(2)}, u32[]{:S(2)}) collective-permute-start(bf16[128,1536]{1,0:T(8,128)(2,1)} %collective-permute-done.36), channel_id=1, source_target_pairs={{0,4},{2,6},{8,0},{10,2},{16,8},{18,10},{24,16},{26,18},{28,24},{3... | collective-permute-start | bytes 1179656 | tf_op jit(solution)/shard_map/ppermute | solution.py:348
  137.0 13.5 %collective-permute-start.40 = (bf16[128,1536]{1,0:T(8,128)(2,1)}, bf16[128,1536]{1,0:T(8,128)(2,1)S(1)}, u32[]{:S(2)}, u32[]{:S(2)}) collective-permute-start(bf16[128,1536]{1,0:T(8,128)(2,1)} %collective-permute-done.39), channel_id=1, source_target_pairs={{0,8},{2,10},{8,16},{10,18},{16,24},{18,26},{24,28},{26,30},{28,20... | collective-permute-start | bytes 1179656 | tf_op jit(solution)/shard_map/ppermute | solution.py:344
  169.4 9.5 %collective-permute-start.16 = (bf16[128,1536]{1,0:T(8,128)(2,1)S(1)}, bf16[128,1536]{1,0:T(8,128)(2,1)S(1)}, u32[]{:S(2)}, u32[]{:S(2)}) collective-permute-start(bf16[128,1536]{1,0:T(8,128)(2,1)S(1)} %get-tuple-element.48), channel_id=1, source_target_pairs={{0,4},{2,6},{8,0},{10,2},{16,8},{18,10},{24,16},{26,18},{28,24},{3... | collective-permute-start | bytes 1179656 | tf_op jit(solution)/shard_map/ppermute | solution.py:348
  194.0 9.9 %collective-permute-start.24 = (bf16[128,1536]{1,0:T(8,128)(2,1)S(1)}, bf16[128,1536]{1,0:T(8,128)(2,1)S(1)}, u32[]{:S(2)}, u32[]{:S(2)}) collective-permute-start(bf16[128,1536]{1,0:T(8,128)(2,1)S(1)} %collective-permute-done.23), channel_id=1, source_target_pairs={{0,8},{2,10},{8,16},{10,18},{16,24},{18,26},{24,28},{26,30},{28,20... | collective-permute-start | bytes 1179656 | tf_op jit(solution)/shard_map/ppermute | solution.py:344
  194.8 10.0 %collective-permute-start.22 = (bf16[128,1536]{1,0:T(8,128)(2,1)S(1)}, bf16[128,1536]{1,0:T(8,128)(2,1)S(1)}, u32[]{:S(2)}, u32[]{:S(2)}) collective-permute-start(bf16[128,1536]{1,0:T(8,128)(2,1)S(1)} %collective-permute-done.21), channel_id=1, source_target_pairs={{0,4},{2,6},{8,0},{10,2},{16,8},{18,10},{24,16},{26,18},{28,24},{3... | collective-permute-start | bytes 1179656 | tf_op jit(solution)/shard_map/ppermute | solution.py:348
  219.8 109.6 %collective-permute-start.68 = (f32[256,1536]{1,0:T(8,128)}, f32[256,1536]{1,0:T(8,128)}, u32[]{:S(2)}, u32[]{:S(2)}) collective-permute-start(f32[256,1536]{1,0:T(8,128)} %fusion.62), channel_id=1, source_target_pairs={{0,2},{2,0},{4,6},{6,4},{8,10},{10,8},{12,14},{14,12},{16,18},{18,... | collective-permute-start | bytes 4718600 | tf_op jit(solution)/shard_map/ppermute | solution.py:352
  219.9 14.4 %collective-permute-start.27 = (bf16[64,1536]{1,0:T(8,128)(2,1)S(1)}, bf16[64,1536]{1,0:T(8,128)(2,1)S(1)}, u32[]{:S(2)}, u32[]{:S(2)}) collective-permute-start(bf16[64,1536]{1,0:T(8,128)(2,1)S(1)} %get-tuple-element.111), channel_id=1, source_target_pairs={{0,8},{2,10},{8,16},{10,18},{16,24},{18,26},{24,28},{26,30},{28,20... | collective-permute-start | bytes 589832 | tf_op jit(solution)/shard_map/ppermute | solution.py:344
  220.8 13.5 %collective-permute-start.31 = (bf16[64,1536]{1,0:T(8,128)(2,1)S(1)}, bf16[64,1536]{1,0:T(8,128)(2,1)S(1)}, u32[]{:S(2)}, u32[]{:S(2)}) collective-permute-start(bf16[64,1536]{1,0:T(8,128)(2,1)S(1)} %get-tuple-element.112), channel_id=1, source_target_pairs={{0,4},{2,6},{8,0},{10,2},{16,8},{18,10},{24,16},{26,18},{28,24},{3... | collective-permute-start | bytes 589832 | tf_op jit(solution)/shard_map/ppermute | solution.py:348
  222.0 9.4 %collective-permute-start.43 = (bf16[64,1536]{1,0:T(8,128)(2,1)S(1)}, bf16[64,1536]{1,0:T(8,128)(2,1)S(1)}, u32[]{:S(2)}, u32[]{:S(2)}) collective-permute-start(bf16[64,1536]{1,0:T(8,128)(2,1)S(1)} %get-tuple-element.107), channel_id=1, source_target_pairs={{0,8},{2,10},{8,16},{10,18},{16,24},{18,26},{24,28},{26,30},{28,20... | collective-permute-start | bytes 589832 | tf_op jit(solution)/shard_map/ppermute | solution.py:344
  232.1 12.1 %collective-permute-start.48 = (bf16[128,1536]{1,0:T(8,128)(2,1)S(1)}, bf16[128,1536]{1,0:T(8,128)(2,1)S(1)}, u32[]{:S(2)}, u32[]{:S(2)}) collective-permute-start(bf16[128,1536]{1,0:T(8,128)(2,1)S(1)} %pad_maximum_fusion.14), channel_id=1, source_target_pairs={{0,4},{2,6},{8,0},{10,2},{16,8},{18,10},{24,16},{26,18},{28,24},{3... | collective-permute-start | bytes 1179656 | tf_op jit(solution)/shard_map/ppermute | solution.py:348
  233.4 12.1 %collective-permute-start.44 = (bf16[128,1536]{1,0:T(8,128)(2,1)S(1)}, bf16[128,1536]{1,0:T(8,128)(2,1)S(1)}, u32[]{:S(2)}, u32[]{:S(2)}) collective-permute-start(bf16[128,1536]{1,0:T(8,128)(2,1)S(1)} %pad_maximum_fusion.13), channel_id=1, source_target_pairs={{0,8},{2,10},{8,16},{10,18},{16,24},{18,26},{24,28},{26,30},{28,20... | collective-permute-start | bytes 1179656 | tf_op jit(solution)/shard_map/ppermute | solution.py:344
  234.4 18.2 %collective-permute-start.32 = (bf16[128,1536]{1,0:T(8,128)(2,1)S(1)}, bf16[128,1536]{1,0:T(8,128)(2,1)S(1)}, u32[]{:S(2)}, u32[]{:S(2)}) collective-permute-start(bf16[128,1536]{1,0:T(8,128)(2,1)S(1)} %pad_maximum_fusion.12), channel_id=1, source_target_pairs={{0,4},{2,6},{8,0},{10,2},{16,8},{18,10},{24,16},{26,18},{28,24},{3... | collective-permute-start | bytes 1179656 | tf_op jit(solution)/shard_map/ppermute | solution.py:348
  235.7 18.2 %collective-permute-start.28 = (bf16[128,1536]{1,0:T(8,128)(2,1)S(1)}, bf16[128,1536]{1,0:T(8,128)(2,1)S(1)}, u32[]{:S(2)}, u32[]{:S(2)}) collective-permute-start(bf16[128,1536]{1,0:T(8,128)(2,1)S(1)} %pad_maximum_fusion.11), channel_id=1, source_target_pairs={{0,8},{2,10},{8,16},{10,18},{16,24},{18,26},{24,28},{26,30},{28,20... | collective-permute-start | bytes 1179656 | tf_op jit(solution)/shard_map/ppermute | solution.py:344
  245.7 16.7 %collective-permute-start.45 = (bf16[128,1536]{1,0:T(8,128)(2,1)S(1)}, bf16[128,1536]{1,0:T(8,128)(2,1)S(1)}, u32[]{:S(2)}, u32[]{:S(2)}) collective-permute-start(bf16[128,1536]{1,0:T(8,128)(2,1)S(1)} %get-tuple-element.95), channel_id=1, source_target_pairs={{0,8},{2,10},{8,16},{10,18},{16,24},{18,26},{24,28},{26,30},{28,20... | collective-permute-start | bytes 1179656 | tf_op jit(solution)/shard_map/ppermute | solution.py:344
  246.6 15.7 %collective-permute-start.49 = (bf16[128,1536]{1,0:T(8,128)(2,1)S(1)}, bf16[128,1536]{1,0:T(8,128)(2,1)S(1)}, u32[]{:S(2)}, u32[]{:S(2)}) collective-permute-start(bf16[128,1536]{1,0:T(8,128)(2,1)S(1)} %get-tuple-element.96), channel_id=1, source_target_pairs={{0,4},{2,6},{8,0},{10,2},{16,8},{18,10},{24,16},{26,18},{28,24},{3... | collective-permute-start | bytes 1179656 | tf_op jit(solution)/shard_map/ppermute | solution.py:348
  254.1 16.7 %collective-permute-start.29 = (bf16[128,1536]{1,0:T(8,128)(2,1)S(1)}, bf16[128,1536]{1,0:T(8,128)(2,1)S(1)}, u32[]{:S(2)}, u32[]{:S(2)}) collective-permute-start(bf16[128,1536]{1,0:T(8,128)(2,1)S(1)} %get-tuple-element.105), channel_id=1, source_target_pairs={{0,8},{2,10},{8,16},{10,18},{16,24},{18,26},{24,28},{26,30},{28,20... | collective-permute-start | bytes 1179656 | tf_op jit(solution)/shard_map/ppermute | solution.py:344
  255.0 15.7 %collective-permute-start.33 = (bf16[128,1536]{1,0:T(8,128)(2,1)S(1)}, bf16[128,1536]{1,0:T(8,128)(2,1)S(1)}, u32[]{:S(2)}, u32[]{:S(2)}) collective-permute-start(bf16[128,1536]{1,0:T(8,128)(2,1)S(1)} %get-tuple-element.106), channel_id=1, source_target_pairs={{0,4},{2,6},{8,0},{10,2},{16,8},{18,10},{24,16},{26,18},{28,24},{3... | collective-permute-start | bytes 1179656 | tf_op jit(solution)/shard_map/ppermute | solution.py:348
  262.5 16.7 %collective-permute-start.46 = (bf16[128,1536]{1,0:T(8,128)(2,1)S(1)}, bf16[128,1536]{1,0:T(8,128)(2,1)S(1)}, u32[]{:S(2)}, u32[]{:S(2)}) collective-permute-start(bf16[128,1536]{1,0:T(8,128)(2,1)S(1)} %get-tuple-element.80), channel_id=1, source_target_pairs={{0,8},{2,10},{8,16},{10,18},{16,24},{18,26},{24,28},{26,30},{28,20... | collective-permute-start | bytes 1179656 | tf_op jit(solution)/shard_map/ppermute | solution.py:344
  263.5 15.7 %collective-permute-start.50 = (bf16[128,1536]{1,0:T(8,128)(2,1)S(1)}, bf16[128,1536]{1,0:T(8,128)(2,1)S(1)}, u32[]{:S(2)}, u32[]{:S(2)}) collective-permute-start(bf16[128,1536]{1,0:T(8,128)(2,1)S(1)} %get-tuple-element.81), channel_id=1, source_target_pairs={{0,4},{2,6},{8,0},{10,2},{16,8},{18,10},{24,16},{26,18},{28,24},{3... | collective-permute-start | bytes 1179656 | tf_op jit(solution)/shard_map/ppermute | solution.py:348
  271.0 14.7 %collective-permute-start.30 = (bf16[128,1536]{1,0:T(8,128)(2,1)S(1)}, bf16[128,1536]{1,0:T(8,128)(2,1)S(1)}, u32[]{:S(2)}, u32[]{:S(2)}) collective-permute-start(bf16[128,1536]{1,0:T(8,128)(2,1)S(1)} %get-tuple-element.88), channel_id=1, source_target_pairs={{0,8},{2,10},{8,16},{10,18},{16,24},{18,26},{24,28},{26,30},{28,20... | collective-permute-start | bytes 1179656 | tf_op jit(solution)/shard_map/ppermute | solution.py:344
  271.9 13.8 %collective-permute-start.34 = (bf16[128,1536]{1,0:T(8,128)(2,1)S(1)}, bf16[128,1536]{1,0:T(8,128)(2,1)S(1)}, u32[]{:S(2)}, u32[]{:S(2)}) collective-permute-start(bf16[128,1536]{1,0:T(8,128)(2,1)S(1)} %get-tuple-element.89), channel_id=1, source_target_pairs={{0,4},{2,6},{8,0},{10,2},{16,8},{18,10},{24,16},{26,18},{28,24},{3... | collective-permute-start | bytes 1179656 | tf_op jit(solution)/shard_map/ppermute | solution.py:348
  291.2 14.4 %all-to-all-start.1 = ((bf16[8,128,192]{1,2,0:T(8,128)(2,1)}), bf16[8,128,192]{1,2,0:T(8,128)(2,1)}, u32[]{:S(2)}, u32[]{:S(2)}) async-start(bf16[8,128,192]{1,2,0:T(8,128)(2,1)} %bitcast.135), calls=%async_computation.1 | async-start | bytes 786432 | tf_op jit(solution)/shard_map/all_to_all | solution.py:832
  295.4 161.6 %reduce-scatter.2.cloned.1.call-start = ((), (), s32[]{:S(2)}) async-start(), calls=%async_computation.4 | async-start | bytes 4866048 | tf_op jit(solution)/shard_map/reduce_scatter | solution.py:840
  320.7 12.3 %collective-permute-start.51 = (f32[1024,256]{1,0:T(8,128)}, f32[1024,256]{1,0:T(8,128)}, u32[]{:S(2)}, u32[]{:S(2)}) collective-permute-start(f32[1024,256]{1,0:T(8,128)} %get-tuple-element.29), channel_id=1, source_target_pairs={{0,2},{2,0},{4,6},{6,4},{8,10},{10,8},{12,14},{14,12},{16,18},{18,... | collective-permute-start | bytes 3145736 | tf_op jit(solution)/shard_map/ppermute | solution.py:352
  324.3 37.3 %collective-permute-start.67 = (f32[512,1536]{1,0:T(8,128)}, f32[512,1536]{1,0:T(8,128)}, u32[]{:S(2)}, u32[]{:S(2)}) collective-permute-start(f32[512,1536]{1,0:T(8,128)} %fusion.14), channel_id=1, source_target_pairs={{0,2},{2,0},{4,6},{6,4},{8,10},{10,8},{12,14},{14,12},{16,18},{18,... | collective-permute-start | bytes 9437192 | tf_op jit(solution)/shard_map/ppermute | solution.py:352
  348.4 9.9 %collective-permute-start.57 = (bf16[128,1536]{1,0:T(8,128)(2,1)S(1)}, bf16[128,1536]{1,0:T(8,128)(2,1)S(1)}, u32[]{:S(2)}, u32[]{:S(2)}) collective-permute-start(bf16[128,1536]{1,0:T(8,128)(2,1)S(1)} %pad_maximum_fusion.16), channel_id=1, source_target_pairs={{0,4},{2,6},{8,0},{10,2},{16,8},{18,10},{24,16},{26,18},{28,24},{3... | collective-permute-start | bytes 1179656 | tf_op jit(solution)/shard_map/ppermute | solution.py:348
  349.7 9.7 %collective-permute-start.53 = (bf16[128,1536]{1,0:T(8,128)(2,1)S(1)}, bf16[128,1536]{1,0:T(8,128)(2,1)S(1)}, u32[]{:S(2)}, u32[]{:S(2)}) collective-permute-start(bf16[128,1536]{1,0:T(8,128)(2,1)S(1)} %pad_maximum_fusion.15), channel_id=1, source_target_pairs={{0,8},{2,10},{8,16},{10,18},{16,24},{18,26},{24,28},{26,30},{28,20... | collective-permute-start | bytes 1179656 | tf_op jit(solution)/shard_map/ppermute | solution.py:344
  350.8 33.6 %collective-permute-start.65 = (f32[2,96,1536]{2,1,0:T(8,128)S(1)}, f32[2,96,1536]{2,1,0:T(8,128)S(1)}, u32[]{:S(2)}, u32[]{:S(2)}) collective-permute-start(f32[2,96,1536]{2,1,0:T(8,128)S(1)} %fusion.17), channel_id=1, source_target_pairs={{0,2},{2,0},{4,6},{6,4},{8,10},{10,8},{12,14},{14,12},{16,18},{18,... | collective-permute-start | bytes 3538952 | tf_op jit(solution)/shard_map/ppermute | solution.py:352
  380.9 74.6 %collective-permute-start.69 = (f32[384,1536]{1,0:T(8,128)S(1)}, f32[384,1536]{1,0:T(8,128)S(1)}, u32[]{:S(2)}, u32[]{:S(2)}) collective-permute-start(f32[384,1536]{1,0:T(8,128)S(1)} %pad_maximum_fusion), channel_id=1, source_target_pairs={{0,1},{1,0},{2,3},{3,2},{4,5},{5,4},{6,7},{7,6},{8,9},{9,8},{10,11... | collective-permute-start | bytes 7077896 | tf_op jit(solution)/shard_map/ppermute | solution.py:360
  388.7 65.2 %collective-permute-start.66 = (f32[96,1536]{1,0:T(8,128)S(1)}, f32[96,1536]{1,0:T(8,128)S(1)}, u32[]{:S(2)}, u32[]{:S(2)}) collective-permute-start(f32[96,1536]{1,0:T(8,128)S(1)} %select_bitcast_fusion), channel_id=1, source_target_pairs={{0,1},{1,0},{2,3},{3,2},{4,5},{5,4},{6,7},{7,6},{8,9},{9,8},{10,11... | collective-permute-start | bytes 1769480 | tf_op jit(solution)/shard_map/ppermute | solution.py:360
  392.4 60.8 %collective-permute-start.64 = (f32[2,48]{1,0:T(2,128)S(1)}, f32[2,48]{1,0:T(2,128)S(1)}, u32[]{:S(2)}, u32[]{:S(2)}) collective-permute-start(f32[2,48]{1,0:T(2,128)S(1)} %broadcast_select_fusion.8), channel_id=1, source_target_pairs={{0,1},{1,0},{2,3},{3,2},{4,5},{5,4},{6,7},{7,6},{8,9},{9,8},{10,11... | collective-permute-start | bytes 1160 | tf_op jit(solution)/shard_map/ppermute | solution.py:360
  (81 other events, 681.1 us)
Sparse Core Ops, SparseCore 0:
  17.2 69.1 all-gather.1
  329.5 115.4 reduce-scatter.1

commit v2 on v0

--- a/solution.py
+++ b/solution.py
@@ -1,6 +1,10 @@
+import functools
+
 import jax
 import jax.numpy as jnp
 from jax import lax
+from jax.experimental import pallas as pl
+from jax.experimental.pallas import tpu as pltpu
 from jax.sharding import PartitionSpec as P
 
 HEADS = 16
@@ -321,6 +325,1112 @@
     )
 
 
+CHIPS = 8
+TOK = 128
+PAIR = 2 * HD
+LANES = 128
+VMEM_LIMIT = 32 << 20
+LOG2E = 1.4426950408889634
+RING = (0, 2, 4, 6, 7, 5, 3, 1)
+SAME_CORE = [[2 * c + core for c in range(CHIPS)] for core in range(2)]
+
+
+def ring_route(step):
+    return [
+        (RING[k] * 2 + core, RING[(k + step) % CHIPS] * 2 + core)
+        for k in range(CHIPS)
+        for core in range(2)
+    ]
+
+
+def ring_up(value):
+    return lax.ppermute(value, "blk", ring_route(1))
+
+
+def ring_down(value):
+    return lax.ppermute(value, "blk", ring_route(-1))
+
+
+def flipped(value, bit):
+    return lax.ppermute(value, "blk", [(i, i ^ bit) for i in range(2 * CHIPS)])
+
+
+def core_swap(value):
+    return flipped(value, 1)
+
+
+def x_swap(value):
+    return lax.ppermute(value, "fsdp", [(0, 1), (1, 0)])
+
+
+def tie(values, deps):
+    deps = [d for d in deps if d is not None]
+    if not deps:
+        return tuple(values)
+    return lax.optimization_barrier((tuple(values), tuple(deps)))[0]
+
+
+def after(value, *deps):
+    return tie((value,), deps)[0]
+
+
+class Gather:
+    def __init__(self, block):
+        self.found = [None] * CHIPS
+        self.found[0] = self.up = self.down = block
+
+    def step(self, number, *deps):
+        self.up, self.down = tie((self.up, self.down), deps)
+        if number < CHIPS // 2:
+            self.up = ring_up(self.up)
+            self.down = ring_down(self.down)
+            self.found[CHIPS - number] = self.up
+            self.found[number] = self.down
+        else:
+            half = self.up.shape[0] // 2
+            self.up = ring_up(self.up[:half])
+            self.down = ring_down(self.down[half:])
+            self.found[number] = (self.up, self.down)
+        return self.up, self.down
+
+
+class Scatter:
+    def __init__(self, make):
+        self.make = make
+        self.up = self.down = None
+
+    def step(self, number, *deps):
+        up, down = tie(self.make(number, self.up, self.down), deps)
+        self.up = ring_up(up)
+        self.down = ring_down(down)
+        return self.up, self.down
+
+
+def dot_nt(left, right):
+    return lax.dot_general(
+        left, right, (((1,), (1,)), ((), ())), preferred_element_type=jnp.float32
+    )
+
+
+def dot_nn(left, right):
+    return lax.dot_general(
+        left, right, (((1,), (0,)), ((), ())), preferred_element_type=jnp.float32
+    )
+
+
+GROUPS = ((0, 1, 7), (2, 6), (3, 5), (4,))
+ARRIVAL = tuple(j for group in GROUPS for j in group)
+
+
+def whole(shape):
+    return pl.BlockSpec(shape, lambda i: (0,) * len(shape), pipeline_mode=pl.Buffered(1))
+
+
+def window(rows, nth, width):
+    return pl.BlockSpec((rows, width), lambda i: (nth, 0), pipeline_mode=pl.Buffered(1))
+
+
+def call(kernel, name, outs, ins, scratch=(), far=(), far_out=(), windows={}):
+    shapes = []
+    for n, (shape, dtype) in enumerate(outs):
+        make = pltpu.HBM if n in far_out else jax.ShapeDtypeStruct
+        shapes.append(make(shape, dtype))
+    ins = list(ins)
+    for n in far:
+        ins[n] = pltpu.with_memory_space_constraint(ins[n], pltpu.HBM)
+    return pl.pallas_call(
+        kernel,
+        grid=(1,),
+        out_shape=tuple(shapes),
+        in_specs=[
+            window(*windows[n], value.shape[1]) if n in windows else whole(value.shape)
+            for n, value in enumerate(ins)
+        ],
+        out_specs=tuple(whole(shape) for shape, _ in outs),
+        scratch_shapes=scratch,
+        compiler_params=pltpu.CompilerParams(vmem_limit_bytes=VMEM_LIMIT),
+        cost_estimate=pl.CostEstimate(flops=0, bytes_accessed=0, transcendentals=0),
+        name=name,
+    )(*ins)
+
+
+def dot_tn(left, right):
+    return lax.dot_general(
+        left, right, (((0,), (0,)), ((), ())), preferred_element_type=jnp.float32
+    )
+
+
+def own_place():
+    index = lax.axis_index("blk")
+    chip = lax.div(index, 2)
+    half = lax.div(chip, 2)
+    spot = jnp.where(lax.rem(chip, 2) == 0, half, CHIPS - 1 - half)
+    return lax.rem(index, 2), lax.axis_index("fsdp"), chip, spot
+
+
+def arriving_chip(nth, spot):
+    at = lax.rem(spot + ARRIVAL[nth], CHIPS)
+    return jnp.where(at < CHIPS // 2, 2 * at, 2 * CHIPS - 1 - 2 * at)
+
+
+def arrival_of(chip, spot):
+    away = lax.rem(RING.index(chip) - spot + CHIPS, CHIPS)
+    late = jnp.where(away <= CHIPS // 2, 2 * away - 1, 2 * (CHIPS - away))
+    return jnp.where(away == 0, 0, late)
+
+
+def heads_kernel(own, near, far, across, out):
+    nq = HD // 2
+    nk = HD // 4
+    half = LANES // 2
+    own_core, own_side, _, _ = own_place()
+    out[...] = jnp.zeros_like(out)
+    for core in range(2):
+        for side in range(2):
+
+            @pl.when((own_core == core) & (own_side == side))
+            def _():
+                for piece, c, f in (
+                    (own, core, side),
+                    (near, core, 1 - side),
+                    (far, 1 - core, side),
+                    (across, 1 - core, 1 - side),
+                ):
+                    at = c * LANES + f * half
+                    out[at : at + nq] = piece[:nq]
+                    at = 2 * LANES + c * half + f * nk
+                    out[at : at + nk] = piece[nq : nq + nk]
+                    at = 3 * LANES + (2 * c + f) * nk
+                    out[at : at + nk] = piece[nq + nk :]
+
+
+def stack_kernel(*refs):
+    out = refs[-1]
+    at = 0
+    for piece in refs[:-1]:
+        out[at : at + piece.shape[0]] = piece[...]
+        at += piece.shape[0]
+
+
+def out_kernel(*refs):
+    own, near, out = refs[:4], refs[4:8], refs[8]
+    side = own_place()[1]
+    rows = own[0].shape[0] // 2
+    for n, j in enumerate(ARRIVAL):
+        away = min(j, CHIPS - j)
+        which = 3 if away in (0, CHIPS // 2) else away - 1
+        here = slice(0, rows) if j in (0, 1, 2, 3) else slice(rows, 2 * rows)
+        for source, f in ((own, side), (near, 1 - side)):
+            at = pl.multiple_of((2 * n + f) * rows, rows)
+            out[pl.ds(at, rows), :] = source[which][here, :]
+
+
+def hidden_kernel(*refs):
+    gate_up, down = refs[-2:]
+    count = refs[0].shape[0]
+    for n in range(4):
+        gate, up, out = refs[3 * n : 3 * n + 3]
+        start = (n // 2) * 4 * count + (n % 2) * count
+        gate_up[start : start + count] = gate[...]
+        gate_up[start + 2 * count : start + 3 * count] = up[...]
+        down[n * count : (n + 1) * count] = out[...]
+
+
+def project_kernel(*refs):
+    blocks = refs[: CHIPS + 1]
+    gain, weight, cosine, sine, normed_out, query_out, kv_out = refs[CHIPS + 1 :]
+    for j in range(CHIPS):
+        if j < CHIPS - 1:
+            values = blocks[j][-TOK:].astype(jnp.float32)
+        else:
+            late = blocks[CHIPS][...].astype(jnp.float32)
+            values = blocks[j][-(TOK - late.shape[0]) :].astype(jnp.float32)
+            values = jnp.concatenate([values, late], axis=0)
+        scale = lax.rsqrt(jnp.mean(values * values, axis=-1, keepdims=True) + EPS)
+        normed_out[j * TOK : (j + 1) * TOK, :] = (values * scale * gain[...]).astype(jnp.bfloat16)
+    pre = dot_nt(normed_out[...], weight[...])
+    for head in range(3):
+        part = pre[:, head * LANES : (head + 1) * LANES]
+        turned = part * cosine[...] + pltpu.roll(part, LANES // 2, 1) * sine[...]
+        if head < 2:
+            query_out[:, head * LANES : (head + 1) * LANES] = turned.astype(jnp.bfloat16)
+        else:
+            kv_out[:, :LANES] = turned.astype(jnp.bfloat16)
+    kv_out[:, LANES:] = pre[:, 3 * LANES :].astype(jnp.bfloat16)
+
+
+def project(blocks, *arrays):
+    rows = CHIPS * TOK
+    width = blocks[0].shape[1]
+    low = jnp.bfloat16
+    assert len(blocks) == CHIPS + 1
+    return call(
+        project_kernel,
+        "project",
+        (((rows, width), low), ((rows, 2 * LANES), low), ((rows, 2 * LANES), low)),
+        (*blocks, *arrays),
+        far=range(CHIPS + 1),
+        far_out=(0,),
+    )
+
+
+def key_index(core, count):
+    row = lax.broadcasted_iota(jnp.int32, (count, 1), 0)
+    return (row // TOK) * (2 * TOK) + core * TOK + row % TOK
+
+
+def query_index(core, chip):
+    lane = lax.broadcasted_iota(jnp.int32, (1, 2 * TOK), 1)
+    return lane % TOK + (2 * chip + core) * TOK
+
+
+def sequence_starts(segments):
+    numbers = segments[...]
+    starts = []
+    for number in range(1, 4):
+        below = (numbers < number).astype(jnp.float32)
+        total = jnp.sum(jnp.sum(below, axis=1, keepdims=True), axis=0, keepdims=True)
+        starts.append(total.astype(jnp.int32))
+    return starts
+
+
+def first_index(starts, at):
+    first = jnp.zeros_like(at)
+    for start in starts:
+        first = jnp.where(at >= start, start, first)
+    return first
+
+
+def both_heads(ref, rows):
+    return jnp.concatenate([ref[rows, :LANES], ref[rows, LANES:]], axis=0)
+
+
+def attend_kernel(
+    segments, query_in, own_in, peer_in, attended, mixed, lse, query, own, peer
+):
+    core, _, _, spot = own_place()
+    starts = sequence_starts(segments)
+    factor = HD ** (-0.5) * LOG2E
+    for source, target in ((query_in, query), (own_in, own), (peer_in, peer)):
+        for chip in range(CHIPS):
+            rows = pl.ds(pl.multiple_of(arrival_of(chip, spot) * TOK, TOK), TOK)
+            target[chip * TOK : (chip + 1) * TOK, :] = source[rows, :]
+    sides = ((own, core), (peer, 1 - core))
+    values_t = [jnp.transpose(kv[:, LANES:]) for kv, _ in sides]
+    for chip in range(CHIPS):
+        count = (chip + 1) * TOK
+        rows = slice(chip * TOK, count)
+        queries = both_heads(query, rows)
+        at = query_index(core, chip)
+        first = first_index(starts, at)
+        scores = []
+        for kv, side in sides:
+            raw = dot_nt(kv[:count, :LANES], queries) * factor
+            keys_at = key_index(side, count)
+            scores.append(jnp.where((keys_at <= at) & (keys_at >= first), raw, NEG))
+        top = jnp.maximum(
+            jnp.max(scores[0], axis=0, keepdims=True), jnp.max(scores[1], axis=0, keepdims=True)
+        )
+        weights = [jnp.exp2(part - top) for part in scores]
+        total = jnp.sum(weights[0], axis=0, keepdims=True) + jnp.sum(
+            weights[1], axis=0, keepdims=True
+        )
+        mix = dot_nn(values_t[0][:, :count], weights[0].astype(jnp.bfloat16)) + dot_nn(
+            values_t[1][:, :count], weights[1].astype(jnp.bfloat16)
+        )
+        mix = mix / total
+        mixed[chip] = mix
+        lse[chip] = top + jnp.log2(total)
+        attended[chip, :HD] = mix[:HD, :TOK].astype(jnp.bfloat16)
+        attended[chip, HD:] = mix[:HD, TOK:].astype(jnp.bfloat16)
+
+
+def attend_heads(segments, query, own, peer):
+    tokens = CHIPS * TOK
+    low = jnp.bfloat16
+    return call(
+        attend_kernel,
+        "attend",
+        (
+            ((CHIPS, PAIR, TOK), low),
+            ((CHIPS, LANES, 2 * TOK), jnp.float32),
+            ((CHIPS, 1, 2 * TOK), jnp.float32),
+            ((tokens, 2 * LANES), low),
+            ((tokens, 2 * LANES), low),
+            ((tokens, 2 * LANES), low),
+        ),
+        (segments, query, own, peer),
+        far_out=(1, 2, 3, 4, 5),
+    )
+
+
+def attend_back_kernel(
+    segments, query, own, peer, grad_out, mixed, lse, cosine, sine,
+    grad_query, own_out, peer_out, grad_own, grad_peer,
+):
+    core, _, _, spot = own_place()
+    starts = sequence_starts(segments)
+    scale = HD ** (-0.5)
+    factor = scale * LOG2E
+    sides = ((own, core, grad_own), (peer, 1 - core, grad_peer))
+    keys_t = [jnp.transpose(kv[:, :LANES]) for kv, _, _ in sides]
+    grad_own[...] = jnp.zeros_like(grad_own)
+    grad_peer[...] = jnp.zeros_like(grad_peer)
+    pad = jnp.zeros((LANES - HD, 2 * TOK), jnp.bfloat16)
+    for chip in range(CHIPS):
+        count = (chip + 1) * TOK
+        rows = slice(chip * TOK, count)
+        kept = pl.ds(pl.multiple_of(arrival_of(chip, spot) * TOK, TOK), TOK)
+        queries = both_heads(query, rows)
+        grads = jnp.concatenate(
+            [
+                jnp.concatenate([grad_out[chip, :HD], grad_out[chip, HD:]], axis=1),
+                pad,
+            ],
+            axis=0,
+        )
+        delta = jnp.sum(grads.astype(jnp.float32) * mixed[chip], axis=0, keepdims=True)
+        at = query_index(core, chip)
+        first = first_index(starts, at)
+        level = lse[chip]
+        grad_q = jnp.zeros((LANES, 2 * TOK), jnp.float32)
+        for (kv, side, grad_kv), key_t in zip(sides, keys_t):
+            raw = dot_nt(kv[:count, :LANES], queries) * factor
+            keys_at = key_index(side, count)
+            allowed = (keys_at <= at) & (keys_at >= first)
+            probs = jnp.exp2(jnp.where(allowed, raw - level, NEG))
+            grad_probs = dot_nn(kv[:count, LANES:], grads)
+            grad_scores = (probs * (grad_probs - delta)).astype(jnp.bfloat16)
+            grad_kv[:count, LANES:] += dot_nt(probs.astype(jnp.bfloat16), grads)
+            grad_kv[:count, :LANES] += dot_nn(grad_scores, queries)
+            grad_q += dot_nn(key_t[:, :count], grad_scores)
+        grad_q = jnp.transpose(grad_q) * scale
+        cos = cosine[kept, :]
+        sin = sine[kept, :]
+        for head in range(2):
+            part = grad_q[head * TOK : (head + 1) * TOK]
+            turned = part * cos - pltpu.roll(part, LANES // 2, 1) * sin
+            grad_query[kept, head * LANES : (head + 1) * LANES] = turned.astype(jnp.bfloat16)
+    for chip in range(CHIPS):
+        rows = slice(chip * TOK, (chip + 1) * TOK)
+        kept = pl.ds(pl.multiple_of(arrival_of(chip, spot) * TOK, TOK), TOK)
+        for grad_kv, out in ((grad_own, own_out), (grad_peer, peer_out)):
+            out[kept, :LANES] = grad_kv[rows, :LANES] * scale
+            out[kept, LANES:] = grad_kv[rows, LANES:]
+
+
+def attend_back(segments, *arrays):
+    tokens = CHIPS * TOK
+    full = jnp.float32
+    return call(
+        attend_back_kernel,
+        "attend_back",
+        (
+            ((tokens, 2 * LANES), jnp.bfloat16),
+            ((tokens, 2 * LANES), full),
+            ((tokens, 2 * LANES), full),
+        ),
+        (segments, *arrays),
+        scratch=[pltpu.VMEM((tokens, 2 * LANES), full)] * 2,
+        far=(1, 2, 3, 5, 6, 7, 8),
+    )
+
+
+def join_kernel(heads, *refs):
+    weights = refs[:2]
+    block, gain, middle_out, normed_out, attended_out, weight_out, held = refs[2:]
+    core, _, _, spot = own_place()
+    size = weights[0].shape[0] // CHIPS
+    for n in range(CHIPS):
+        for piece, side in zip(weights, (core, 1 - core)):
+            at = pl.multiple_of((2 * arriving_chip(n, spot) + side) * size, size)
+            weight_out[pl.ds(at, size), :] = piece[n * size : (n + 1) * size, :]
+    for chip in range(CHIPS):
+        held[chip * PAIR : (chip + 1) * PAIR, :] = heads[chip]
+    attended_out[...] = jnp.transpose(held[...])
+    middle = block[...].astype(jnp.float32) + dot_nt(attended_out[...], weight_out[...])
+    middle_out[...] = middle
+    scale = lax.rsqrt(jnp.mean(middle * middle, axis=-1, keepdims=True) + EPS)
+    normed_out[...] = (middle * scale * gain[...]).astype(jnp.bfloat16)
+
+
+def ffn_kernel(number, *refs):
+    blocks = refs[:number]
+    outers = refs[number : 2 * number]
+    gate_up, down_rows = refs[2 * number : 2 * number + 2]
+    rows, outer_rows, hidden, grad_gu = refs[2 * number + 2 : 2 * number + 6]
+    wide = hidden.shape[1] // 2
+    size = rows.shape[0] // number
+    for n in range(number):
+        rows[n * size : (n + 1) * size, :] = blocks[n][...]
+        outer_rows[n * size : (n + 1) * size, :] = outers[n][...]
+    grads = dot_nt(outer_rows[...], down_rows[...])
+    pre = dot_nt(rows[...], gate_up[...])
+    for part in range(2):
+        at = part * 2 * wide
+        gate = pre[:, at : at + wide]
+        up = pre[:, at + wide : at + 2 * wide]
+        back = grads[:, part * wide : (part + 1) * wide]
+        sigma = 1.0 / (1.0 + jnp.exp(-gate))
+        active = gate * sigma
+        hidden[:, part * wide : (part + 1) * wide] = (active * up).astype(jnp.bfloat16)
+        slope = back * up * sigma * (1.0 + gate * (1.0 - sigma))
+        grad_gu[:, at : at + wide] = slope.astype(jnp.bfloat16)
+        grad_gu[:, at + wide : at + 2 * wide] = (back * active).astype(jnp.bfloat16)
+    outs = refs[2 * number + 6 :]
+    back = dot_nn(grad_gu[...], gate_up[...])
+    if len(outs) == 1:
+        outs[0][...] = back
+    else:
+        outs[0][...] = back[: TOK // 2].astype(jnp.bfloat16)
+        outs[1][...] = back[TOK // 2 :].astype(jnp.bfloat16)
+
+
+def ffn(blocks, outers, gate_up, down):
+    number = len(blocks)
+    rows = number * blocks[0].shape[0]
+    width = blocks[0].shape[1]
+    units = down.shape[0]
+    low = jnp.bfloat16
+    if rows > TOK:
+        terms = [((rows, width), jnp.float32)]
+    else:
+        terms = [((TOK // 2, width), low)] * 2
+    return call(
+        functools.partial(ffn_kernel, number),
+        "ffn",
+        [((rows, width), low)] * 2 + [((rows, units), low), ((rows, 2 * units), low)] + terms,
+        (*blocks, *outers, gate_up, down),
+    )
+
+
+def add_terms(up_term, down_term, up, down, up_out, down_out):
+    size = up.shape[0]
+    rest = up_out.shape[0] - size
+    low = jnp.bfloat16
+    full = jnp.float32
+    up_out[:size] = (up_term[:size] + up.astype(full)).astype(low)
+    down_out[rest:] = (down_term[rest:] + down.astype(full)).astype(low)
+    if rest:
+        up_out[size:] = up_term[size:].astype(low)
+        down_out[:rest] = down_term[:rest].astype(low)
+
+
+def add_kernel(up_term, down_term, up, down, up_out, down_out):
+    add_terms(up_term, down_term, up[...], down[...], up_out, down_out)
+
+
+def leaving(width, rows=TOK):
+    return [((rows, width), jnp.bfloat16)] * 2
+
+
+STEP_ROWS = {1: 7 * TOK, 2: 5 * TOK, 3: 3 * TOK, 4: TOK}
+
+
+def branch_kernel(hidden, down_rows, *outs):
+    found = dot_nn(hidden[...], down_rows[...])
+    at = 0
+    for out in outs[:-2]:
+        out[...] = found[at : at + out.shape[0]]
+        at += out.shape[0]
+    outs[-2][...] = found[at : at + TOK // 2].astype(jnp.bfloat16)
+    outs[-1][...] = found[at + TOK // 2 :].astype(jnp.bfloat16)
+
+
+def result_kernel(terms, up, down, middle, out):
+    full = jnp.float32
+    branch = terms[...] + (up[...].astype(full) + down[...].astype(full))
+    out[...] = (middle[...] + branch).astype(jnp.bfloat16)
+
+
+def grads_kernel(number, *refs):
+    rows_in, outer_in, hidden_in, grads_in = (refs[n * number : (n + 1) * number] for n in range(4))
+    keep_gu, keep_down, send_gu, send_down, hidden, rows, grads = refs[4 * number :]
+    at = 0
+    for block, hid, grad in zip(rows_in, hidden_in, grads_in):
+        here = slice(at, at + block.shape[0])
+        rows[here, :] = block[...]
+        hidden[here, :] = hid[...]
+        grads[here, :] = grad[...]
+        at += block.shape[0]
+    half = keep_gu.shape[0]
+    send_gu[...] = dot_tn(grads[:, half:], rows[...])
+    keep_gu[...] = dot_tn(grads[:, :half], rows[...])
+    at = 0
+    for block in outer_in:
+        rows[at : at + block.shape[0], :] = block[...]
+        at += block.shape[0]
+    half = keep_down.shape[0]
+    send_down[...] = dot_tn(hidden[:, half:], rows[...])
+    keep_down[...] = dot_tn(hidden[:, :half], rows[...])
+
+
+def owners_kernel(keep_gu, keep_down, other_gu, other_down, *outs):
+    count = outs[0].shape[0]
+    for n, (value, other, at) in enumerate(
+        ((keep_gu, other_gu, 0), (keep_gu, other_gu, 2 * count), (keep_down, other_down, 0))
+    ):
+        near = at + count
+        outs[n][...] = value[at:near] + other[at:near]
+        given = value[near : near + count] + other[near : near + count]
+        outs[3 + n][...] = given.astype(jnp.bfloat16)
+
+
+def turn_kernel(*refs):
+    own, up, down, middle_ref, outer, gain, weight, middle_out, branch_out, heads, gain_out = refs
+    grad = own[...] + (up[...].astype(jnp.float32) + down[...].astype(jnp.float32))
+    middle = middle_ref[...]
+    scale = lax.rsqrt(jnp.mean(middle * middle, axis=-1, keepdims=True) + EPS)
+    weighted = grad * gain[...]
+    inner = jnp.mean(weighted * middle, axis=-1, keepdims=True)
+    gain_out[...] = jnp.sum(grad * middle * scale, axis=0, keepdims=True)
+    total = outer[...].astype(jnp.float32) + (scale * weighted - middle * (scale**3 * inner))
+    middle_out[...] = total
+    branch = total.astype(jnp.bfloat16)
+    branch_out[...] = branch
+    back = jnp.transpose(dot_nn(branch, weight[...]).astype(jnp.bfloat16))
+    for chip in range(CHIPS):
+        heads[chip] = back[chip * PAIR : (chip + 1) * PAIR]
+
+
+def outer_kernel(branch, attended, keep, give, held):
+    held[...] = dot_tn(branch[...], attended[...])
+    core = own_place()[0]
+    size = keep.shape[1]
+    for chip in range(CHIPS):
+        at = pl.multiple_of((2 * chip + core) * size, size)
+        keep[chip] = held[pl.ds(at, size), :].astype(jnp.bfloat16)
+        at = pl.multiple_of((2 * chip + 1 - core) * size, size)
+        give[chip] = held[pl.ds(at, size), :].astype(jnp.bfloat16)
+
+
+def settle_kernel(keep, other, total):
+    spot = own_place()[3]
+    rows = keep.shape[1]
+    for n in range(CHIPS):
+        chip = arriving_chip(n, spot)
+        found = keep[chip].astype(jnp.float32) + other[chip].astype(jnp.float32)
+        total[n * rows : (n + 1) * rows] = found.astype(jnp.bfloat16)
+
+
+def first_two(left, right, second, up_out, down_out):
+    begin = STEP_ROWS[1]
+    terms = dot_nn(left[begin : begin + TOK], right[...]).astype(jnp.bfloat16)
+    rows = second.shape[0] // CHIPS
+    begin = (CHIPS - 1) * rows
+    half = TOK // 2
+    up_out[:half] = terms[:half]
+    down_out[:half] = terms[half:]
+    up_out[half:] = second[begin : begin + rows // 2]
+    down_out[half:] = second[begin + rows // 2 : begin + rows]
+
+
+def both_kernel(
+    up_left, down_left, right, up_second, down_second, up, down, up_out, down_out
+):
+    rows = up_second.shape[0]
+    full = jnp.float32
+    cut = up.shape[0] * TOK // (TOK + rows)
+    terms = dot_nn(jnp.concatenate([up_left[...], down_left[...]], axis=0), right[...])
+    add_terms(
+        terms[:TOK], terms[TOK:], up[:cut], down[:cut], up_out.at[:TOK], down_out.at[:TOK]
+    )
+    add_terms(
+        up_second[...].astype(full),
+        down_second[...].astype(full),
+        up[cut:],
+        down[cut:],
+        up_out.at[TOK:],
+        down_out.at[TOK:],
+    )
+
+
+def spread_kernel(query, own, other, cosine, sine, weight, second, joined, up_out, down_out):
+    joined[:, : 2 * LANES] = query[...]
+    total = own[...] + other[...]
+    part = total[:, :LANES]
+    turned = part * cosine[...] - pltpu.roll(part, LANES // 2, 1) * sine[...]
+    joined[:, 2 * LANES : 3 * LANES] = turned.astype(jnp.bfloat16)
+    joined[:, 3 * LANES :] = total[:, LANES:].astype(jnp.bfloat16)
+    first_two(joined, weight, second, up_out, down_out)
+
+
+def heads_grad_kernel(*refs):
+    own_core, own_side, _, _ = own_place()
+    joined, weight, gain, second, normed, mine, send, gains, grad = refs
+    grad[...] = dot_tn(joined[...], normed[...])
+    first = jnp.sum(grad[...] * weight[...].astype(jnp.float32), axis=0, keepdims=True) / gain[...]
+    nq = HD // 2
+    nk = HD // 4
+    half = LANES // 2
+    gains[:1] = first
+    gains[1:] = second[...]
+    for core in range(2):
+        for side in range(2):
+
+            @pl.when((own_core == core) & (own_side == side))
+            def _():
+                for c in range(2):
+                    for f in range(2):
+                        out = mine if c == core else send
+                        which = 0 if f == side else 1
+                        at = c * LANES + f * half
+                        out[which, :nq] = grad[at : at + nq]
+                        at = 2 * LANES + c * half + f * nk
+                        out[which, nq : nq + nk] = grad[at : at + nk]
+                        at = 3 * LANES + (2 * c + f) * nk
+                        out[which, nq + nk :] = grad[at : at + nk]
+
+
+def owned_kernel(second, up, down, keep, give):
+    side = own_place()[1]
+    rows = keep.shape[0]
+    full = jnp.float32
+    total = second[...].astype(full) + (up[TOK:].astype(full) + down[TOK:].astype(full))
+    keep[...] = jnp.where(side == 0, total[:rows], total[rows:])
+    give[...] = jnp.where(side == 0, total[rows:], total[:rows]).astype(jnp.bfloat16)
+
+
+def last_kernel(joined, weight, up, down, block, middle, gain, out):
+    grad = dot_nn(joined[...], weight[...])
+    grad = grad + (up[:TOK].astype(jnp.float32) + down[:TOK].astype(jnp.float32))
+    values = block[...].astype(jnp.float32)
+    scale = lax.rsqrt(jnp.mean(values * values, axis=-1, keepdims=True) + EPS)
+    weighted = grad * gain[...]
+    inner = jnp.mean(weighted * values, axis=-1, keepdims=True)
+    out[...] = middle[...] + (scale * weighted - values * (scale**3 * inner))
+
+
+def plane_shards(
+    tokens,
+    cotangent,
+    segments,
+    positions,
+    gain_attn,
+    gain_ffn,
+    w_query,
+    w_key,
+    w_value,
+    w_output,
+    w_gate,
+    w_up,
+    w_down,
+):
+    full = jnp.float32
+    low = jnp.bfloat16
+    block = tokens[0]
+    outer = cotangent[0]
+    width = block.shape[1]
+    index = lax.axis_index("blk")
+    side = lax.axis_index("fsdp")
+    core = index % 2
+    chip = index // 2
+    spot = jnp.where(chip % 2 == 0, chip // 2, CHIPS - 1 - chip // 2)
+
+    segs = segments[0]
+    numbers = segs.reshape(2 * CHIPS, TOK)
+    starts = [jnp.sum((segs < number).astype(jnp.int32)) for number in range(1, 4)]
+    row = lax.broadcasted_iota(jnp.int32, (CHIPS * TOK, LANES), 0)
+    nth = row >> 7
+    away = jnp.where((nth & 1) == 1, (nth + 1) >> 1, CHIPS - (nth >> 1))
+    at = (spot + away) & (CHIPS - 1)
+    token = jnp.where(at < CHIPS // 2, 2 * at, 2 * CHIPS - 1 - 2 * at) * (2 * TOK)
+    token = token + core * TOK + (row & (TOK - 1))
+    first = jnp.zeros_like(token)
+    for start in starts:
+        first = jnp.where(token >= start, start, first)
+    half = HD // 2
+    freqs = ROPE_BASE ** (-(jnp.arange(half, dtype=full) * 2.0 / HD))
+    spare = jnp.zeros((LANES // 2 - half,), full)
+    both = jnp.concatenate([freqs, spare, freqs, spare])
+    angles = (token - first).astype(full) * both[None, :]
+    sign = jnp.where(jnp.arange(LANES) < LANES // 2, -1.0, 1.0).astype(full)
+    cosine = jnp.cos(angles)
+    sine = jnp.sin(angles) * sign[None, :]
+
+    ended = [()]
+
+    def held(value):
+        return after(value, *ended[-1])
+
+    def close(*results):
+        flat = []
+        for result in results:
+            flat += list(result) if isinstance(result, (list, tuple)) else [result]
+        ended.append(tuple(flat))
+
+    def to_chips(value):
+        return lax.all_to_all(
+            value, "blk", split_axis=0, concat_axis=0, axis_index_groups=SAME_CORE, tiled=True
+        )
+
+    nq = w_query.shape[0]
+    nk = w_key.shape[0]
+    count = w_gate.shape[0]
+    units = 2 * count
+
+    def wider(vector, bit):
+        other = flipped(vector, bit) if bit else x_swap(vector)
+        return jnp.where(
+            ((index & bit) if bit else side) == 0,
+            jnp.concatenate([vector, other], axis=1),
+            jnp.concatenate([other, vector], axis=1),
+        )
+
+    both = call(
+        stack_kernel, "stack_tokens", (((nq + TOK, width), low),), (w_output, block), far=(0, 1)
+    )[0]
+    tokens_ring = Gather(both)
+    x1 = tokens_ring.step(1)
+    gains = wider(wider(jnp.stack([gain_attn, gain_ffn]), 0), 1)
+    close(x1, gains, cosine, sine)
+
+    x2 = tokens_ring.step(2, *ended[-1])
+    packed = call(
+        stack_kernel,
+        "stack_heads",
+        (((nq + 2 * nk, width), low),),
+        (w_query, w_key, held(w_value)),
+        far=range(3),
+    )[0]
+    near = x_swap(packed)
+    far = core_swap(packed)
+    gains = wider(held(gains), 2)
+    close(x2, near, far, gains)
+
+    def out_pair(first, second):
+        return call(
+            stack_kernel,
+            "stack_pair",
+            (((2 * nq, width), low),),
+            (first, second),
+            far=(0, 1),
+            windows={0: (nq, 0), 1: (nq, 0)},
+        )[0]
+
+    found = tokens_ring.found
+    x3 = tokens_ring.step(3, *ended[-1])
+    across = core_swap(held(near))
+    gains = wider(held(gains), 4)
+    own_outs = [out_pair(held(found[1]), found[7])]
+    near_outs = [x_swap(own_outs[0])]
+    close(x3, across, gains, near_outs)
+
+    x4 = tokens_ring.step(4, *ended[-1])
+    w_heads = call(
+        heads_kernel,
+        "head_rows",
+        (((4 * LANES, width), low),),
+        (packed, near, far, held(across)),
+        far=range(4),
+    )[0]
+    own_outs.append(out_pair(held(found[2]), found[6]))
+    near_outs.append(x_swap(own_outs[1]))
+    gains = wider(held(gains), 8).astype(full)
+    gain_one = gains[:1]
+    gain_two = gains[1:]
+    close(x4, gains, w_heads, near_outs[1])
+
+    outer_ring = Gather(held(outer))
+    e1 = outer_ring.step(1)
+    blocks = [found[j] for j in ARRIVAL[:-1]] + list(found[4])
+    normed, query, kv = project(
+        [held(blocks[0])] + blocks[1:], gain_one, w_heads, cosine, sine
+    )
+    own_outs.append(out_pair(held(found[3]), found[5]))
+    near_outs.append(x_swap(own_outs[2]))
+    own_outs.append(out_pair(held(found[0]), found[4][0]))
+    close(e1, near_outs[2], kv, own_outs[3])
+
+    kv_peer = core_swap(held(kv))
+    close(kv_peer)
+
+    e2 = outer_ring.step(2, *ended[-1])
+    near_outs.append(x_swap(held(own_outs[3])))
+    heads, mixed, lse, query_all, kv_all, kv_peer_all = attend_heads(
+        numbers, query, kv, held(kv_peer)
+    )
+    close(e2, near_outs[3], heads)
+
+    swapped = to_chips(held(heads))
+    near_gate = x_swap(held(w_gate))
+    out_rows = call(
+        out_kernel,
+        "stack_out",
+        (((CHIPS * 2 * nq, width), low),),
+        own_outs + near_outs[:3] + [held(near_outs[3])],
+        far=range(8),
+    )[0]
+    far_ffn = [core_swap(held(w_gate)), core_swap(held(w_up)), core_swap(held(w_down))]
+    close(swapped, near_gate, out_rows, far_ffn)
+
+    e3 = outer_ring.step(3, *ended[-1])
+    out_rows_peer = core_swap(held(out_rows))
+    across_ffn = [core_swap(held(near_gate))]
+    near_up = x_swap(held(w_up))
+    middle, normed_two, attended, w_out = call(
+        join_kernel,
+        "join",
+        (
+            ((TOK, width), full),
+            ((TOK, width), low),
+            ((TOK, width), low),
+            ((width, width), low),
+        ),
+        (held(swapped), out_rows, out_rows_peer, block, gain_two),
+        scratch=[pltpu.VMEM((width, TOK), low)],
+        far=(3,),
+        far_out=(0, 2, 3),
+    )
+    close(e3, normed_two, across_ffn, near_up)
+
+    normed_ring = Gather(held(normed_two))
+    fed = []
+
+    def ffn_group(n):
+        group = GROUPS[n]
+        if len(group) > 1:
+            blocks, outers = ([ring.found[j] for j in group] for ring in (normed_ring, outer_ring))
+        else:
+            blocks, outers = (list(ring.found[group[0]]) for ring in (normed_ring, outer_ring))
+        blocks[0] = held(blocks[0])
+        fed.append(ffn(blocks, outers, w_gu, w_dn))
+        return fed[-1][3]
+
+    h1 = normed_ring.step(1)
+    e4 = outer_ring.step(4, *ended[-1])
+    near_down = x_swap(held(w_down))
+    close(h1, e4, near_down)
+
+    h2 = normed_ring.step(2, *ended[-1])
+    across_ffn += [core_swap(held(near_up)), core_swap(held(near_down))]
+    w_gu, w_dn = call(
+        hidden_kernel,
+        "hidden_rows",
+        (((4 * units, width), low), ((2 * units, width), low)),
+        (w_gate, w_up, w_down, near_gate, near_up, near_down, *far_ffn, *across_ffn),
+        far=range(12),
+    )
+    close(h2, w_gu)
+
+    h3 = normed_ring.step(3, *ended[-1])
+    close(h3, ffn_group(0), ffn_group(1))
+
+    h4 = normed_ring.step(4, *ended[-1])
+    close(h4, ffn_group(2))
+
+    ffn_group(3)
+
+    def stored(terms, name, far=()):
+        def make(number, up, down):
+            if number == 1:
+                return terms[3:]
+            begin = 1 if number == 4 else 0
+            part = terms[4 - number]
+            return call(
+                add_kernel,
+                name,
+                leaving(width),
+                (part, part, up, down),
+                far=far,
+                windows={0: (TOK, begin), 1: (TOK, begin + 1)},
+            )
+
+        return make
+
+    back_ring = Scatter(stored([part[4] for part in fed[:3]] + list(fed[3][4:]), "back_add"))
+    close(back_ring.step(1))
+
+    d2 = back_ring.step(2, *ended[-1])
+    arrays = [part[n] for n in range(4) for part in fed]
+    arrays[0] = held(arrays[0])
+    sums = call(
+        functools.partial(grads_kernel, len(GROUPS)),
+        "ffn_grads",
+        [((2 * units, width), full), ((units, width), full)] * 2 + [((CHIPS * TOK, 2 * units), low)],
+        arrays,
+        scratch=[
+            pltpu.VMEM((CHIPS * TOK, width), low),
+            pltpu.VMEM((CHIPS * TOK, 4 * units), low),
+        ],
+        far_out=(4,),
+    )
+    close(d2, sums[2])
+
+    d3 = back_ring.step(3, *ended[-1])
+    others = [core_swap(held(value)) for value in sums[2:4]]
+    branch = call(
+        branch_kernel,
+        "branch",
+        [((len(group) * TOK, width), full) for group in GROUPS[:3]] + leaving(width, TOK // 2),
+        (held(sums[4]), w_dn),
+        far_out=(0, 1, 2),
+    )
+    close(d3, others, branch[-1])
+
+    d4 = back_ring.step(4, *ended[-1])
+    kept = call(
+        owners_kernel,
+        "ffn_owners",
+        [((count, width), full)] * 3 + [((count, width), low)] * 3,
+        (*sums[:2], held(others[0]), others[1]),
+        far_out=(0, 1, 2),
+    )
+    near_grads = [x_swap(kept[3])]
+    close(d4, near_grads)
+
+    branch_ring = Scatter(stored(branch, "branch_add", (0, 1)))
+    z1 = branch_ring.step(1, *ended[-1])
+    grad_middle, grad_branch, grad_heads, second_gain_grad = call(
+        turn_kernel,
+        "turn",
+        (
+            ((TOK, width), full),
+            ((TOK, width), low),
+            ((CHIPS, PAIR, TOK), low),
+            ((1, width), full),
+        ),
+        (fed[0][4], *d4, middle, outer, gain_two, w_out),
+        far=(3, 4, 6),
+        far_out=(0,),
+        windows={0: (TOK, 0)},
+    )
+    close(z1, grad_heads)
+
+    grad_heads = to_chips(held(grad_heads))
+    z2 = branch_ring.step(2, *ended[-1])
+    near_grads.append(x_swap(held(kept[4])))
+    keep, give = call(
+        outer_kernel,
+        "outer",
+        (((CHIPS, 2 * nq, width), low), ((CHIPS, 2 * nq, width), low)),
+        (held(grad_branch), attended),
+        far=(1,),
+        far_out=(0,),
+        scratch=[pltpu.VMEM((width, width), full)],
+    )
+    close(grad_heads, z2, near_grads[1], give)
+
+    z3 = branch_ring.step(3, *ended[-1])
+    other = core_swap(held(give))
+    grad_query, grad_own, grad_peer = attend_back(
+        numbers, query_all, kv_all, kv_peer_all, held(grad_heads), mixed, lse, cosine, sine
+    )
+    close(z3, other, grad_query)
+
+    z4 = branch_ring.step(4, *ended[-1])
+    second = call(
+        settle_kernel,
+        "settle",
+        (((CHIPS * 2 * nq, width), low),),
+        (keep, held(other)),
+        far=(0,),
+    )[0]
+    joined, *leave = call(
+        spread_kernel,
+        "spread",
+        [((CHIPS * TOK, 4 * LANES), low)] + leaving(width, TOK // 2 + nq),
+        (grad_query, grad_own, core_swap(held(grad_peer)), cosine, sine, w_heads, second),
+        far=(3, 4, 5),
+    )
+    close(z4, leave)
+
+    def last_terms(number, up, down):
+        if number == 1:
+            return leave
+        begin = STEP_ROWS[number] // TOK
+        return call(
+            both_kernel,
+            "last_terms",
+            leaving(width, TOK + 2 * nq),
+            (joined, joined, w_heads, second, second, up, down),
+            far=(0, 1, 2, 3, 4),
+            windows={
+                0: (TOK, begin),
+                1: (TOK, begin + 1),
+                3: (2 * nq, begin),
+                4: (2 * nq, begin + 1),
+            },
+        )
+
+    last_ring = Scatter(last_terms)
+    t1 = last_ring.step(1, *ended[-1])
+    mine, send, gain_grads = call(
+        heads_grad_kernel,
+        "heads_grad",
+        (((2, HD, width), full), ((2, HD, width), full), ((2, width), full)),
+        (held(joined), w_heads, gain_one, second_gain_grad, normed),
+        scratch=[pltpu.VMEM((4 * LANES, width), full)],
+        far=range(1, 5),
+    )
+    near_grads.append(x_swap(held(kept[5])))
+    close(t1, send, gain_grads, near_grads[2])
+
+    t2 = last_ring.step(2, *ended[-1])
+    other = core_swap(held(send))
+    result = call(
+        result_kernel,
+        "result",
+        (((TOK, width), low),),
+        (branch[0], held(z4[0]), z4[1], middle),
+        far=(0, 3),
+        far_out=(0,),
+        windows={0: (TOK, 0)},
+    )[0]
+    gain_grads = gain_grads + flipped(held(gain_grads), 2)
+    close(t2, other, result, gain_grads)
+
+    t3 = last_ring.step(3, *ended[-1])
+    mine = mine + held(other)
+    heads_grad = mine[0] + x_swap(mine[1].astype(low)).astype(full)
+    gain_grads = gain_grads + flipped(held(gain_grads), 4)
+    close(t3, heads_grad, gain_grads)
+
+    t4 = last_ring.step(4, *ended[-1])
+    gain_grads = gain_grads + flipped(held(gain_grads), 8)
+    ffn_grad = [own + held(other).astype(full) for own, other in zip(kept[:3], near_grads)]
+    close(t4, gain_grads, ffn_grad)
+
+    keep, give = call(
+        owned_kernel,
+        "owned",
+        (((nq, width), full), ((nq, width), low)),
+        (second, held(t4[0]), t4[1]),
+        far=(0,),
+        windows={0: (2 * nq, 0)},
+    )
+    output_grad = keep + x_swap(give).astype(full)
+    gain_grads = gain_grads + core_swap(held(gain_grads))
+    gain_grads = gain_grads + x_swap(gain_grads)
+    gain_grads = lax.dynamic_slice_in_dim(gain_grads, (2 * index + side) * nq, nq, 1)
+    grad_tokens = call(
+        last_kernel,
+        "last",
+        (((TOK, width), full),),
+        (joined, w_heads, held(t4[0]), t4[1], block, grad_middle, gain_one),
+        far=(0, 1, 4, 5),
+        far_out=(0,),
+        windows={0: (TOK, 0)},
+    )[0]
+    return (
+        result[None],
+        grad_tokens[None],
+        gain_grads[0],
+        gain_grads[1],
+        heads_grad[:nq],
+        heads_grad[nq : nq + nk],
+        heads_grad[nq + nk :],
+        output_grad,
+        ffn_grad[0],
+        ffn_grad[1],
+        ffn_grad[2],
+    )
+
+
+def by_plane(mesh):
+    return dict(mesh.shape) == {"blk": 2 * CHIPS, "fsdp": 2} and KVH == CHIPS
+
+
 def solution(mesh):
     in_specs = (
         P("fsdp", "blk", None),
@@ -350,4 +1460,5 @@
         P(("blk", "fsdp"), None),
         P(("blk", "fsdp"), None),
     )
-    return jax.shard_map(shards, mesh=mesh, in_specs=in_specs, out_specs=out_specs, check_vma=False)
+    body = plane_shards if by_plane(mesh) else shards
+    return jax.shard_map(body, mesh=mesh, in_specs=in_specs, out_specs=out_specs, check_vma=False)

time: 2360 us -> 358 us (0.15)
  waiting for transfers between devices: 1750 us -> 135 us
  matrix products: 230 us -> 0 us
  local copies, waits for them, and re-layouts: 114 us -> 9.9 us
  Pallas kernels: 0 us -> 97.7 us
  blocking collectives: 79.4 us -> 0 us
  other arithmetic: 80.3 us -> 12.7 us
  starting transfers between devices: 66.1 us -> 94.1 us
    reduce_scatter x7 -> x0, waiting for transfers between devices: 1150 us -> none  [the longest x1 253 us: shards(): lax.psum_scatter(up_grad, ('blk', 'fsdp'), scatter_dimension=0, tiled=True)]
    all_gather x9 -> x0, waiting for transfers between devices: 480 us -> none  [the longest x1 93.5 us: fetch_ffn(): lax.all_gather(w_gate, ('blk', 'fsdp'), axis=0, tiled=True)]
    dot_general x109 -> x0, matrix products: 230 us -> none  [the longest x7 47.7 us: product_tn(): lax.dot_general(left, right, (((0,), (0,)), ((), ())), preferred_element_...]
    pallas_call x0 -> x37, Pallas kernels: none -> 97.7 us  [call(): pl.pallas_call(kernel, grid=(1,), out_shape=tuple(shapes), in_specs=[wind...]
    unnamed x2 -> x0, blocking collectives: 79.4 us -> none
    convert_element_type x41 -> x1, other arithmetic: 56 us -> 0.01 us  [plane_shards(): gains = wider(held(gains), 8).astype(full)]
    while x68 -> x0, local copies, waits for them, and re-layouts: 40.8 us -> none
    dynamic_slice x41 -> x0, local copies, waits for them, and re-layouts: 33.6 us -> none  [the longest x16 19.8 us: cycle_back(): final, unused = lax.scan(step, start, jnp.arange(count, dtype=jnp.int32))]
  transfers between devices with their start and end apart: 80 -> 88, of which waited for: 47 -> 43; matrix products, arithmetic and copies ran while one was open for 16% -> 5% of each run, Pallas kernels for 0% -> 26%
where the time goes in v2:
time: 358 us; the launch traced here: 352 us
  waiting for transfers between devices  135 us (38%)
  Pallas kernels  97.7 us (27%)
  starting transfers between devices  94.1 us (26%)
  other arithmetic  12.7 us (4%)
  local copies, waits for them, and re-layouts  9.9 us (3%)
    pallas_call x37, Pallas kernels, call(): pl.pallas_call(kernel, grid=(1,), out_shape=tuple(shapes), in_specs=[wind...  97.7 us
    ppermute x24, waiting for transfers between devices, ring_up(): return lax.ppermute(value, 'blk', ring_route(1))  47.6 us
    ppermute x23, waiting for transfers between devices, flipped(): return lax.ppermute(value, 'blk', [(i, i ^ bit) for i in range(2 * CHIPS)])  46.4 us
    ppermute x24, waiting for transfers between devices, ring_down(): return lax.ppermute(value, 'blk', ring_route(-1))  29 us
    ppermute x24, starting transfers between devices, ring_up(): return lax.ppermute(value, 'blk', ring_route(1))  27.3 us
    ppermute x24, starting transfers between devices, ring_down(): return lax.ppermute(value, 'blk', ring_route(-1))  26 us
    ppermute x15, starting transfers between devices, x_swap(): return lax.ppermute(value, 'fsdp', [(0, 1), (1, 0)])  20.7 us
    ppermute x23, starting transfers between devices, flipped(): return lax.ppermute(value, 'blk', [(i, i ^ bit) for i in range(2 * CHIPS)])  13.2 us
  transfers between devices with their start and end apart: 88, of which 43 were waited for; matrix products, arithmetic and copies ran while one was open for 5% of the time, Pallas kernels for 26%

profile of v2, /device:TPU:0, one launch (start us, length us, event | category | flops | bytes accessed | tf_op | source)
XLA Modules:
  0.0 351.7 jit_solution(1265446661334329209)
XLA Ops:
  1.8 3.0 collective-permute-start.1
  10.0 4.2 %sine_multiply_fusion = (f32[1024,128]{1,0:T(8,128)S(1)}, f32[1024,128]{1,0:T(8,128)S(1)}) fusion(f32[128]{0:T(128)S(1)} %get-tuple-element.390, f32[128]{0:T(128)S(1)} %get-tuple-element.391, s32[]{:T(128)} %get-tuple-element.378, s32[]{:T(128)} %get-tuple-element.379, s32[]{:T(128)} %get-tuple-element.377, s32[1024]{0:T(1024)S(1)} %get-tuple-element.388, ...), kind=kLoop, calls=%fused_computation.10 | loop fusion | flops 2621440 | bytes 1062932 | tf_op jit(solution)/shard_map/mul | solution.py:1049
  14.3 2.8 collective-permute-done.1.refs_0_.refs_1_
  24.8 6.7 %collective-permute-done.8 = bf16[2,192]{1,0:T(2,128)(2,1)S(1)} collective-permute-done((bf16[2,192]{1,0:T(2,128)(2,1)S(1)}, bf16[2,192]{1,0:T(2,128)(2,1)S(1)}, u32[]{:S(2)}, u32[]{:S(2)}) %collective-permute-start.8) | collective-permute-done | bytes 800 | tf_op jit(solution)/shard_map/ppermute | solution.py:355
  38.1 7.4 %collective-permute-done.12 = bf16[2,384]{1,0:T(2,128)(2,1)S(1)} collective-permute-done((bf16[2,384]{1,0:T(2,128)(2,1)}, bf16[2,384]{1,0:T(2,128)(2,1)S(1)}, u32[]{:S(2)}, u32[]{:S(2)}) %collective-permute-start.12) | collective-permute-done | bytes 1568 | tf_op jit(solution)/shard_map/ppermute | solution.py:355
  53.5 3.5 %collective-permute-start.16 = (bf16[2,768]{1,0:T(2,128)(2,1)S(1)}, bf16[2,768]{1,0:T(2,128)(2,1)S(1)}, u32[]{:S(2)}, u32[]{:S(2)}) collective-permute-start(bf16[2,768]{1,0:T(2,128)(2,1)S(1)} %broadcast_select_fusion.1), channel_id=1, source_target_pairs={{0,16},{2,18},{4,20},{6,22},{8,24},{10,26},{12,28},{14,30},{16,0},... | collective-permute-start | bytes 9224 | tf_op jit(solution)/shard_map/ppermute | solution.py:355
  58.5 2.0 collective-permute-done.16
  66.8 5.5 %project.1 = (bf16[1024,1536]{1,0:T(8,128)(2,1)}, bf16[1024,256]{1,0:T(8,128)(2,1)S(1)}, bf16[1024,256]{1,0:T(8,128)(2,1)S(1)}) custom-call(bf16[176,1536]{1,0:T(8,128)(2,1)} %copy-done.5, bf16[176,1536]{1,0:T(8,128)(2,1)} %copy-done.26, bf16[176,1536]{1,0:T(8,128)(2,1)} %copy-done.27, bf16[176,1536]{1,0:T(8,128)(2,1)} %collective-permute-done.5.refs_0_.refs_3_, ...), custom_call_target="tpu_custom_call" | custom-call | tf_op jit(solution)/shard_map/project/pallas_call | solution.py:441
  78.4 6.7 %attend.1 = (bf16[8,192,128]{2,1,0:T(8,128)(2,1)}, f32[8,128,256]{2,1,0:T(8,128)}, f32[8,1,256]{2,1,0:T(1,128)}, bf16[1024,256]{1,0:T(8,128)(2,1)}, bf16[1024,25...) custom-call(s32[16,128]{1,0:T(8,128)S(1)} %bitcast.21, bf16[1024,256]{1,0:T(8,128)(2,1)S(1)} %get-tuple-element.209.query_in, ...), custom_call_target="tpu_custom_call" | custom-call | tf_op jit(solution)/shard_map/attend/pallas_call | solution.py:441
  85.7 2.0 collective-permute-done.23.refs_2_
  87.7 3.5 all-to-all-start
  95.1 8.0 %collective-permute-done.25.refs_3_ = bf16[128,1536]{1,0:T(8,128)(2,1)} collective-permute-done((bf16[128,1536]{1,0:T(8,128)(2,1)}, bf16[128,1536]{1,0:T(8,128)(2,1)}, u32[]{:S(2)}, u32[]{:S(2)}) %collective-permute-start.25) | collective-permute-done | bytes 393248 | tf_op jit(solution)/shard_map/ppermute | solution.py:363
  108.4 4.4 %join.1 = (f32[128,1536]{1,0:T(8,128)}, bf16[128,1536]{1,0:T(8,128)(2,1)S(1)}, bf16[128,1536]{1,0:T(8,128)(2,1)}, bf16[1536,1536]{1,0:T(8,128)(2,1)}) custom-call(bf16[8,192,128]{2,1,0:T(8,128)(2,1)S(1)} %all-to-all-done.heads, bf16[768,1536]{1,0:T(8,128)(2,1)S(1)} %stack_out.1.refs_0_, bf16[768,1536]{1,0:T(8,128)(2,1)S(1)} %collective-permute-done.29.refs_1_, ...), custom_call_target="tpu_custom_call" | custom-call | tf_op jit(solution)/shard_map/join/pallas_call | solution.py:441
  112.8 2.8 collective-permute-done.30.refs_3_
  123.3 9.5 %collective-permute-done.37.refs_3_ = bf16[64,1536]{1,0:T(8,128)(2,1)S(1)} collective-permute-done((bf16[64,1536]{1,0:T(8,128)(2,1)S(1)}, bf16[64,1536]{1,0:T(8,128)(2,1)S(1)}, u32[]{:S(2)}, u32[]{:S(2)}) %collective-permute-start.37) | collective-permute-done | bytes 196640 | tf_op jit(solution)/shard_map/ppermute | solution.py:351
  138.4 2.6 hidden_rows.1
  141.0 5.0 %collective-permute-done.39.refs_1_ = bf16[128,1536]{1,0:T(8,128)(2,1)S(1)} collective-permute-done((bf16[128,1536]{1,0:T(8,128)(2,1)S(1)}, bf16[128,1536]{1,0:T(8,128)(2,1)S(1)}, u32[]{:S(2)}, u32[]{:S(2)}) %collective-permute-start.39) | collective-permute-done | bytes 393248 | tf_op jit(solution)/shard_map/ppermute | solution.py:347
  148.2 2.3 ffn.5
  150.5 3.4 ffn.4
  153.9 2.4 collective-permute-done.43.refs_1_
  159.7 2.3 ffn.6
  163.9 2.1 ffn.7
  168.1 4.6 %collective-permute-done.47.up = bf16[64,1536]{1,0:T(8,128)(2,1)S(1)} collective-permute-done((bf16[64,1536]{1,0:T(8,128)(2,1)S(1)}, bf16[64,1536]{1,0:T(8,128)(2,1)S(1)}, u32[]{:S(2)}, u32[]{:S(2)}) %collective-permute-start.47) | collective-permute-done | bytes 196640 | tf_op jit(solution)/shard_map/ppermute | solution.py:347
  176.6 6.6 %ffn_grads.1 = (f32[512,1536]{1,0:T(8,128)S(1)}, f32[256,1536]{1,0:T(8,128)S(1)}, f32[512,1536]{1,0:T(8,128)}, f32[256,1536]{1,0:T(8,128)S(1)}, bf16[1024,512]{1,0:T(8,128)(2,1)}) custom-call(bf16[384,1536]{1,0:T(8,128)(2,1)S(1)} %get-tuple-element.255.refs_0_, bf16[256,1536]{1,0:T(8,128)(2,1)S(1)} %get-tuple-element.256.refs_1_, ...), custom_call_target="tpu_custom_call" | custom-call | tf_op jit(solution)/shard_map/ffn_grads/pallas_call | solution.py:441
  186.5 4.0 %branch.1 = (f32[384,1536]{1,0:T(8,128)}, f32[256,1536]{1,0:T(8,128)}, f32[256,1536]{1,0:T(8,128)}, bf16[64,1536]{1,0:T(8,128)(2,1)S(1)}, bf16[64,1536]{1,0:T(8,128)(2,1)S(1)}) custom-call(bf16[1024,512]{1,0:T(8,128)(2,1)S(1)} %copy-done.13, bf16[512,1536]{1,0:T(8,128)(2,1)S(1)} %get-tuple-element.241.refs_7_.refs_5_.down_rows), custom_call_target="tpu_custom_call" | custom-call | tf_op jit(solution)/shard_map/branch/pallas_call | solution.py:441
  190.5 5.0 %collective-permute-done.51.up = bf16[128,1536]{1,0:T(8,128)(2,1)S(1)} collective-permute-done((bf16[128,1536]{1,0:T(8,128)(2,1)S(1)}, bf16[128,1536]{1,0:T(8,128)(2,1)S(1)}, u32[]{:S(2)}, u32[]{:S(2)}) %collective-permute-start.51) | collective-permute-done | bytes 393248 | tf_op jit(solution)/shard_map/ppermute | solution.py:347
  202.4 5.0 %collective-permute-done.55.refs_1_ = bf16[128,1536]{1,0:T(8,128)(2,1)S(1)} collective-permute-done((bf16[128,1536]{1,0:T(8,128)(2,1)S(1)}, bf16[128,1536]{1,0:T(8,128)(2,1)S(1)}, u32[]{:S(2)}, u32[]{:S(2)}) %collective-permute-start.55) | collective-permute-done | bytes 393248 | tf_op jit(solution)/shard_map/ppermute | solution.py:347
  212.5 4.7 %turn.1 = (f32[128,1536]{1,0:T(8,128)}, bf16[128,1536]{1,0:T(8,128)(2,1)S(1)}, bf16[8,192,128]{2,1,0:T(8,128)(2,1)}, f32[1,1536]{1,0:T(1,128)S(1)}) custom-call(f32[384,1536]{1,0:T(8,128)S(1)} %get-tuple-element.281.up_term.down_term.refs_0_, bf16[128,1536]{1,0:T(8,128)(2,1)S(1)} %collective-permute-done.55.refs_1_, ...), custom_call_target="tpu_custom_call" | custom-call | tf_op jit(solution)/shard_map/turn/pallas_call | solution.py:441
  217.8 3.5 all-to-all-start.1
  226.3 4.8 %outer.1 = (bf16[8,96,1536]{2,1,0:T(8,128)(2,1)}, bf16[8,96,1536]{2,1,0:T(8,128)(2,1)S(1)}) custom-call(bf16[128,1536]{1,0:T(8,128)(2,1)S(1)} %get-tuple-element.313.branch, bf16[128,1536]{1,0:T(8,128)(2,1)} %get-tuple-element.314.attended), custom_call_target="tpu_custom_call" | custom-call | tf_op jit(solution)/shard_map/outer/pallas_call | solution.py:441
  232.5 2.3 collective-permute-done.60.up
  238.3 2.7 collective-permute-start.63
  241.3 8.9 %attend_back.1 = (bf16[1024,256]{1,0:T(8,128)(2,1)S(1)}, f32[1024,256]{1,0:T(8,128)S(1)}, f32[1024,256]{1,0:T(8,128)S(1)}) custom-call(s32[16,128]{1,0:T(8,128)S(1)} %bitcast.22, bf16[1024,256]{1,0:T(8,128)(2,1)} %get-tuple-element.321.query, bf16[1024,256]{1,0:T(8,128)(2,1)} %get-tuple-element.322.own, bf16[1024,256]{1,0:T(8,128)(2,1)} %get-tuple-element.323.peer, ...), custom_call_target="tpu_custom_call" | custom-call | tf_op jit(solution)/shard_map/attend_back/pallas_call | solution.py:441
  250.2 2.3 collective-permute-done.64.down
  256.1 2.2 settle.1.second.up_second.down_second
  258.3 3.1 spread.1
  261.5 4.1 %collective-permute-done.66.up = bf16[128,1536]{1,0:T(8,128)(2,1)S(1)} collective-permute-done((bf16[128,1536]{1,0:T(8,128)(2,1)S(1)}, bf16[128,1536]{1,0:T(8,128)(2,1)S(1)}, u32[]{:S(2)}, u32[]{:S(2)}) %collective-permute-start.66) | collective-permute-done | bytes 393248 | tf_op jit(solution)/shard_map/ppermute | solution.py:347
  269.2 4.4 %heads_grad.1 = (f32[2,96,1536]{2,1,0:T(8,128)S(1)}, f32[2,96,1536]{2,1,0:T(8,128)S(1)}, f32[2,1536]{1,0:T(2,128)S(1)}) custom-call(bf16[1024,512]{1,0:T(8,128)(2,1)S(1)} %get-tuple-element.340.refs_0_.up_left.down_left.joined, bf16[512,1536]{1,0:T(8,128)(2,1)} %copy-done.1, f32[1,1536]{1,0:T(1,128)} %copy-done.18, f32[1,1536]{1,0:T(1,128)} %copy-done.22, ...), custom_call_target="tpu_custom_call" | custom-call | tf_op jit(solution)/shard_map/heads_grad/pallas_call | solution.py:441
  273.6 2.9 collective-permute-done.69.up
  276.6 2.3 last_terms.3
  282.9 2.3 result.1
  285.2 11.9 %collective-permute-done.75 = f32[2,1536]{1,0:T(2,128)S(1)} collective-permute-done((f32[2,1536]{1,0:T(2,128)S(1)}, f32[2,1536]{1,0:T(2,128)S(1)}, u32[]{:S(2)}, u32[]{:S(2)}) %collective-permute-start.75) | collective-permute-done | bytes 12320 | tf_op jit(solution)/shard_map/ppermute | solution.py:355
  299.1 2.4 last_terms.4
  305.2 14.4 %collective-permute-done.79 = f32[2,1536]{1,0:T(2,128)S(1)} collective-permute-done((f32[2,1536]{1,0:T(2,128)S(1)}, f32[2,1536]{1,0:T(2,128)S(1)}, u32[]{:S(2)}, u32[]{:S(2)}) %collective-permute-start.79) | collective-permute-done | bytes 12320 | tf_op jit(solution)/shard_map/ppermute | solution.py:355
  319.8 2.3 collective-permute-start.82
  322.1 2.4 last_terms.5
  329.6 10.0 %collective-permute-done.80.up = bf16[224,1536]{1,0:T(8,128)(2,1)S(1)} collective-permute-done((bf16[224,1536]{1,0:T(8,128)(2,1)S(1)}, bf16[224,1536]{1,0:T(8,128)(2,1)S(1)}, u32[]{:S(2)}, u32[]{:S(2)}) %collective-permute-start.80) | collective-permute-done | bytes 688160 | tf_op jit(solution)/shard_map/ppermute | solution.py:347
  345.8 3.2 last.1
  (289 shorter events, 135.3 us)
Async XLA Ops:
  1.8 15.4 %collective-permute-start.1 = (bf16[176,1536]{1,0:T(8,128)(2,1)S(1)}, bf16[176,1536]{1,0:T(8,128)(2,1)S(1)}, u32[]{:S(2)}, u32[]{:S(2)}) collective-permute-start(bf16[176,1536]{1,0:T(8,128)(2,1)S(1)} %stack_tokens.1.refs_0_), channel_id=1, source_target_pairs={{0,4},{2,6},{8,0},{10,2},{16,8},{18,10},{24,16},{26,18},{28,24},{3... | collective-permute-start | bytes 1622024 | tf_op jit(solution)/shard_map/ppermute | solution.py:351
  4.8 13.7 %collective-permute-start = (bf16[176,1536]{1,0:T(8,128)(2,1)S(1)}, bf16[176,1536]{1,0:T(8,128)(2,1)S(1)}, u32[]{:S(2)}, u32[]{:S(2)}) collective-permute-start(bf16[176,1536]{1,0:T(8,128)(2,1)S(1)} %stack_tokens.1.refs_0_), channel_id=1, source_target_pairs={{0,8},{2,10},{8,16},{10,18},{16,24},{18,26},{24,28},{26,30},{28,20... | collective-permute-start | bytes 1622024 | tf_op jit(solution)/shard_map/ppermute | solution.py:347
  18.5 13.6 %collective-permute-start.4 = (bf16[176,1536]{1,0:T(8,128)(2,1)S(1)}, bf16[176,1536]{1,0:T(8,128)(2,1)}, u32[]{:S(2)}, u32[]{:S(2)}) collective-permute-start(bf16[176,1536]{1,0:T(8,128)(2,1)S(1)} %collective-permute-done.refs_1_.refs_2_), channel_id=1, source_target_pairs={{0,8},{2,10},{8,16},{10,18},{16,24},{18,26},{24,28},{26,30},{28,20... | collective-permute-start | bytes 1622024 | tf_op jit(solution)/shard_map/ppermute | solution.py:347
  18.9 13.9 %collective-permute-start.5 = (bf16[176,1536]{1,0:T(8,128)(2,1)S(1)}, bf16[176,1536]{1,0:T(8,128)(2,1)}, u32[]{:S(2)}, u32[]{:S(2)}) collective-permute-start(bf16[176,1536]{1,0:T(8,128)(2,1)S(1)} %collective-permute-done.1.refs_0_.refs_1_), channel_id=1, source_target_pairs={{0,4},{2,6},{8,0},{10,2},{16,8},{18,10},{24,16},{26,18},{28,24},{3... | collective-permute-start | bytes 1622024 | tf_op jit(solution)/shard_map/ppermute | solution.py:351
  21.6 10.5 %collective-permute-start.7 = (bf16[96,1536]{1,0:T(8,128)(2,1)S(1)}, bf16[96,1536]{1,0:T(8,128)(2,1)S(1)}, u32[]{:S(2)}, u32[]{:S(2)}) collective-permute-start(bf16[96,1536]{1,0:T(8,128)(2,1)S(1)} %stack_heads.1.own), channel_id=1, source_target_pairs={{0,2},{2,0},{4,6},{6,4},{8,10},{10,8},{12,14},{14,12},{16,18},{18,... | collective-permute-start | bytes 884744 | tf_op jit(solution)/shard_map/ppermute | solution.py:355
  32.8 13.5 %collective-permute-start.9 = (bf16[176,1536]{1,0:T(8,128)(2,1)}, bf16[176,1536]{1,0:T(8,128)(2,1)S(1)}, u32[]{:S(2)}, u32[]{:S(2)}) collective-permute-start(bf16[176,1536]{1,0:T(8,128)(2,1)} %collective-permute-done.4.refs_1_.refs_4_), channel_id=1, source_target_pairs={{0,8},{2,10},{8,16},{10,18},{16,24},{18,26},{24,28},{26,30},{28,20... | collective-permute-start | bytes 1622024 | tf_op jit(solution)/shard_map/ppermute | solution.py:347
  33.5 13.5 %collective-permute-start.10 = (bf16[176,1536]{1,0:T(8,128)(2,1)}, bf16[176,1536]{1,0:T(8,128)(2,1)S(1)}, u32[]{:S(2)}, u32[]{:S(2)}) collective-permute-start(bf16[176,1536]{1,0:T(8,128)(2,1)} %collective-permute-done.5.refs_0_.refs_3_), channel_id=1, source_target_pairs={{0,4},{2,6},{8,0},{10,2},{16,8},{18,10},{24,16},{26,18},{28,24},{3... | collective-permute-start | bytes 1622024 | tf_op jit(solution)/shard_map/ppermute | solution.py:351
  48.3 12.2 %collective-permute-start.17 = (bf16[96,1536]{1,0:T(8,128)(2,1)S(1)}, bf16[96,1536]{1,0:T(8,128)(2,1)}, u32[]{:S(2)}, u32[]{:S(2)}) collective-permute-start(bf16[96,1536]{1,0:T(8,128)(2,1)S(1)} %stack_pair.5.refs_1_), channel_id=1, source_target_pairs={{0,1},{1,0},{2,3},{3,2},{4,5},{5,4},{6,7},{7,6},{8,9},{9,8},{10,11... | collective-permute-start | bytes 884744 | tf_op jit(solution)/shard_map/ppermute | solution.py:363
  60.6 11.7 %collective-permute-start.19 = (bf16[128,1536]{1,0:T(8,128)(2,1)S(1)}, bf16[128,1536]{1,0:T(8,128)(2,1)S(1)}, u32[]{:S(2)}, u32[]{:S(2)}) collective-permute-start(bf16[128,1536]{1,0:T(8,128)(2,1)S(1)} %bitcast.18), channel_id=1, source_target_pairs={{0,4},{2,6},{8,0},{10,2},{16,8},{18,10},{24,16},{26,18},{28,24},{3... | collective-permute-start | bytes 1179656 | tf_op jit(solution)/shard_map/ppermute | solution.py:351
  74.3 11.3 %collective-permute-start.22 = (bf16[128,1536]{1,0:T(8,128)(2,1)S(1)}, bf16[128,1536]{1,0:T(8,128)(2,1)S(1)}, u32[]{:S(2)}, u32[]{:S(2)}) collective-permute-start(bf16[128,1536]{1,0:T(8,128)(2,1)S(1)} %collective-permute-done.18.refs_5_), channel_id=1, source_target_pairs={{0,8},{2,10},{8,16},{10,18},{16,24},{18,26},{24,28},{26,30},{28,20... | collective-permute-start | bytes 1179656 | tf_op jit(solution)/shard_map/ppermute | solution.py:347
  76.3 11.4 %collective-permute-start.23 = (bf16[128,1536]{1,0:T(8,128)(2,1)S(1)}, bf16[128,1536]{1,0:T(8,128)(2,1)S(1)}, u32[]{:S(2)}, u32[]{:S(2)}) collective-permute-start(bf16[128,1536]{1,0:T(8,128)(2,1)S(1)} %collective-permute-done.19.refs_4_), channel_id=1, source_target_pairs={{0,4},{2,6},{8,0},{10,2},{16,8},{18,10},{24,16},{26,18},{28,24},{3... | collective-permute-start | bytes 1179656 | tf_op jit(solution)/shard_map/ppermute | solution.py:351
  87.7 16.2 %all-to-all-start = ((bf16[8,192,128]{2,1,0:T(8,128)(2,1)}), bf16[8,192,128]{2,1,0:T(8,128)(2,1)S(1)}, u32[]{:S(2)}, u32[]{:S(2)}) async-start(bf16[8,192,128]{2,1,0:T(8,128)(2,1)} %get-tuple-element.219), calls=%async_computation | async-start | bytes 786432 | tf_op jit(solution)/shard_map/all_to_all | solution.py:1063
  91.2 11.8 %collective-permute-start.25 = (bf16[128,1536]{1,0:T(8,128)(2,1)}, bf16[128,1536]{1,0:T(8,128)(2,1)}, u32[]{:S(2)}, u32[]{:S(2)}) collective-permute-start(bf16[128,1536]{1,0:T(8,128)(2,1)} %refs_0_.5), channel_id=1, source_target_pairs={{0,1},{1,0},{2,3},{3,2},{4,5},{5,4},{6,7},{7,6},{8,9},{9,8},{10,11... | collective-permute-start | bytes 1179656 | tf_op jit(solution)/shard_map/ppermute | solution.py:363
  93.0 10.9 %collective-permute-start.28 = (bf16[128,1536]{1,0:T(8,128)(2,1)}, bf16[128,1536]{1,0:T(8,128)(2,1)}, u32[]{:S(2)}, u32[]{:S(2)}) collective-permute-start(bf16[128,1536]{1,0:T(8,128)(2,1)} %refs_2_.2), channel_id=1, source_target_pairs={{0,2},{2,0},{4,6},{6,4},{8,10},{10,8},{12,14},{14,12},{16,18},{18,... | collective-permute-start | bytes 1179656 | tf_op jit(solution)/shard_map/ppermute | solution.py:355
  103.9 11.7 %collective-permute-start.30 = (bf16[128,1536]{1,0:T(8,128)(2,1)S(1)}, bf16[128,1536]{1,0:T(8,128)(2,1)S(1)}, u32[]{:S(2)}, u32[]{:S(2)}) collective-permute-start(bf16[128,1536]{1,0:T(8,128)(2,1)S(1)} %collective-permute-done.22.refs_3_), channel_id=1, source_target_pairs={{0,8},{2,10},{8,16},{10,18},{16,24},{18,26},{24,28},{26,30},{28,20... | collective-permute-start | bytes 1179656 | tf_op jit(solution)/shard_map/ppermute | solution.py:347
  105.8 11.2 %collective-permute-start.31 = (bf16[128,1536]{1,0:T(8,128)(2,1)S(1)}, bf16[128,1536]{1,0:T(8,128)(2,1)S(1)}, u32[]{:S(2)}, u32[]{:S(2)}) collective-permute-start(bf16[128,1536]{1,0:T(8,128)(2,1)S(1)} %collective-permute-done.23.refs_2_), channel_id=1, source_target_pairs={{0,4},{2,6},{8,0},{10,2},{16,8},{18,10},{24,16},{26,18},{28,24},{3... | collective-permute-start | bytes 1179656 | tf_op jit(solution)/shard_map/ppermute | solution.py:351
  105.9 11.1 %collective-permute-start.32 = (bf16[128,1536]{1,0:T(8,128)(2,1)}, bf16[128,1536]{1,0:T(8,128)(2,1)S(1)}, u32[]{:S(2)}, u32[]{:S(2)}) collective-permute-start(bf16[128,1536]{1,0:T(8,128)(2,1)} %collective-permute-done.25.refs_3_), channel_id=1, source_target_pairs={{0,2},{2,0},{4,6},{6,4},{8,10},{10,8},{12,14},{14,12},{16,18},{18,... | collective-permute-start | bytes 1179656 | tf_op jit(solution)/shard_map/ppermute | solution.py:355
  106.0 11.7 %collective-permute-start.33 = (bf16[128,1536]{1,0:T(8,128)(2,1)}, bf16[128,1536]{1,0:T(8,128)(2,1)S(1)}, u32[]{:S(2)}, u32[]{:S(2)}) collective-permute-start(bf16[128,1536]{1,0:T(8,128)(2,1)} %refs_1_.3), channel_id=1, source_target_pairs={{0,1},{1,0},{2,3},{3,2},{4,5},{5,4},{6,7},{7,6},{8,9},{9,8},{10,11... | collective-permute-start | bytes 1179656 | tf_op jit(solution)/shard_map/ppermute | solution.py:363
  117.7 16.6 %collective-permute-start.35 = (bf16[128,1536]{1,0:T(8,128)(2,1)S(1)}, bf16[128,1536]{1,0:T(8,128)(2,1)S(1)}, u32[]{:S(2)}, u32[]{:S(2)}) collective-permute-start(bf16[128,1536]{1,0:T(8,128)(2,1)S(1)} %get-tuple-element.240.refs_0_), channel_id=1, source_target_pairs={{0,4},{2,6},{8,0},{10,2},{16,8},{18,10},{24,16},{26,18},{28,24},{3... | collective-permute-start | bytes 1179656 | tf_op jit(solution)/shard_map/ppermute | solution.py:351
  119.6 14.7 %collective-permute-start.34 = (bf16[128,1536]{1,0:T(8,128)(2,1)S(1)}, bf16[128,1536]{1,0:T(8,128)(2,1)S(1)}, u32[]{:S(2)}, u32[]{:S(2)}) collective-permute-start(bf16[128,1536]{1,0:T(8,128)(2,1)S(1)} %get-tuple-element.240.refs_0_), channel_id=1, source_target_pairs={{0,8},{2,10},{8,16},{10,18},{16,24},{18,26},{24,28},{26,30},{28,20... | collective-permute-start | bytes 1179656 | tf_op jit(solution)/shard_map/ppermute | solution.py:347
  119.7 14.6 %collective-permute-start.38 = (bf16[128,1536]{1,0:T(8,128)(2,1)}, bf16[128,1536]{1,0:T(8,128)(2,1)S(1)}, u32[]{:S(2)}, u32[]{:S(2)}) collective-permute-start(bf16[128,1536]{1,0:T(8,128)(2,1)} %refs_2_.2), channel_id=1, source_target_pairs={{0,1},{1,0},{2,3},{3,2},{4,5},{5,4},{6,7},{7,6},{8,9},{9,8},{10,11... | collective-permute-start | bytes 1179656 | tf_op jit(solution)/shard_map/ppermute | solution.py:363
  121.2 11.6 %collective-permute-start.37 = (bf16[64,1536]{1,0:T(8,128)(2,1)S(1)}, bf16[64,1536]{1,0:T(8,128)(2,1)S(1)}, u32[]{:S(2)}, u32[]{:S(2)}) collective-permute-start(bf16[64,1536]{1,0:T(8,128)(2,1)S(1)} %slice.51), channel_id=1, source_target_pairs={{0,4},{2,6},{8,0},{10,2},{16,8},{18,10},{24,16},{26,18},{28,24},{3... | collective-permute-start | bytes 589832 | tf_op jit(solution)/shard_map/ppermute | solution.py:351
  123.2 11.1 %collective-permute-start.36 = (bf16[64,1536]{1,0:T(8,128)(2,1)S(1)}, bf16[64,1536]{1,0:T(8,128)(2,1)S(1)}, u32[]{:S(2)}, u32[]{:S(2)}) collective-permute-start(bf16[64,1536]{1,0:T(8,128)(2,1)S(1)} %slice.50), channel_id=1, source_target_pairs={{0,8},{2,10},{8,16},{10,18},{16,24},{18,26},{24,28},{26,30},{28,20... | collective-permute-start | bytes 589832 | tf_op jit(solution)/shard_map/ppermute | solution.py:347
  134.9 11.1 %collective-permute-start.39 = (bf16[128,1536]{1,0:T(8,128)(2,1)S(1)}, bf16[128,1536]{1,0:T(8,128)(2,1)S(1)}, u32[]{:S(2)}, u32[]{:S(2)}) collective-permute-start(bf16[128,1536]{1,0:T(8,128)(2,1)S(1)} %collective-permute-done.34.refs_2_), channel_id=1, source_target_pairs={{0,8},{2,10},{8,16},{10,18},{16,24},{18,26},{24,28},{26,30},{28,20... | collective-permute-start | bytes 1179656 | tf_op jit(solution)/shard_map/ppermute | solution.py:347
  135.2 10.8 %collective-permute-start.40 = (bf16[128,1536]{1,0:T(8,128)(2,1)S(1)}, bf16[128,1536]{1,0:T(8,128)(2,1)S(1)}, u32[]{:S(2)}, u32[]{:S(2)}) collective-permute-start(bf16[128,1536]{1,0:T(8,128)(2,1)S(1)} %collective-permute-done.35.refs_1_), channel_id=1, source_target_pairs={{0,4},{2,6},{8,0},{10,2},{16,8},{18,10},{24,16},{26,18},{28,24},{3... | collective-permute-start | bytes 1179656 | tf_op jit(solution)/shard_map/ppermute | solution.py:351
  183.8 13.4 %collective-permute-start.53 = (f32[512,1536]{1,0:T(8,128)}, f32[512,1536]{1,0:T(8,128)S(1)}, u32[]{:S(2)}, u32[]{:S(2)}) collective-permute-start(f32[512,1536]{1,0:T(8,128)} %get-tuple-element.289), channel_id=1, source_target_pairs={{0,2},{2,0},{4,6},{6,4},{8,10},{10,8},{12,14},{14,12},{16,18},{18,... | collective-permute-start | bytes 9437192 | tf_op jit(solution)/shard_map/ppermute | solution.py:355
  183.8 13.4 %collective-permute-start.54 = (f32[256,1536]{1,0:T(8,128)S(1)}, f32[256,1536]{1,0:T(8,128)S(1)}, u32[]{:S(2)}, u32[]{:S(2)}) collective-permute-start(f32[256,1536]{1,0:T(8,128)S(1)} %get-tuple-element.291), channel_id=1, source_target_pairs={{0,2},{2,0},{4,6},{6,4},{8,10},{10,8},{12,14},{14,12},{16,18},{18,... | collective-permute-start | bytes 4718600 | tf_op jit(solution)/shard_map/ppermute | solution.py:355
  184.5 11.1 %collective-permute-start.51 = (bf16[128,1536]{1,0:T(8,128)(2,1)S(1)}, bf16[128,1536]{1,0:T(8,128)(2,1)S(1)}, u32[]{:S(2)}, u32[]{:S(2)}) collective-permute-start(bf16[128,1536]{1,0:T(8,128)(2,1)S(1)} %get-tuple-element.285), channel_id=1, source_target_pairs={{0,8},{2,10},{8,16},{10,18},{16,24},{18,26},{24,28},{26,30},{28,20... | collective-permute-start | bytes 1179656 | tf_op jit(solution)/shard_map/ppermute | solution.py:347
  186.0 11.0 %collective-permute-start.52 = (bf16[128,1536]{1,0:T(8,128)(2,1)S(1)}, bf16[128,1536]{1,0:T(8,128)(2,1)S(1)}, u32[]{:S(2)}, u32[]{:S(2)}) collective-permute-start(bf16[128,1536]{1,0:T(8,128)(2,1)S(1)} %get-tuple-element.286), channel_id=1, source_target_pairs={{0,4},{2,6},{8,0},{10,2},{16,8},{18,10},{24,16},{26,18},{28,24},{3... | collective-permute-start | bytes 1179656 | tf_op jit(solution)/shard_map/ppermute | solution.py:351
  217.8 18.9 %all-to-all-start.1 = ((bf16[8,192,128]{2,1,0:T(8,128)(2,1)}), bf16[8,192,128]{2,1,0:T(8,128)(2,1)S(1)}, u32[]{:S(2)}, u32[]{:S(2)}) async-start(bf16[8,192,128]{2,1,0:T(8,128)(2,1)} %get-tuple-element.309), calls=%async_computation.1 | async-start | bytes 786432 | tf_op jit(solution)/shard_map/all_to_all | solution.py:1063
  224.3 10.5 %collective-permute-start.60 = (bf16[128,1536]{1,0:T(8,128)(2,1)S(1)}, bf16[128,1536]{1,0:T(8,128)(2,1)S(1)}, u32[]{:S(2)}, u32[]{:S(2)}) collective-permute-start(bf16[128,1536]{1,0:T(8,128)(2,1)S(1)} %get-tuple-element.305), channel_id=1, source_target_pairs={{0,8},{2,10},{8,16},{10,18},{16,24},{18,26},{24,28},{26,30},{28,20... | collective-permute-start | bytes 1179656 | tf_op jit(solution)/shard_map/ppermute | solution.py:347
  226.2 10.5 %collective-permute-start.61 = (bf16[128,1536]{1,0:T(8,128)(2,1)S(1)}, bf16[128,1536]{1,0:T(8,128)(2,1)S(1)}, u32[]{:S(2)}, u32[]{:S(2)}) collective-permute-start(bf16[128,1536]{1,0:T(8,128)(2,1)S(1)} %get-tuple-element.306), channel_id=1, source_target_pairs={{0,4},{2,6},{8,0},{10,2},{16,8},{18,10},{24,16},{26,18},{28,24},{3... | collective-permute-start | bytes 1179656 | tf_op jit(solution)/shard_map/ppermute | solution.py:351
  236.7 15.8 %collective-permute-start.65 = (bf16[8,96,1536]{2,1,0:T(8,128)(2,1)}, bf16[8,96,1536]{2,1,0:T(8,128)(2,1)S(1)}, u32[]{:S(2)}, u32[]{:S(2)}) collective-permute-start(bf16[8,96,1536]{2,1,0:T(8,128)(2,1)} %copy-done.23), channel_id=1, source_target_pairs={{0,2},{2,0},{4,6},{6,4},{8,10},{10,8},{12,14},{14,12},{16,18},{18,... | collective-permute-start | bytes 7077896 | tf_op jit(solution)/shard_map/ppermute | solution.py:355
  238.3 11.9 %collective-permute-start.63 = (bf16[128,1536]{1,0:T(8,128)(2,1)S(1)}, bf16[128,1536]{1,0:T(8,128)(2,1)S(1)}, u32[]{:S(2)}, u32[]{:S(2)}) collective-permute-start(bf16[128,1536]{1,0:T(8,128)(2,1)S(1)} %get-tuple-element.316), channel_id=1, source_target_pairs={{0,8},{2,10},{8,16},{10,18},{16,24},{18,26},{24,28},{26,30},{28,20... | collective-permute-start | bytes 1179656 | tf_op jit(solution)/shard_map/ppermute | solution.py:347
  241.0 11.5 %collective-permute-start.64 = (bf16[128,1536]{1,0:T(8,128)(2,1)S(1)}, bf16[128,1536]{1,0:T(8,128)(2,1)S(1)}, u32[]{:S(2)}, u32[]{:S(2)}) collective-permute-start(bf16[128,1536]{1,0:T(8,128)(2,1)S(1)} %get-tuple-element.317), channel_id=1, source_target_pairs={{0,4},{2,6},{8,0},{10,2},{16,8},{18,10},{24,16},{26,18},{28,24},{3... | collective-permute-start | bytes 1179656 | tf_op jit(solution)/shard_map/ppermute | solution.py:351
  254.0 11.6 %collective-permute-start.66 = (bf16[128,1536]{1,0:T(8,128)(2,1)S(1)}, bf16[128,1536]{1,0:T(8,128)(2,1)S(1)}, u32[]{:S(2)}, u32[]{:S(2)}) collective-permute-start(bf16[128,1536]{1,0:T(8,128)(2,1)S(1)} %get-tuple-element.328), channel_id=1, source_target_pairs={{0,8},{2,10},{8,16},{10,18},{16,24},{18,26},{24,28},{26,30},{28,20... | collective-permute-start | bytes 1179656 | tf_op jit(solution)/shard_map/ppermute | solution.py:347
  254.4 11.2 %collective-permute-start.68 = (bf16[128,1536]{1,0:T(8,128)(2,1)S(1)}, bf16[128,1536]{1,0:T(8,128)(2,1)S(1)}, u32[]{:S(2)}, u32[]{:S(2)}) collective-permute-start(bf16[128,1536]{1,0:T(8,128)(2,1)S(1)} %get-tuple-element.336), channel_id=1, source_target_pairs={{0,4},{2,6},{8,0},{10,2},{16,8},{18,10},{24,16},{26,18},{28,24},{3... | collective-permute-start | bytes 1179656 | tf_op jit(solution)/shard_map/ppermute | solution.py:351
  265.7 10.9 %collective-permute-start.71 = (bf16[128,1536]{1,0:T(8,128)(2,1)S(1)}, bf16[128,1536]{1,0:T(8,128)(2,1)S(1)}, u32[]{:S(2)}, u32[]{:S(2)}) collective-permute-start(bf16[128,1536]{1,0:T(8,128)(2,1)S(1)} %get-tuple-element.346), channel_id=1, source_target_pairs={{0,1},{1,0},{2,3},{3,2},{4,5},{5,4},{6,7},{7,6},{8,9},{9,8},{10,11... | collective-permute-start | bytes 1179656 | tf_op jit(solution)/shard_map/ppermute | solution.py:363
  276.6 21.6 %collective-permute-start.74 = (f32[2,96,1536]{2,1,0:T(8,128)S(1)}, f32[2,96,1536]{2,1,0:T(8,128)S(1)}, u32[]{:S(2)}, u32[]{:S(2)}) collective-permute-start(f32[2,96,1536]{2,1,0:T(8,128)S(1)} %get-tuple-element.354), channel_id=1, source_target_pairs={{0,2},{2,0},{4,6},{6,4},{8,10},{10,8},{12,14},{14,12},{16,18},{18,... | collective-permute-start | bytes 3538952 | tf_op jit(solution)/shard_map/ppermute | solution.py:355
  278.9 18.2 %collective-permute-start.72 = (bf16[224,1536]{1,0:T(8,128)(2,1)S(1)}, bf16[224,1536]{1,0:T(8,128)(2,1)S(1)}, u32[]{:S(2)}, u32[]{:S(2)}) collective-permute-start(bf16[224,1536]{1,0:T(8,128)(2,1)S(1)} %get-tuple-element.350), channel_id=1, source_target_pairs={{0,8},{2,10},{8,16},{10,18},{16,24},{18,26},{24,28},{26,30},{28,20... | collective-permute-start | bytes 2064392 | tf_op jit(solution)/shard_map/ppermute | solution.py:347
  280.3 17.8 %collective-permute-start.73 = (bf16[224,1536]{1,0:T(8,128)(2,1)S(1)}, bf16[224,1536]{1,0:T(8,128)(2,1)S(1)}, u32[]{:S(2)}, u32[]{:S(2)}) collective-permute-start(bf16[224,1536]{1,0:T(8,128)(2,1)S(1)} %get-tuple-element.351), channel_id=1, source_target_pairs={{0,4},{2,6},{8,0},{10,2},{16,8},{18,10},{24,16},{26,18},{28,24},{3... | collective-permute-start | bytes 2064392 | tf_op jit(solution)/shard_map/ppermute | solution.py:351
  281.3 15.8 %collective-permute-start.75 = (f32[2,1536]{1,0:T(2,128)S(1)}, f32[2,1536]{1,0:T(2,128)S(1)}, u32[]{:S(2)}, u32[]{:S(2)}) collective-permute-start(f32[2,1536]{1,0:T(2,128)S(1)} %get-tuple-element.355), channel_id=1, source_target_pairs={{0,4},{2,6},{4,0},{6,2},{8,12},{10,14},{12,8},{14,10},{16,20},{18,... | collective-permute-start | bytes 36872 | tf_op jit(solution)/shard_map/ppermute | solution.py:355
  298.4 21.3 %collective-permute-start.78 = (bf16[96,1536]{1,0:T(8,128)(2,1)S(1)}, bf16[96,1536]{1,0:T(8,128)(2,1)S(1)}, u32[]{:S(2)}, u32[]{:S(2)}) collective-permute-start(bf16[96,1536]{1,0:T(8,128)(2,1)S(1)} %fusion.5), channel_id=1, source_target_pairs={{0,1},{1,0},{2,3},{3,2},{4,5},{5,4},{6,7},{7,6},{8,9},{9,8},{10,11... | collective-permute-start | bytes 884744 | tf_op jit(solution)/shard_map/ppermute | solution.py:363
  301.6 18.2 %collective-permute-start.76 = (bf16[224,1536]{1,0:T(8,128)(2,1)S(1)}, bf16[224,1536]{1,0:T(8,128)(2,1)S(1)}, u32[]{:S(2)}, u32[]{:S(2)}) collective-permute-start(bf16[224,1536]{1,0:T(8,128)(2,1)S(1)} %get-tuple-element.356), channel_id=1, source_target_pairs={{0,8},{2,10},{8,16},{10,18},{16,24},{18,26},{24,28},{26,30},{28,20... | collective-permute-start | bytes 2064392 | tf_op jit(solution)/shard_map/ppermute | solution.py:347
  303.2 16.6 %collective-permute-start.77 = (bf16[224,1536]{1,0:T(8,128)(2,1)S(1)}, bf16[224,1536]{1,0:T(8,128)(2,1)S(1)}, u32[]{:S(2)}, u32[]{:S(2)}) collective-permute-start(bf16[224,1536]{1,0:T(8,128)(2,1)S(1)} %get-tuple-element.357), channel_id=1, source_target_pairs={{0,4},{2,6},{8,0},{10,2},{16,8},{18,10},{24,16},{26,18},{28,24},{3... | collective-permute-start | bytes 2064392 | tf_op jit(solution)/shard_map/ppermute | solution.py:351
  303.6 16.0 %collective-permute-start.79 = (f32[2,1536]{1,0:T(2,128)S(1)}, f32[2,1536]{1,0:T(2,128)S(1)}, u32[]{:S(2)}, u32[]{:S(2)}) collective-permute-start(f32[2,1536]{1,0:T(2,128)S(1)} %add.75), channel_id=1, source_target_pairs={{0,8},{2,10},{4,12},{6,14},{8,0},{10,2},{12,4},{14,6},{16,24},{18,... | collective-permute-start | bytes 36872 | tf_op jit(solution)/shard_map/ppermute | solution.py:355
  324.6 15.0 %collective-permute-start.80 = (bf16[224,1536]{1,0:T(8,128)(2,1)S(1)}, bf16[224,1536]{1,0:T(8,128)(2,1)S(1)}, u32[]{:S(2)}, u32[]{:S(2)}) collective-permute-start(bf16[224,1536]{1,0:T(8,128)(2,1)S(1)} %get-tuple-element.363), channel_id=1, source_target_pairs={{0,8},{2,10},{8,16},{10,18},{16,24},{18,26},{24,28},{26,30},{28,20... | collective-permute-start | bytes 2064392 | tf_op jit(solution)/shard_map/ppermute | solution.py:347
  324.9 15.0 %collective-permute-start.81 = (bf16[224,1536]{1,0:T(8,128)(2,1)S(1)}, bf16[224,1536]{1,0:T(8,128)(2,1)S(1)}, u32[]{:S(2)}, u32[]{:S(2)}) collective-permute-start(bf16[224,1536]{1,0:T(8,128)(2,1)S(1)} %get-tuple-element.364), channel_id=1, source_target_pairs={{0,4},{2,6},{8,0},{10,2},{16,8},{18,10},{24,16},{26,18},{28,24},{3... | collective-permute-start | bytes 2064392 | tf_op jit(solution)/shard_map/ppermute | solution.py:351
  (84 other events, 772.6 us)
